TPU v7x, 32 devices: a whole 2x2x4 slice. The times are simulated.
32 devices in a mesh: wide: 8 (over z, x), narrow: 4 (over y, core).
Axes of the slice: x: 2, y: 2, z: 4, core: 2. Of those that a mesh axis runs over, the one named last changes fastest.
Arguments:
- latents: bfloat16 [128, 32, 32, 384], P('wide', 'narrow'), may hold values from -6 to 6
- timesteps: int32 [128], P('wide'), may hold values from 0 to 999
- out_grad: bfloat16 [128, 16, 16, 768], P(('wide', 'narrow')), may hold values from -6 to 6
- ada_weight: bfloat16 [256, 2304], replicated, may hold values from -1 to 1
- ada_bias: bfloat16 [2304], replicated, may hold values from -4 to 4
- conv_attn: bfloat16 [3, 3, 384], replicated, may hold values from -2 to 2
- qkv_weight: bfloat16 [384, 1152], replicated, may hold values from -0.3125 to 0.3125
- proj_weight: bfloat16 [384, 384], replicated, may hold values from -1.25 to 1.25
- fc1_weight: bfloat16 [384, 1536], replicated, may hold values from -0.3125 to 0.3125
- fc1_bias: bfloat16 [1536], replicated, may hold values from -6 to 6
- conv_ffn: bfloat16 [3, 3, 1536], replicated, may hold values from -2 to 2
- fc2_weight: bfloat16 [1536, 384], replicated, may hold values from -0.15625 to 0.15625
- fc2_bias: bfloat16 [384], replicated, may hold values from -4 to 4
- down_weight: bfloat16 [1536, 768], replicated, may hold values from -0.15625 to 0.15625
- down_bias: bfloat16 [768], replicated, may hold values from -4 to 4
Outputs:
- result: bfloat16 [128, 16, 16, 768], P(('wide', 'narrow'))
- grad_latents: float32 [128, 32, 32, 384], P('wide', 'narrow')
- grad_ada_weight: float32 [256, 2304], replicated
- grad_ada_bias: float32 [2304], replicated
- grad_conv_attn: float32 [3, 3, 384], replicated
- grad_qkv_weight: float32 [384, 1152], replicated
- grad_proj_weight: float32 [384, 384], replicated
- grad_fc1_weight: float32 [384, 1536], replicated
- grad_fc1_bias: float32 [1536], replicated
- grad_conv_ffn: float32 [3, 3, 1536], replicated
- grad_fc2_weight: float32 [1536, 384], replicated
- grad_fc2_bias: float32 [384], replicated
- grad_down_weight: float32 [1536, 768], replicated
- grad_down_bias: float32 [768], replicated
All inputs are finite; a program needn't handle non-finite values.
Results may differ from a plain program's by a relative error of at most 0.018.
The roundings to bfloat16 on the way count: a program that leaves them out, or rounds other values in their place, can miss the bound.
Values may be sent and summed in bfloat16 or wider, within the bound.
No kernel may reach another device: no remote copies, remote signals or barrier semaphores. Data moves between devices by JAX's collectives and lax.ppermute only.
A program may use at most 384 MiB of HBM per device.

v0:
```python
import functools
import math

import jax
import jax.numpy as jnp
from jax import lax
from jax.experimental import pallas as pl
from jax.experimental.pallas import tpu as pltpu
from jax.sharding import PartitionSpec as P

HEADS = 6
EPSILON = 1e-06
HIGH = lax.Precision.HIGHEST
BF = jnp.bfloat16
F32 = jnp.float32
NN = ((1,), (0,))
NT = ((1,), (1,))
TN = ((0,), (0,))
LANES = 128
CHUNK = 256
TILE = 64
GELU_A = math.sqrt(2.0 / math.pi)
GELU_B = 0.044715
AXES = ("wide", "narrow")


def mm(left, right, dims=NN):
    return lax.dot_general(left, right, (dims, ((), ())), preferred_element_type=F32)


def col_sum(values):
    return jnp.sum(values, axis=0, keepdims=True)


def row_mean(values):
    return jnp.mean(values, axis=1, keepdims=True)


def normed(values):
    center = values - row_mean(values)
    spread = row_mean(center * center)
    inverse = lax.rsqrt(spread + EPSILON)
    return center * inverse, inverse


def norm_back(grad_normed, normed_values, inverse):
    return inverse * (
        grad_normed - row_mean(grad_normed) - normed_values * row_mean(grad_normed * normed_values)
    )


def tap_source(phase, tap):
    distance = phase + tap - 1
    return distance % 2, distance // 2


def tap_ref(plain, moved, row_phase, col_phase, row_tap, col_tap, cols, start, size, lanes):
    source_row, row_move = tap_source(row_phase, row_tap)
    source_col, col_move = tap_source(col_phase, col_tap)
    held = plain if col_move == 0 else moved
    return held[2 * source_row + source_col, pl.ds(cols + cols * row_move + start, size), lanes]


def fill_planes(plain, moved, plane, col_phase_matrix, values_low, cols, lanes):
    tokens = values_low.shape[0]
    plain[plane, pl.ds(cols, tokens), lanes] = values_low.astype(F32)
    moved[plane, pl.ds(cols, tokens), lanes] = mm(col_phase_matrix, values_low)


def conv_tile(plain, moved, weight, row_phase, col_phase, cols, start, size, lanes, lanes_weight):
    total = None
    for row_tap in range(3):
        for col_tap in range(3):
            window = tap_ref(
                plain, moved, row_phase, col_phase, row_tap, col_tap, cols, start, size, lanes
            )
            part = window * weight[pl.ds(row_tap * 3 + col_tap, 1), lanes_weight]
            total = part if total is None else total + part
    return total


def conv_back_tile(
    plain, moved, weight, inputs, kernel_grad, row_phase, col_phase, cols, start, size, lanes, lanes_weight
):
    total = None
    for row_tap in range(3):
        for col_tap in range(3):
            window = tap_ref(
                plain, moved, row_phase, col_phase, row_tap, col_tap, cols, start, size, lanes
            )
            mirror = (2 - row_tap) * 3 + (2 - col_tap)
            part = window * weight[pl.ds(mirror, 1), lanes_weight]
            total = part if total is None else total + part
            product = jnp.sum((window * inputs).reshape(size // 8, 8, LANES), axis=0)
            kernel_grad[mirror, :, lanes_weight] += product
    return total


def packed(values):
    return values.reshape(values.shape[0] // 8, 8, values.shape[1])


def kernel_rows(weight, lanes):
    return [jnp.broadcast_to(weight[pl.ds(tap, 1), lanes], (8, lanes.size)) for tap in range(9)]


def conv_packed(plain, moved, taps, row_phase, col_phase, cols, start, lanes):
    total = None
    for row_tap in range(3):
        for col_tap in range(3):
            window = packed(
                tap_ref(plain, moved, row_phase, col_phase, row_tap, col_tap, cols, start, TILE, lanes)
            )
            part = window * taps[row_tap * 3 + col_tap]
            total = part if total is None else total + part
    return total


def conv_back_packed(plain, moved, taps, inputs, row_phase, col_phase, cols, start, lanes):
    total = None
    sums = [None] * 9
    for row_tap in range(3):
        for col_tap in range(3):
            window = packed(
                tap_ref(plain, moved, row_phase, col_phase, row_tap, col_tap, cols, start, TILE, lanes)
            )
            mirror = (2 - row_tap) * 3 + (2 - col_tap)
            part = window * taps[mirror]
            total = part if total is None else total + part
            product = window * inputs
            count = product.shape[0]
            while count > 1:
                count //= 2
                product = product[:count] + product[count:]
            sums[mirror] = product[0].astype(F32)
    return total, sums


def fill_packed(plain, moved, plane, matrix, values_low, cols):
    tokens = values_low.shape[0]
    plain[plane, pl.ds(cols, tokens), :] = values_low
    moved[plane, pl.ds(cols, tokens), :] = mm(matrix, values_low).astype(BF)


def place_rows(ref, values, first_row, rank, parts):
    share = ref.shape[0] // parts
    step = math.gcd(math.gcd(share, values.shape[0]), first_row)
    for at in range(0, values.shape[0], step):
        part, rest = divmod(first_row + at, share)
        row = pl.multiple_of((part ^ rank) * share + rest, step)
        ref[pl.ds(row, step), :] = values[at : at + step]


def zero_pads(buffer, cols):
    planes, padded, width = buffer.shape
    edge = jnp.zeros((planes, cols, width), buffer.dtype)
    buffer[:, pl.ds(0, cols), :] = edge
    buffer[:, pl.ds(padded - cols, cols), :] = edge


def attention_forward_kernel(strips, begin, rank_ref, *refs):
    pieces, refs = refs[:strips], refs[strips:]
    mod_ref, qkv_w, conv_a, perm, moves = refs[:5]
    refs = refs[5:] if begin else refs[10:]
    xp_ref, co_ref, qkv_ref, mix_ref, stat_ref, plain_h, moved_h = refs
    tokens = moves.shape[1]
    cols = tokens // 16
    width = xp_ref.shape[2]
    quarter = perm.shape[0] // 4
    all_lanes = pl.ds(0, width)
    for ref in (plain_h, moved_h):
        zero_pads(ref, cols)
    shift_one, scale_one = (mod_ref[0, pl.ds(part, 1), :] for part in range(2))

    for at, piece in enumerate(pieces):
        strip = at ^ rank_ref[1]
        moved_piece = mm(perm[...], piece[...]).astype(BF)
        for plane in range(4):
            row = pl.multiple_of(plane * tokens + strip * quarter, quarter)
            xp_ref[0, pl.ds(row, quarter), :] = moved_piece[plane * quarter : (plane + 1) * quarter]

    for plane in range(4):
        unit, _ = normed(xp_ref[0, pl.ds(plane * tokens, tokens), :].astype(F32))
        low = (unit * (1.0 + scale_one) + shift_one).astype(BF)
        fill_planes(plain_h, moved_h, plane, moves[plane % 2], low, cols, all_lanes)
    for plane in range(4):
        for lane in range(0, width, LANES):
            for start in range(0, tokens, 128):
                lanes = pl.ds(lane, LANES)
                total = conv_tile(
                    plain_h, moved_h, conv_a, plane // 2, plane % 2, cols, start, 128, lanes, lanes
                )
                co_ref[0, pl.ds(plane * tokens + start, 128), lanes] = total.astype(BF)

    head_size = width // HEADS
    factor = head_size ** (-0.5)

    def attend(plane, carry):
        rows = pl.ds(pl.multiple_of(plane * tokens, tokens), tokens)
        qkv_ref[0, rows, :] = mm(co_ref[0, rows, :], qkv_w[...]).astype(BF)
        even = lax.broadcasted_iota(jnp.int32, (tokens, LANES), 1) < head_size
        scores = []
        for pair in range(width // LANES):
            query = qkv_ref[0, rows, pl.ds(pair * LANES, LANES)]
            key = qkv_ref[0, rows, pl.ds(width + pair * LANES, LANES)] * jnp.asarray(factor, BF)
            for mine in (even, ~even):
                scores.append(mm(jnp.where(mine, key, jnp.zeros_like(key)), query, NT))
        tops = [jnp.max(score, axis=0, keepdims=True) for score in scores]
        grown = [jnp.exp(score - top) for score, top in zip(scores, tops)]
        totals = [col_sum(values) for values in grown]
        probs = [(values * (1.0 / total)).astype(BF) for values, total in zip(grown, totals)]
        for pair in range(width // LANES):
            value_t = qkv_ref[0, rows, pl.ds(2 * width + pair * LANES, LANES)].T
            mixed_t = jnp.concatenate(
                [
                    mm(value_t[half * head_size : (half + 1) * head_size], probs[2 * pair + half])
                    for half in range(2)
                ],
                axis=0,
            )
            mix_ref[0, rows, pl.ds(pair * LANES, LANES)] = mixed_t.astype(BF).T
        for head in range(HEADS):
            stat_ref[0, plane, pl.ds(head, 1), :] = tops[head] + jnp.log(totals[head])
        return carry

    lax.fori_loop(0, 4, attend, 0)


def feed_forward_kernel(
    rank_ref,
    xp_ref,
    mix_ref,
    mod_ref,
    og_ref,
    proj_w,
    fc1_w,
    fc1_b,
    fc2_w,
    fc2_b,
    down_w,
    down_b,
    conv_f,
    moves,
    res_ref,
    gmid_ref,
    gmod_ref,
    big_ref,
    small_ref,
    fout_s,
    ghid_s,
    plain_p,
    moved_p,
    plain_g,
    moved_g,
    attn_s,
    gffn_s,
    hid_s,
    act_s,
    gpre_s,
    gact_s,
    hid_t,
    gffn_t,
    low_s,
    dconv_s,
    fc1_sum,
    fc2_sum,
    down_sum,
    *,
    parts,
):
    image = pl.program_id(0)
    tokens = moves.shape[1]
    cols = tokens // 16
    width = xp_ref.shape[2]
    hidden = fc1_w.shape[1]

    @pl.when(image == 0)
    def _():
        for ref in (fc1_sum, fc2_sum, down_sum, small_ref, dconv_s):
            ref[...] = jnp.zeros(ref.shape, F32)
        for ref in (plain_g, moved_g):
            zero_pads(ref, cols)
        for ref in (plain_p, moved_p):
            for slot in range(2):
                zero_pads(ref.at[slot], cols)

    gmod_ref[...] = jnp.zeros(gmod_ref.shape, F32)
    gate_one, shift_two, scale_two, gate_two = (mod_ref[0, pl.ds(part, 1), :] for part in range(2, 6))
    attn_s[...] = mm(mix_ref[0], proj_w[...])

    grad_low = og_ref[0]
    small_ref[pl.ds(10, 1), pl.ds(width, 2 * width)] += col_sum(grad_low.astype(F32))
    for plane in range(4):
        rows = pl.ds(plane * tokens, tokens)
        grad_after = mm(grad_low, down_w[pl.ds(plane * width, width), :], NT)
        gmid_ref[0, rows, :] = grad_after
        grad_out = (gate_two * grad_after).astype(BF)
        gffn_s[rows, :] = grad_out
        small_ref[pl.ds(10, 1), pl.ds(0, width)] += col_sum(grad_out.astype(F32))
        after = xp_ref[0, rows, :].astype(F32) + gate_one * attn_s[rows, :]
        unit, _ = normed(after)
        hid_s[rows, :] = (unit * (1.0 + scale_two) + shift_two).astype(BF)

    hid_t[...] = hid_s[...].T
    gffn_t[...] = gffn_s[...].T
    chunks = hidden // CHUNK

    def units_of(chunk):
        return pl.ds(pl.multiple_of(chunk * CHUNK, CHUNK), CHUNK)

    def prepare(chunk, slot):
        units = units_of(chunk)
        pre = (mm(hid_s[...], fc1_w[:, units]) + fc1_b[:, units]).astype(BF)
        for plane in range(4):
            fill_packed(
                plain_p.at[slot],
                moved_p.at[slot],
                plane,
                moves[plane % 2],
                pre[plane * tokens : (plane + 1) * tokens],
                cols,
            )
        gact_s[slot] = mm(gffn_s[...], fc2_w[units, :], NT).astype(gact_s.dtype)

    def collect(chunk, slot):
        units = units_of(chunk)
        ones = jnp.ones((16, act_s.shape[1]), BF)
        grad_pre = gpre_s[slot]
        active = act_s[slot]
        fc1_sum[:, units] += mm(hid_t[...], grad_pre)
        small_ref[pl.ds(9, 1), units] += mm(ones, grad_pre)[:1]
        fc2_sum[:, units] += mm(gffn_t[...], active)
        out = mm(active, fc2_w[units, :])
        grad_hid = mm(grad_pre, fc1_w[:, units], NT)
        for plane in range(4):
            part = slice(plane * tokens, (plane + 1) * tokens)
            fout_s[plane] += out[part]
            ghid_s[plane] += grad_hid[part]

    def convolve(chunk, slot):
        units = units_of(chunk)
        taps = kernel_rows(conv_f, units)
        chunk_lanes = pl.ds(0, CHUNK)
        plain, moved = plain_p.at[slot], moved_p.at[slot]
        for plane in range(4):
            for start in range(0, tokens, TILE):
                rows = pl.ds(plane * tokens + start, TILE)
                value = conv_packed(plain, moved, taps, plane // 2, plane % 2, cols, start, chunk_lanes)
                value_low = value.reshape(TILE, CHUNK)
                value = value_low.astype(F32)
                square = value * value
                half = 0.5 * jnp.tanh(value * (GELU_A + (GELU_A * GELU_B) * square))
                gate = 0.5 + half
                act_s[slot, rows, :] = (value * gate).astype(BF)
                gate_low = gate.astype(BF)
                bend = (value_low * (0.5 - half).astype(BF)) * (
                    jnp.asarray(2.0 * GELU_A, BF)
                    + (value_low * value_low) * jnp.asarray(6.0 * GELU_A * GELU_B, BF)
                )
                slope = gate_low + gate_low * bend
                plain_g[plane, pl.ds(cols + start, TILE), :] = slope * gact_s[slot, rows, :]
            rows = pl.ds(cols, tokens)
            moved_g[plane, rows, :] = mm(moves[plane % 2], plain_g[plane, rows, :]).astype(BF)
        kernel_grads = None
        for plane in range(4):
            for start in range(0, tokens, TILE):
                inputs = packed(plain[plane, pl.ds(cols + start, TILE), :])
                total, sums = conv_back_packed(
                    plain_g, moved_g, taps, inputs, plane // 2, plane % 2, cols, start, chunk_lanes
                )
                gpre_s[slot, pl.ds(plane * tokens + start, TILE), :] = total.reshape(TILE, CHUNK)
                kernel_grads = (
                    sums if kernel_grads is None else [a + b for a, b in zip(kernel_grads, sums)]
                )
        for tap in range(9):
            dconv_s[tap, :, units] += kernel_grads[tap]

    for ref in (fout_s, ghid_s):
        ref[...] = jnp.zeros(ref.shape, F32)
    for ref in (act_s, gpre_s):
        ref[1] = jnp.zeros(ref.shape[1:], BF)
    prepare(0, 0)

    def feed(step, carry):
        chunk = 2 * step
        prepare(chunk + 1, 1)
        collect(jnp.maximum(chunk - 1, 0), 1)
        convolve(chunk, 0)
        prepare(jnp.minimum(chunk + 2, chunks - 1), 0)
        collect(chunk, 0)
        convolve(chunk + 1, 1)
        return carry

    lax.fori_loop(0, chunks // 2, feed, 0)
    collect(chunks - 1, 1)

    grad_gate_one = grad_shift_two = grad_scale_two = grad_gate_two = jnp.zeros((1, width), F32)
    for plane in range(4):
        rows = pl.ds(plane * tokens, tokens)
        attn = attn_s[rows, :]
        after = xp_ref[0, rows, :].astype(F32) + gate_one * attn
        grad_after = gmid_ref[0, rows, :]
        out = fout_s[plane] + fc2_b[...]
        grad_gate_two += col_sum(out * grad_after)
        low_s[:, pl.ds(plane * width, width)] = (after + gate_two * out).astype(BF)
        grad_hid = ghid_s[plane]
        unit, inverse = normed(after)
        grad_shift_two += col_sum(grad_hid)
        grad_scale_two += col_sum(grad_hid * unit)
        grad_mid = grad_after + norm_back(grad_hid * (1.0 + scale_two), unit, inverse)
        gmid_ref[0, rows, :] = grad_mid
        grad_gate_one += col_sum(attn * grad_mid)
    gmod_ref[0, pl.ds(0, 1), :] = grad_gate_one
    gmod_ref[0, pl.ds(1, 1), :] = grad_shift_two
    gmod_ref[0, pl.ds(2, 1), :] = grad_scale_two
    gmod_ref[0, pl.ds(3, 1), :] = grad_gate_two

    res_ref[0] = (mm(low_s[...], down_w[...]) + down_b[...]).astype(BF)
    grad_low_t = grad_low.T

    def down_weights(chunk, carry):
        units = pl.ds(pl.multiple_of(chunk * CHUNK, CHUNK), CHUNK)
        down_sum[:, units] += mm(grad_low_t, low_s[:, units])
        return carry

    lax.fori_loop(0, low_s.shape[1] // CHUNK, down_weights, 0)

    @pl.when(image == pl.num_programs(0) - 1)
    def _():
        for tap in range(9):
            small_ref[pl.ds(tap, 1), :] = col_sum(dconv_s[tap])

        rank = rank_ref[0]
        for chunk in range(hidden // CHUNK):
            units = pl.ds(chunk * CHUNK, CHUNK)
            place_rows(big_ref, fc2_sum[:, units].T.astype(BF), chunk * CHUNK, rank, parts)
            down = down_sum[:, units].T.astype(BF)
            for half in range(2):
                place_rows(
                    big_ref,
                    down[:, half * width : (half + 1) * width],
                    (1 + half) * hidden + chunk * CHUNK,
                    rank,
                    parts,
                )
        for part in range(hidden // width):
            block = fc1_sum[:, pl.ds(part * width, width)].astype(BF)
            place_rows(big_ref, block, 3 * hidden + part * width, rank, parts)


def attention_back_kernel(
    rank_ref,
    mod_ref,
    gmid_ref,
    co_ref,
    qkv_ref,
    mix_ref,
    stat_ref,
    proj_w,
    small_ref,
    *rest,
    parts,
    begin,
    fresh,
    last,
):
    image = pl.program_id(0)
    width = mix_ref.shape[2]
    tokens = mix_ref.shape[1] // 4
    rest = list(rest)
    before_ref = None if begin else rest.pop(0)
    if not fresh:
        rest.pop(0)
    gqkv_ref = rest.pop(0)
    sum_ref = rest.pop(0)
    rows_ref = rest.pop(0) if last else None
    gout_s, gmix_s = rest

    @pl.when(image == 0)
    def _():
        sum_ref[...] = jnp.zeros(sum_ref.shape, F32) if begin else before_ref[...]

    gate_one = mod_ref[0, pl.ds(2, 1), :]
    head_size = width // HEADS
    factor = jnp.asarray(head_size ** (-0.5), BF)

    def attend(plane, carry):
        rows = pl.ds(pl.multiple_of(plane * tokens, tokens), tokens)
        grad_out = (gate_one * gmid_ref[0, rows, :]).astype(BF)
        gout_s[rows, :] = grad_out
        gmix_s[...] = mm(grad_out, proj_w[...], NT).astype(BF)
        even = lax.broadcasted_iota(jnp.int32, (tokens, LANES), 1) < head_size
        zero = jnp.zeros((tokens, LANES), BF)
        for pair in range(width // LANES):
            lane = pair * LANES
            query = qkv_ref[0, rows, pl.ds(lane, LANES)]
            key = qkv_ref[0, rows, pl.ds(width + lane, LANES)] * factor
            value = qkv_ref[0, rows, pl.ds(2 * width + lane, LANES)]
            query_low = query * factor
            key_t = key.T
            grad_mixed = gmix_s[:, pl.ds(lane, LANES)]
            masks = (even, ~even)
            scores = [mm(jnp.where(mine, key, zero), query, NT) for mine in masks]
            grad_probs = [mm(jnp.where(mine, value, zero), grad_mixed, NT) for mine in masks]
            probs = [
                jnp.exp(score - stat_ref[0, plane, pl.ds(2 * pair + half, 1), :])
                for half, score in enumerate(scores)
            ]
            weighted = [a * b for a, b in zip(probs, grad_probs)]
            inner = [col_sum(values) for values in weighted]
            grad_scores = [
                (values - prob * total).astype(BF)
                for values, prob, total in zip(weighted, probs, inner)
            ]
            grad_value = sum(
                mm(prob.astype(BF), jnp.where(mine, grad_mixed, zero))
                for prob, mine in zip(probs, masks)
            )
            grad_key = sum(
                mm(values, jnp.where(mine, query_low, zero)) for values, mine in zip(grad_scores, masks)
            )
            grad_query_t = jnp.concatenate(
                [
                    mm(key_t[half * head_size : (half + 1) * head_size], grad_scores[half])
                    for half in range(2)
                ],
                axis=0,
            )
            gqkv_ref[0, rows, pl.ds(lane, LANES)] = grad_query_t.astype(BF).T
            gqkv_ref[0, rows, pl.ds(width + lane, LANES)] = grad_key.astype(BF)
            gqkv_ref[0, rows, pl.ds(2 * width + lane, LANES)] = grad_value.astype(BF)
        return carry

    lax.fori_loop(0, 4, attend, 0)

    sum_ref[:, pl.ds(3 * width, width)] += mm(mix_ref[0].T, gout_s[...])
    conv_t = co_ref[0].T
    for part in range(3):
        lanes = pl.ds(part * width, width)
        sum_ref[:, lanes] += mm(conv_t, gqkv_ref[0, :, lanes])

    if last:

        @pl.when(image == pl.num_programs(0) - 1)
        def _():
            rank = rank_ref[0]
            rows_ref[...] = jnp.zeros(rows_ref.shape, BF)
            for part in range(4):
                lanes = pl.ds(part * width, width)
                place_rows(rows_ref, sum_ref[:, lanes].astype(BF), part * width, rank, parts)
            for part in range(4):
                lanes = pl.ds(part * width, width)
                place_rows(rows_ref, small_ref[:, lanes].astype(BF), 4 * width + part * 16, rank, parts)


def conv_attn_back_kernel(
    strips,
    rank_ref,
    xp_ref,
    mod_ref,
    gmid_ref,
    gqkv_ref,
    qkv_w,
    conv_a,
    perm_back,
    moves,
    *refs,
):
    pieces, refs = refs[:strips], refs[strips:]
    gmod_ref, d_conv, plain_h, plain_g, moved_g, gout_s, glat_s, dconv_s = refs
    image = pl.program_id(0)
    tokens = moves.shape[1]
    cols = tokens // 16
    width = xp_ref.shape[2]
    quarter = perm_back.shape[0] // 4
    all_lanes = pl.ds(0, width)

    @pl.when(image == 0)
    def _():
        d_conv[...] = jnp.zeros(d_conv.shape, F32)
        dconv_s[...] = jnp.zeros(dconv_s.shape, F32)
        for ref in (plain_g, moved_g):
            zero_pads(ref, cols)

    gmod_ref[...] = jnp.zeros(gmod_ref.shape, F32)
    shift_one, scale_one = (mod_ref[0, pl.ds(part, 1), :] for part in range(2))
    for plane in range(4):
        rows = pl.ds(plane * tokens, tokens)
        grad_conv = mm(gqkv_ref[0, rows, :], qkv_w[...], NT).astype(BF)
        fill_planes(plain_g, moved_g, plane, moves[plane % 2], grad_conv, cols, all_lanes)
        unit, _ = normed(xp_ref[0, rows, :].astype(F32))
        low = (unit * (1.0 + scale_one) + shift_one).astype(BF)
        plain_h[rows, :] = low.astype(F32)
    for plane in range(4):
        for lane in range(0, width, LANES):
            for start in range(0, tokens, 128):
                lanes = pl.ds(lane, LANES)
                rows = pl.ds(plane * tokens + start, 128)
                total = conv_back_tile(
                    plain_g,
                    moved_g,
                    conv_a,
                    plain_h[rows, lanes],
                    dconv_s,
                    plane // 2,
                    plane % 2,
                    cols,
                    start,
                    128,
                    lanes,
                    lanes,
                )
                glat_s[rows, lanes] = total
    grad_shift = grad_scale = jnp.zeros((1, width), F32)
    for plane in range(4):
        rows = pl.ds(plane * tokens, tokens)
        grad_hid = glat_s[rows, :]
        unit, inverse = normed(xp_ref[0, rows, :].astype(F32))
        grad_shift += col_sum(grad_hid)
        grad_scale += col_sum(grad_hid * unit)
        gout_s[rows, :] = (
            gmid_ref[0, rows, :] + norm_back(grad_hid * (1.0 + scale_one), unit, inverse)
        ).astype(BF)
    gmod_ref[0, pl.ds(0, 1), :] = grad_shift
    gmod_ref[0, pl.ds(1, 1), :] = grad_scale
    for at, piece in enumerate(pieces):
        strip = at ^ rank_ref[1]
        gathered = jnp.concatenate(
            [
                gout_s[pl.ds(pl.multiple_of(plane * tokens + strip * quarter, quarter), quarter), :]
                for plane in range(4)
            ],
            axis=0,
        )
        piece[0] = mm(perm_back[...], gathered).astype(BF)

    @pl.when(image == pl.num_programs(0) - 1)
    def _():
        for tap in range(9):
            d_conv[pl.ds(tap, 1), :] = col_sum(dconv_s[tap])


FINISH_STEPS = 8


def finish_big_kernel(rank_ref, rows_ref, fc1_ref, fc2_ref, down_ref):
    step = pl.program_id(0)
    count, share, width = rows_ref.shape
    inner = rank_ref[0] % count

    def write(ref, flat):
        for at in range(count):
            values = rows_ref[at ^ inner].astype(F32)
            if flat:
                ref[pl.ds(at * share, share), :] = values
            else:
                block, row = divmod(at * share, width)
                ref[pl.ds(row, share), pl.ds(block * width, width)] = values

    @pl.when(step < 2)
    def _():
        write(fc2_ref, True)

    @pl.when((step >= 2) & (step < 6))
    def _():
        write(down_ref, True)

    @pl.when(step >= 6)
    def _():
        write(fc1_ref, False)


def finish_rest_kernel(rank_ref, rows_ref, qkv_ref, proj_ref, small_ref, *, share):
    width = proj_ref.shape[0]
    rank = rank_ref[0]
    for part in range(rows_ref.shape[0]):
        values = rows_ref[part ^ rank, pl.ds(0, share), :].astype(F32)
        block, row = divmod(part * share, width)
        if block < 3:
            qkv_ref[pl.ds(row, share), pl.ds(block * width, width)] = values
        elif block == 3:
            proj_ref[pl.ds(row, share), :] = values
        elif block == 4 and row < 64:
            small = min(share, 16)
            for at in range(0, share, small):
                lanes = pl.ds((row + at) // 16 * width, width)
                small_ref[:, lanes] = values[at : at + small]


def per_image(shape, first=0):
    rest = len(shape) - 1
    return pl.BlockSpec((1,) + tuple(shape[1:]), lambda b, *_: (b + first,) + (0,) * rest)


def resident(shape):
    rank = len(shape)
    return pl.BlockSpec(tuple(shape), lambda b, *_: (0,) * rank, pipeline_mode=pl.Buffered(1))


def out_of(shape, dtype):
    return jax.ShapeDtypeStruct(shape, dtype)


PARAMS = pltpu.CompilerParams(
    dimension_semantics=("arbitrary",), vmem_limit_bytes=63 * 1024 * 1024
)


def token_tables(cols, strip):
    half = cols // 2
    spot = jnp.arange(strip)
    from_row, from_col = spot // cols, spot % cols
    target = ((from_row % 2) * 2 + from_col % 2) * (strip // 4) + (from_row // 2) * half + from_col // 2
    perm_back = (target[:, None] == spot[None, :]).astype(BF)
    perm = (spot[:, None] == target[None, :]).astype(BF)
    spot = jnp.arange(half * half)
    ahead = ((spot[None, :] == spot[:, None] + 1) & (spot[:, None] % half != half - 1)).astype(BF)
    behind = ((spot[None, :] == spot[:, None] - 1) & (spot[:, None] % half != 0)).astype(BF)
    return perm, perm_back, jnp.stack([ahead, behind])


def attention_forward_call(rank, image, images, pieces, mod, qkv_w, conv_a, perm, moves, held):
    strips = len(pieces)
    width = pieces[0].shape[1]
    tokens = moves.shape[1]
    shared = (qkv_w, conv_a, perm, moves)
    rows = 4 * tokens
    outs = [
        ((images, rows, width), BF),
        ((images, rows, width), BF),
        ((images, rows, 3 * width), BF),
        ((images, rows, width), BF),
        ((images, 4, 8, tokens), F32),
    ]
    begin = held is None
    held = () if begin else tuple(held)
    grid = pltpu.PrefetchScalarGridSpec(
        num_scalar_prefetch=1,
        grid=(1,),
        in_specs=[resident(piece.shape) for piece in pieces]
        + [per_image(mod.shape, image)]
        + [resident(w.shape) for w in shared]
        + [pl.BlockSpec(memory_space=pl.ANY)] * len(held),
        out_specs=[per_image(shape, image) for shape, _ in outs],
        scratch_shapes=[pltpu.VMEM((4, tokens + 32, width), F32)] * 2,
    )
    return pl.pallas_call(
        functools.partial(attention_forward_kernel, strips, begin),
        grid_spec=grid,
        out_shape=[out_of(shape, dtype) for shape, dtype in outs],
        input_output_aliases={} if begin else {strips + 6 + at: at for at in range(5)},
        compiler_params=PARAMS,
        cost_estimate=cost(1, 5e9, 8e6),
        name="attention_forward",
    )(rank, *pieces, mod, *shared, *held)


def feed_forward_call(rank, parts, xp, mix, mod, og, weights, moves):
    proj_w, fc1_w, fc1_b, fc2_w, fc2_b, down_w, down_b, conv_f = weights
    images, all_tokens, width = xp.shape
    tokens = moves.shape[1]
    hidden = fc1_w.shape[1]
    padded = tokens + 32
    per = (xp, mix, mod, og)
    shared = (*weights, moves)
    outs = [
        (og.shape[:2] + (down_w.shape[1],), BF),
        (xp.shape, F32),
        ((images, 8, width), F32),
    ]
    sums = [((4 * hidden, width), BF), ((16, hidden), F32)]
    grid = pltpu.PrefetchScalarGridSpec(
        num_scalar_prefetch=1,
        grid=(images,),
        in_specs=[per_image(v.shape) for v in per] + [resident(w.shape) for w in shared],
        out_specs=[per_image(s) for s, _ in outs] + [resident(s) for s, _ in sums],
        scratch_shapes=[
            pltpu.VMEM((4, tokens, width), F32),
            pltpu.VMEM((4, tokens, width), F32),
            pltpu.VMEM((2, 4, padded, CHUNK), BF),
            pltpu.VMEM((2, 4, padded, CHUNK), BF),
            pltpu.VMEM((4, padded, CHUNK), BF),
            pltpu.VMEM((4, padded, CHUNK), BF),
            pltpu.VMEM((all_tokens, width), F32),
            pltpu.VMEM((all_tokens, width), BF),
            pltpu.VMEM((all_tokens, width), BF),
            pltpu.VMEM((2, all_tokens, CHUNK), BF),
            pltpu.VMEM((2, all_tokens, CHUNK), BF),
            pltpu.VMEM((2, all_tokens, CHUNK), BF),
            pltpu.VMEM((width, all_tokens), BF),
            pltpu.VMEM((width, all_tokens), BF),
            pltpu.VMEM((tokens, 4 * width), BF),
            pltpu.VMEM((9, 8, hidden), F32),
            pltpu.VMEM((width, hidden), F32),
            pltpu.VMEM((width, hidden), F32),
            pltpu.VMEM((down_w.shape[1], hidden), F32),
        ],
    )
    return pl.pallas_call(
        functools.partial(feed_forward_kernel, parts=parts),
        grid_spec=grid,
        out_shape=[out_of(s, d) for s, d in outs + sums],
        compiler_params=PARAMS,
        cost_estimate=cost(images, 14e9, 20e6),
        name="feed_forward",
    )(rank, *per, *shared)


def cost(images, flops, moved):
    return pl.CostEstimate(
        flops=int(images * flops), bytes_accessed=int(images * moved), transcendentals=0
    )


def attention_back_call(rank, parts, image, last, group, mod, gmid, co, qkv, mix, stat, proj_w, small, before, held):
    width = mix.shape[2]
    all_tokens = mix.shape[1]
    first, count = group
    begin = before is None
    fresh = held is None
    per = (mod, gmid, co, qkv, mix, stat)
    shared = (proj_w, small) + (() if begin else (before,))
    aliased = () if fresh else (held,)
    outs = [((count,) + qkv.shape[1:], BF)]
    share = 64 if parts <= 32 else 16
    sums = [((width, 4 * width), F32)] + ([((share * parts, width), BF)] if last else [])
    grid = pltpu.PrefetchScalarGridSpec(
        num_scalar_prefetch=1,
        grid=(1,),
        in_specs=[per_image(v.shape, image) for v in per]
        + [resident(w.shape) for w in shared]
        + [pl.BlockSpec(memory_space=pl.ANY)] * len(aliased),
        out_specs=[per_image(s, image - first) for s, _ in outs] + [resident(s) for s, _ in sums],
        scratch_shapes=[
            pltpu.VMEM((all_tokens, width), BF),
            pltpu.VMEM((all_tokens // 4, width), BF),
        ],
    )
    return pl.pallas_call(
        functools.partial(attention_back_kernel, parts=parts, begin=begin, fresh=fresh, last=last),
        grid_spec=grid,
        out_shape=[out_of(s, d) for s, d in outs + sums],
        input_output_aliases={} if fresh else {1 + len(per) + len(shared): 0},
        compiler_params=PARAMS,
        cost_estimate=cost(1, 8e9, 10e6),
        name="attention_back",
    )(rank, *per, *shared, *aliased)


def conv_attn_back_call(rank, strips, first, xp, mod, gmid, gqkv, weights, perm_back, moves):
    qkv_w, conv_a = weights
    images, all_tokens, width = gqkv.shape[0], xp.shape[1], xp.shape[2]
    tokens = moves.shape[1]
    padded = tokens + 32
    shared = (qkv_w, conv_a, perm_back, moves)
    outs = [((images, all_tokens // strips, width), BF)] * strips + [((images, 8, width), F32)]
    sums = [(16, width)]
    grid = pltpu.PrefetchScalarGridSpec(
        num_scalar_prefetch=1,
        grid=(images,),
        in_specs=[per_image(v.shape, first) for v in (xp, mod, gmid)]
        + [per_image(gqkv.shape)]
        + [resident(w.shape) for w in shared],
        out_specs=[per_image(s) for s, _ in outs] + [resident(s) for s in sums],
        scratch_shapes=[
            pltpu.VMEM((all_tokens, width), F32),
            pltpu.VMEM((4, padded, width), F32),
            pltpu.VMEM((4, padded, width), F32),
            pltpu.VMEM((all_tokens, width), BF),
            pltpu.VMEM((all_tokens, width), F32),
            pltpu.VMEM((9, 8, width), F32),
        ],
    )
    return pl.pallas_call(
        functools.partial(conv_attn_back_kernel, strips),
        grid_spec=grid,
        out_shape=[out_of(s, d) for s, d in outs] + [out_of(s, F32) for s in sums],
        compiler_params=PARAMS,
        cost_estimate=cost(images, 4e9, 8e6),
        name="conv_attn_back",
    )(rank, xp, mod, gmid, gqkv, *shared)


def finish_latents_kernel(strips, rank_ref, *refs):
    out_ref = refs[-1]
    for at in range(strips):
        out_ref[at ^ rank_ref[1], 0] = refs[at][0].astype(F32)


def finish_latents_call(rank, images, first, pieces, held):
    strips = len(pieces)
    count, tokens, width = pieces[0].shape
    shape = (strips, images, tokens, width)
    held = () if held is None else (held,)
    grid = pltpu.PrefetchScalarGridSpec(
        num_scalar_prefetch=1,
        grid=(count,),
        in_specs=[per_image(piece.shape) for piece in pieces]
        + [pl.BlockSpec(memory_space=pl.ANY)] * len(held),
        out_specs=pl.BlockSpec((strips, 1, tokens, width), lambda b, *_: (0, b + first, 0, 0)),
    )
    return pl.pallas_call(
        functools.partial(finish_latents_kernel, strips),
        grid_spec=grid,
        out_shape=out_of(shape, F32),
        input_output_aliases={strips + 1: 0} if held else {},
        compiler_params=PARAMS,
        cost_estimate=cost(count, 0, 3e6),
        name="finish_latents",
    )(rank, *pieces, *held)


def finish_big_call(rank, rows, hidden, width):
    parts, share, _ = rows.shape
    count = parts // FINISH_STEPS
    deep = count * share
    grid = pltpu.PrefetchScalarGridSpec(
        num_scalar_prefetch=1,
        grid=(FINISH_STEPS,),
        in_specs=[pl.BlockSpec((count, share, width), lambda i, rank: (i ^ (rank[0] // count), 0, 0))],
        out_specs=[
            pl.BlockSpec((width, deep), lambda i, rank: (0, jnp.maximum(i - 6, 0))),
            pl.BlockSpec((deep, width), lambda i, rank: (jnp.minimum(i, 1), 0)),
            pl.BlockSpec(
                (deep, width), lambda i, rank: (jnp.clip(i - 2, 0, 3) % 2, jnp.clip(i - 2, 0, 3) // 2)
            ),
        ],
    )
    return pl.pallas_call(
        finish_big_kernel,
        grid_spec=grid,
        out_shape=[out_of((width, hidden), F32), out_of((hidden, width), F32), out_of((hidden, 2 * width), F32)],
        compiler_params=PARAMS,
        cost_estimate=cost(1, 0, 15e6),
        name="finish_big",
    )(rank, rows)


def finish_rest_call(rank, rows, share, width):
    shapes = [(width, 3 * width), (width, width), (16, 4 * width)]
    grid = pltpu.PrefetchScalarGridSpec(
        num_scalar_prefetch=1,
        grid=(1,),
        in_specs=[resident(rows.shape)],
        out_specs=[resident(shape) for shape in shapes],
    )
    return pl.pallas_call(
        functools.partial(finish_rest_kernel, share=share),
        grid_spec=grid,
        out_shape=[out_of(shape, F32) for shape in shapes],
        compiler_params=PARAMS,
        cost_estimate=cost(1, 0, 5e6),
        name="finish_rest",
    )(rank, rows)


def stages(devices):
    bits = devices.bit_length() - 1
    found = [[1]]
    for at in range(1, bits, 2):
        group = [1 << b for b in range(at, min(at + 2, bits))]
        found.append(group)
    return found


def group_masks(group):
    if len(group) == 1:
        return [0, group[0]]
    return [0, group[1], group[0], group[0] | group[1]]


def exchange(values, mask, devices):
    return lax.ppermute(values, AXES, [(i, i ^ mask) for i in range(devices)])


def swap_strips(values, mask):
    count = lax.axis_size("narrow")
    return lax.ppermute(values, "narrow", [(i, i ^ mask) for i in range(count)])


def sent_strips(pieces):
    return [piece if at == 0 else swap_strips(piece, at) for at, piece in enumerate(pieces)]


def scatter_stage(values, group, devices):
    masks = group_masks(group)
    size = values.shape[0] // len(masks)
    total = values[:size].astype(F32)
    for at, mask in enumerate(masks[1:], 1):
        total = total + exchange(values[at * size : (at + 1) * size], mask, devices).astype(F32)
    return total.astype(BF)


def gather_stage(values, group, devices):
    masks = group_masks(group)
    return jnp.concatenate(
        [values] + [exchange(values, mask, devices) for mask in masks[1:]], axis=0
    )


def flat_rank(devices):
    index = lax.axis_index("wide") * lax.axis_size("narrow") + lax.axis_index("narrow")
    rank = jnp.zeros((), jnp.int32)
    bits = devices.bit_length() - 1
    for bit in range(bits):
        rank = rank | (((index >> bit) & 1) << (bits - 1 - bit))
    return jnp.stack([rank, lax.axis_index("narrow")])


def shards(
    latents,
    timesteps,
    out_grad,
    ada_weight,
    ada_bias,
    conv_attn,
    qkv_weight,
    proj_weight,
    fc1_weight,
    fc1_bias,
    conv_ffn,
    fc2_weight,
    fc2_bias,
    down_weight,
    down_bias,
):
    images, cols, width = out_grad.shape[0], latents.shape[2], latents.shape[3]
    height = latents.shape[1] * lax.axis_size("narrow")
    hidden = fc1_weight.shape[1]
    devices = lax.axis_size("wide") * lax.axis_size("narrow")
    rank = flat_rank(devices)
    steps = stages(devices)
    strips = lax.axis_size("narrow")
    strip_tokens = latents.shape[1] * cols
    place = lax.axis_index("narrow")
    sources = latents.reshape(strips, images, strip_tokens, width)
    own_steps = lax.dynamic_slice_in_dim(timesteps, lax.axis_index("narrow") * images, images)
    half_count = ada_weight.shape[0] // 2
    freq = jnp.exp(-math.log(10000.0) * jnp.arange(half_count, dtype=F32) / half_count)
    angles = own_steps.astype(F32)[:, None] * freq[None, :]
    features = jnp.concatenate([jnp.cos(angles), jnp.sin(angles)], axis=1)
    cond = jax.nn.silu(features).astype(BF)
    mod = jnp.dot(cond, ada_weight, preferred_element_type=F32) + ada_bias.astype(F32)
    mod = jnp.pad(mod.reshape(images, 6, width), ((0, 0), (0, 2), (0, 0)))
    perm, perm_back, moves = token_tables(cols, strip_tokens)
    conv_a = jnp.pad(conv_attn.reshape(9, width).astype(F32), ((0, 7), (0, 0)))
    conv_f = jnp.pad(conv_ffn.reshape(9, hidden), ((0, 7), (0, 0)))
    low = out_grad.reshape(images, height * cols // 4, out_grad.shape[3])
    held = None
    behind = None
    for image in range(images):
        pieces = [
            lax.dynamic_slice(sources, (place ^ at, image, 0, 0), (1, 1, strip_tokens, width)).reshape(
                strip_tokens, width
            )
            for at in range(strips)
        ]
        if behind is not None:
            behind, *pieces = lax.optimization_barrier((behind, *pieces))
            held = attention_forward_call(
                rank, image - 1, images, behind, mod, qkv_weight, conv_a, perm, moves, held
            )
        behind = tuple(
            piece if at == 0 else swap_strips(piece, at) for at, piece in enumerate(pieces)
        )
    xp, co, qkv, mix, stat = attention_forward_call(
        rank, images - 1, images, behind, mod, qkv_weight, conv_a, perm, moves, held
    )
    res, gmid, gmod_two, big, small = feed_forward_call(
        rank,
        devices,
        xp,
        mix,
        mod,
        low,
        (
            proj_weight,
            fc1_weight,
            fc1_bias.astype(F32)[None],
            fc2_weight,
            fc2_bias.astype(F32)[None],
            down_weight,
            down_bias.astype(F32)[None],
            conv_f,
        ),
        moves,
    )
    halves = [(0, images)] if images == 1 else [(0, images // 2), (images // 2, images - images // 2)]
    calls = images + len(halves)
    plan = [(0, 0), (1, 0), (1, 0), (2, 0), (3, 0), (4, 1)] if calls == 6 else [(min(at, 3), 0) for at in range(calls)]
    large = [functools.partial(scatter_stage, group=group, devices=devices) for group in steps]
    large += [functools.partial(gather_stage, group=group, devices=devices) for group in reversed(steps)]
    little = [functools.partial(scatter_stage, group=group, devices=devices) for group in steps]
    large_at = little_at = 0
    rest = before = None
    gqkv_parts = []

    def advance(call):
        nonlocal large_at, little_at, big, rest, mod
        while large_at < plan[call][0]:
            big = large[large_at](big)
            large_at += 1
        while little_at < plan[call][1]:
            rest = little[little_at](rest)
            little_at += 1
        if large_at:
            mod, big, rest = lax.optimization_barrier((mod, big, rest))

    for group in halves:
        gqkv = None
        for image in range(group[0], sum(group)):
            advance(image)
            gqkv, before, *final = attention_back_call(
                rank,
                devices,
                image,
                image == images - 1,
                group,
                mod,
                gmid,
                co,
                qkv,
                mix,
                stat,
                proj_weight,
                small,
                before,
                gqkv,
            )
        gqkv_parts.append(gqkv)
    rest = final[0]
    outs, mods, convs = [], [], []
    made = ()
    for at, ((first, count), gqkv) in enumerate(zip(halves, gqkv_parts)):
        advance(images + at)
        if at:
            mod, big, rest, made = lax.optimization_barrier((mod, big, rest, made))
            outs.append(sent_strips(made))
        *made, gmod_one, d_ca = conv_attn_back_call(
            rank, strips, first, xp, mod, gmid, gqkv, (qkv_weight, conv_a), perm_back, moves
        )
        mods.append(gmod_one)
        convs.append(d_ca)
    arrived = outs
    while large_at < len(large) or little_at < len(little):
        if large_at < len(large):
            big = large[large_at](big)
            large_at += 1
        if little_at < len(little):
            rest = little[little_at](rest)
            little_at += 1
        if made is not None:
            big, rest, made = lax.optimization_barrier((big, rest, made))
            sent, made = sent_strips(made), None
        else:
            big, rest, arrived = lax.optimization_barrier((big, rest, arrived))
    outs = [*arrived, sent]
    grad_mod = jnp.concatenate([jnp.concatenate(mods, axis=0)[:, :2], gmod_two[:, :4]], axis=1)
    late = jnp.concatenate(
        [
            sum(convs),
            grad_mod.reshape(images * 6, width),
            jnp.pad(cond.astype(F32), ((0, 0), (0, width - cond.shape[1]))),
        ],
        axis=0,
    )
    late = jnp.pad(late, ((0, -late.shape[0] % 16), (0, 0))).astype(BF)
    share = rest.shape[0]
    rest = jnp.concatenate([rest, late], axis=0)
    finished = None
    for at, group in enumerate(reversed(steps)):
        rest = gather_stage(rest, group, devices)
        if at == 0:
            rest, outs = lax.optimization_barrier((rest, outs))
        if at == 1:
            finished = finish_big_call(rank, big.reshape(devices, -1, width), hidden, width)
            rest, finished = lax.optimization_barrier((rest, finished))
    grad_fc1, grad_fc2, grad_down = finished
    grad_latents = None
    for (first, count), pieces in zip(halves, outs):
        grad_latents = finish_latents_call(rank, images, first, pieces, grad_latents)
    rest = rest.reshape(devices, -1, width)
    rest, grad_latents = lax.optimization_barrier((rest, grad_latents))
    grad_qkv, grad_proj, small = finish_rest_call(rank, rest, share, width)
    late = rest[:, share:]
    grad_conv_attn = jnp.sum(late[:, :9].astype(F32), axis=0)
    all_mod = late[:, 16 : 16 + 6 * images].reshape(devices * images, 6 * width)
    all_cond = late[:, 16 + 6 * images : 16 + 7 * images, : cond.shape[1]]
    all_cond = all_cond.reshape(devices * images, cond.shape[1])
    grad_ada = lax.dot_general(all_cond, all_mod, (TN, ((), ())), preferred_element_type=F32)
    grad_ada_bias = jnp.sum(all_mod.astype(F32), axis=0)
    return (
        res.reshape(out_grad.shape),
        grad_latents.reshape(latents.shape),
        grad_ada,
        grad_ada_bias,
        grad_conv_attn.reshape(conv_attn.shape),
        grad_qkv,
        grad_proj,
        grad_fc1,
        small[9],
        small[:9].reshape(conv_ffn.shape),
        grad_fc2,
        small[10, :width],
        grad_down,
        small[10, width : 3 * width],
    )


def solution(mesh):
    strip = P("wide", "narrow", None, None)
    image = P(AXES, None, None, None)
    in_specs = (strip, P("wide"), image) + (P(),) * 12
    out_specs = (image, strip) + (P(),) * 12
    return jax.shard_map(shards, mesh=mesh, in_specs=in_specs, out_specs=out_specs, check_vma=False)
```

profile of v0, /device:TPU:0, one launch (start us, length us, event | category | flops | bytes accessed | tf_op | source)
XLA Modules:
  0.0 416.6 jit_solution(10917576903541848181)
XLA Ops:
  0.8 3.4 dynamic-slice_bitcast_fusion
  4.1 2.5 collective-permute-start.2
  14.5 1.7 collective-permute-done.1.refs_2_
  16.3 2.4 collective-permute-start.4
  18.8 10.4 %attention_forward.4 = (bf16[4,1024,384]{2,1,0:T(8,128)(2,1)}, bf16[4,1024,384]{2,1,0:T(8,128)(2,1)}, bf16[4,1024,1152]{2,1,0:T(8,128)(2,1)}, bf16[4,1024,384]{2,1,0:T(8,128)(2,1)}, f32[4,4,8,256]{3,2,1,0:T(8,128)}) custom-call(s32[2]{0:T(128)} %pad_add_fusion.rank_ref, bf16[256,384]{1,0:T(8,128)(2,1)} %get-tuple-element.154.refs_0_, ...), custom_call_target="tpu_custom_call" | custom-call | flops 5000000000 | bytes 8000000 | tf_op jit(solution)/shard_map/attention_forward/pallas_call | solution.py:747
  30.1 2.0 collective-permute-start.7
  32.1 10.2 %attention_forward.5 = (bf16[4,1024,384]{2,1,0:T(8,128)(2,1)}, bf16[4,1024,384]{2,1,0:T(8,128)(2,1)}, bf16[4,1024,1152]{2,1,0:T(8,128)(2,1)}, bf16[4,1024,384]{2,1,0:T(8,128)(2,1)}, f32[4,4,8,256]{3,2,1,0:T(8,128)}) custom-call(s32[2]{0:T(128)} %pad_add_fusion.rank_ref, ...), custom_call_target="tpu_custom_call", output_to_operand_aliasing={{0}: (10, {}), {1}: (11, {}), {2}: (12, {}), {3}: (13, {}),... | custom-call | flops 5000000000 | bytes 8000000 | tf_op jit(solution)/shard_map/attention_forward/pallas_call | solution.py:747
  42.5 1.9 collective-permute-start.10
  44.5 10.2 %attention_forward.6 = (bf16[4,1024,384]{2,1,0:T(8,128)(2,1)}, bf16[4,1024,384]{2,1,0:T(8,128)(2,1)}, bf16[4,1024,1152]{2,1,0:T(8,128)(2,1)}, bf16[4,1024,384]{2,1,0:T(8,128)(2,1)}, f32[4,4,8,256]{3,2,1,0:T(8,128)}) custom-call(s32[2]{0:T(128)} %pad_add_fusion.rank_ref, ...), custom_call_target="tpu_custom_call", output_to_operand_aliasing={{0}: (10, {}), {1}: (11, {}), {2}: (12, {}), {3}: (13, {}),... | custom-call | flops 5000000000 | bytes 8000000 | tf_op jit(solution)/shard_map/attention_forward/pallas_call | solution.py:747
  55.4 10.1 %attention_forward.7 = (bf16[4,1024,384]{2,1,0:T(8,128)(2,1)}, bf16[4,1024,384]{2,1,0:T(8,128)(2,1)}, bf16[4,1024,1152]{2,1,0:T(8,128)(2,1)}, bf16[4,1024,384]{2,1,0:T(8,128)(2,1)}, f32[4,4,8,256]{3,2,1,0:T(8,128)}) custom-call(s32[2]{0:T(128)} %pad_add_fusion.rank_ref, ...), custom_call_target="tpu_custom_call", output_to_operand_aliasing={{0}: (10, {}), {1}: (11, {}), {2}: (12, {}), {3}: (13, {}),... | custom-call | flops 5000000000 | bytes 8000000 | tf_op jit(solution)/shard_map/attention_forward/pallas_call | solution.py:747
  65.6 111.5 %feed_forward.1 = (bf16[4,256,768]{2,1,0:T(8,128)(2,1)}, f32[4,1024,384]{2,1,0:T(8,128)}, f32[4,8,384]{2,1,0:T(8,128)}, bf16[6144,384]{1,0:T(8,128)(2,1)}, f32[16,1536]{1,0:T(8,128)}) custom-call(s32[2]{0:T(128)} %pad_add_fusion.rank_ref, bf16[4,1024,384]{2,1,0:T(8,128)(2,1)} %get-tuple-element.173.xp_ref, bf16[4,1024,384]{2,1,0:T(8,128)(2,1)} %get-tuple-element.174.mix_ref, ...), custom_call_target="tpu_custom_call" | custom-call | flops 56000000000 | bytes 80000000 | tf_op jit(solution)/shard_map/feed_forward/pallas_call | solution.py:799
  177.0 3.3 slice.94
  180.5 13.8 %attention_back.4 = (bf16[2,1024,1152]{2,1,0:T(8,128)(2,1)}, f32[384,1536]{1,0:T(8,128)}) custom-call(s32[2]{0:T(128)} %pad_add_fusion.rank_ref, f32[4,8,384]{2,1,0:T(8,128)} %pad.24.refs_4_.mod_ref, f32[4,1024,384]{2,1,0:T(8,128)} %get-tuple-element.181.gmid_ref, bf16[4,1024,384]{2,1,0:T(8,128)(2,1)} %get-tuple-element.182.co_ref, ...), custom_call_target="tpu_custom_call" | custom-call | flops 8000000000 | bytes 10000000 | tf_op jit(solution)/shard_map/attention_back/pallas_call | solution.py:839
  194.3 3.0 add_convert_fusion
  199.9 1.9 collective-permute-start.13
  203.4 14.7 %attention_back.5 = (bf16[2,1024,1152]{2,1,0:T(8,128)(2,1)}, f32[384,1536]{1,0:T(8,128)}) custom-call(s32[2]{0:T(128)} %pad_add_fusion.rank_ref, f32[4,8,384]{2,1,0:T(8,128)} %pad.24.refs_4_.mod_ref, f32[4,1024,384]{2,1,0:T(8,128)} %get-tuple-element.181.gmid_ref, bf16[4,1024,384]{2,1,0:T(8,128)(2,1)} %get-tuple-element.182.co_ref, ...), custom_call_target="tpu_custom_call", output_to_operand_aliasing={{0}: (10, {})} | custom-call | flops 8000000000 | bytes 10000000 | tf_op jit(solution)/shard_map/attention_back/pallas_call | solution.py:839
  218.1 14.9 %attention_back.6 = (bf16[2,1024,1152]{2,1,0:T(8,128)(2,1)}, f32[384,1536]{1,0:T(8,128)}) custom-call(s32[2]{0:T(128)} %pad_add_fusion.rank_ref, f32[4,8,384]{2,1,0:T(8,128)} %pad.24.refs_4_.mod_ref, f32[4,1024,384]{2,1,0:T(8,128)} %get-tuple-element.181.gmid_ref, bf16[4,1024,384]{2,1,0:T(8,128)(2,1)} %get-tuple-element.182.co_ref, ...), custom_call_target="tpu_custom_call" | custom-call | flops 8000000000 | bytes 10000000 | tf_op jit(solution)/shard_map/attention_back/pallas_call | solution.py:839
  232.9 1.9 add_convert_fusion.2
  235.5 3.0 collective-permute-start.16
  240.1 15.5 %attention_back.7 = (bf16[2,1024,1152]{2,1,0:T(8,128)(2,1)}, f32[384,1536]{1,0:T(8,128)}, bf16[2048,384]{1,0:T(8,128)(2,1)}) custom-call(s32[2]{0:T(128)} %pad_add_fusion.rank_ref, f32[4,8,384]{2,1,0:T(8,128)} %pad.24.refs_4_.mod_ref, f32[4,1024,384]{2,1,0:T(8,128)} %get-tuple-element.181.gmid_ref, ...), custom_call_target="tpu_custom_call", output_to_operand_aliasing={{0}: (10, {})} | custom-call | flops 8000000000 | bytes 10000000 | tf_op jit(solution)/shard_map/attention_back/pallas_call | solution.py:839
  256.8 3.0 collective-permute-start.21
  262.5 15.6 %conv_attn_back.2 = (bf16[2,256,384]{2,1,0:T(8,128)(2,1)}, bf16[2,256,384]{2,1,0:T(8,128)(2,1)}, bf16[2,256,384]{2,1,0:T(8,128)(2,1)}, bf16[2,256,384]{2,1,0:T(8...) custom-call(s32[2]{0:T(128)} %pad_add_fusion.rank_ref, bf16[4,1024,384]{2,1,0:T(8,128)(2,1)} %get-tuple-element.173.xp_ref, ...), custom_call_target="tpu_custom_call" | custom-call | flops 8000000000 | bytes 16000000 | tf_op jit(solution)/shard_map/conv_attn_back/pallas_call | solution.py:874
  278.1 1.9 pad_maximum_fusion.4
  280.1 1.6 add_convert_fusion.1
  283.9 1.5 collective-permute-start.25
  290.1 1.6 collective-permute-start.27
  291.6 15.3 %conv_attn_back.3 = (bf16[2,256,384]{2,1,0:T(8,128)(2,1)}, bf16[2,256,384]{2,1,0:T(8,128)(2,1)}, bf16[2,256,384]{2,1,0:T(8,128)(2,1)}, bf16[2,256,384]{2,1,0:T(8...) custom-call(s32[2]{0:T(128)} %pad_add_fusion.rank_ref, bf16[4,1024,384]{2,1,0:T(8,128)(2,1)} %get-tuple-element.173.xp_ref, ...), custom_call_target="tpu_custom_call" | custom-call | flops 8000000000 | bytes 16000000 | tf_op jit(solution)/shard_map/conv_attn_back/pallas_call | solution.py:874
  306.9 13.5 %collective-permute-done.28 = bf16[256,384]{1,0:T(8,128)(2,1)} collective-permute-done((bf16[256,384]{1,0:T(8,128)(2,1)}, bf16[256,384]{1,0:T(8,128)(2,1)}, u32[]{:S(2)}, u32[]{:S(2)}) %collective-permute-start.28) | collective-permute-done | bytes 196640 | tf_op jit(solution)/shard_map/ppermute | solution.py:973
  323.2 1.8 pad_maximum_fusion.2
  326.6 2.0 collective-permute-start.30
  330.2 2.4 collective-permute-done.30
  334.6 4.4 %pad_maximum_fusion = bf16[6144,384]{1,0:T(8,128)(2,1)} fusion(bf16[3072,384]{1,0:T(8,128)(2,1)} %collective-permute-done.29, bf16[3072,384]{1,0:T(8,128)(2,1)S(1)} %pad_maximum_fusion.2), kind=kLoop, calls=%fused_computation | loop fusion | flops 9437184 | bytes 9437184 | tf_op jit(solution)/shard_map/concatenate | solution.py:996
  339.1 5.8 %collective-permute-done.34.refs_2_ = bf16[2,256,384]{2,1,0:T(8,128)(2,1)S(1)} collective-permute-done((bf16[2,256,384]{2,1,0:T(8,128)(2,1)}, bf16[2,256,384]{2,1,0:T(8,128)(2,1)S(1)}, u32[]{:S(2)}, u32[]{:S(2)}) %collective-permute-start.34) | collective-permute-done | bytes 393248 | tf_op jit(solution)/shard_map/ppermute | solution.py:978
  344.9 4.3 %collective-permute-done.35.refs_3_ = bf16[2,256,384]{2,1,0:T(8,128)(2,1)S(1)} collective-permute-done((bf16[2,256,384]{2,1,0:T(8,128)(2,1)}, bf16[2,256,384]{2,1,0:T(8,128)(2,1)S(1)}, u32[]{:S(2)}, u32[]{:S(2)}) %collective-permute-start.35) | collective-permute-done | bytes 393248 | tf_op jit(solution)/shard_map/ppermute | solution.py:978
  353.3 3.2 collective-permute-start.38
  356.8 5.3 %collective-permute-done.37 = bf16[112,384]{1,0:T(8,128)(2,1)S(1)} collective-permute-done((bf16[112,384]{1,0:T(8,128)(2,1)S(1)}, bf16[112,384]{1,0:T(8,128)(2,1)S(1)}, u32[]{:S(2)}, u32[]{:S(2)}) %collective-permute-start.37) | collective-permute-done | bytes 86048 | tf_op jit(solution)/shard_map/ppermute | solution.py:973
  362.2 1.6 collective-permute-done.40.refs_2_
  363.8 6.7 %collective-permute-done.41.refs_3_ = bf16[2,256,384]{2,1,0:T(8,128)(2,1)S(1)} collective-permute-done((bf16[2,256,384]{2,1,0:T(8,128)(2,1)S(1)}, bf16[2,256,384]{2,1,0:T(8,128)(2,1)S(1)}, u32[]{:S(2)}, u32[]{:S(2)}) %collective-permute-start.41) | collective-permute-done | bytes 393248 | tf_op jit(solution)/shard_map/ppermute | solution.py:978
  370.5 1.6 collective-permute-start.44
  374.0 9.1 %finish_big.1 = (f32[384,1536]{1,0:T(8,128)}, f32[1536,384]{1,0:T(8,128)}, f32[1536,768]{1,0:T(8,128)}) custom-call(s32[2]{0:T(128)} %pad_add_fusion.rank_ref, bf16[32,192,384]{2,1,0:T(8,128)(2,1)} %bitcast.46), custom_call_target="tpu_custom_call" | custom-call | bytes 15000000 | tf_op jit(solution)/shard_map/finish_big/pallas_call | solution.py:929
  383.1 6.4 %collective-permute-done.43 = bf16[448,384]{1,0:T(8,128)(2,1)} collective-permute-done((bf16[448,384]{1,0:T(8,128)(2,1)S(1)}, bf16[448,384]{1,0:T(8,128)(2,1)}, u32[]{:S(2)}, u32[]{:S(2)}) %collective-permute-start.43) | collective-permute-done | bytes 344096 | tf_op jit(solution)/shard_map/ppermute | solution.py:973
  389.5 2.4 pad_maximum_fusion.3
  392.0 3.7 finish_latents.2.refs_4_
  395.7 3.7 finish_latents.3
  399.3 2.0 pad_maximum_fusion.1
  402.9 3.9 finish_rest.1
  412.7 1.6 reshape.448
  414.3 1.9 fusion.21
  (199 shorter events, 49.0 us)
Async XLA Ops:
  4.1 10.4 %collective-permute-start.2 = (bf16[256,384]{1,0:T(8,128)(2,1)S(1)}, bf16[256,384]{1,0:T(8,128)(2,1)S(1)}, u32[]{:S(2)}, u32[]{:S(2)}) collective-permute-start(bf16[256,384]{1,0:T(8,128)(2,1)S(1)} %get-tuple-element.266), channel_id=1, source_target_pairs={{0,3},{1,2},{2,1},{3,0},{4,7},{5,6},{6,5},{7,4},{8,11},{9,10},{10,... | collective-permute-start | bytes 589832 | tf_op jit(solution)/shard_map/ppermute | solution.py:978
  6.6 9.7 %collective-permute-start.1 = (bf16[256,384]{1,0:T(8,128)(2,1)S(1)}, bf16[256,384]{1,0:T(8,128)(2,1)S(1)}, u32[]{:S(2)}, u32[]{:S(2)}) collective-permute-start(bf16[256,384]{1,0:T(8,128)(2,1)S(1)} %get-tuple-element.267), channel_id=1, source_target_pairs={{0,2},{1,3},{2,0},{3,1},{4,6},{5,7},{6,4},{7,5},{8,10},{9,11},{10,... | collective-permute-start | bytes 589832 | tf_op jit(solution)/shard_map/ppermute | solution.py:978
  7.2 9.0 %collective-permute-start = (bf16[256,384]{1,0:T(8,128)(2,1)S(1)}, bf16[256,384]{1,0:T(8,128)(2,1)S(1)}, u32[]{:S(2)}, u32[]{:S(2)}) collective-permute-start(bf16[256,384]{1,0:T(8,128)(2,1)S(1)} %get-tuple-element.268), channel_id=1, source_target_pairs={{0,1},{1,0},{2,3},{3,2},{4,5},{5,4},{6,7},{7,6},{8,9},{9,8},{10,11... | collective-permute-start | bytes 589832 | tf_op jit(solution)/shard_map/ppermute | solution.py:978
  16.3 12.9 %collective-permute-start.3 = (bf16[256,384]{1,0:T(8,128)(2,1)}, bf16[256,384]{1,0:T(8,128)(2,1)S(1)}, u32[]{:S(2)}, u32[]{:S(2)}) collective-permute-start(bf16[256,384]{1,0:T(8,128)(2,1)} %get-tuple-element.135), channel_id=1, source_target_pairs={{0,1},{1,0},{2,3},{3,2},{4,5},{5,4},{6,7},{7,6},{8,9},{9,8},{10,11... | collective-permute-start | bytes 589832 | tf_op jit(solution)/shard_map/ppermute | solution.py:978
  16.3 12.8 %collective-permute-start.4 = (bf16[256,384]{1,0:T(8,128)(2,1)S(1)}, bf16[256,384]{1,0:T(8,128)(2,1)S(1)}, u32[]{:S(2)}, u32[]{:S(2)}) collective-permute-start(bf16[256,384]{1,0:T(8,128)(2,1)S(1)} %get-tuple-element.136), channel_id=1, source_target_pairs={{0,2},{1,3},{2,0},{3,1},{4,6},{5,7},{6,4},{7,5},{8,10},{9,11},{10,... | collective-permute-start | bytes 589832 | tf_op jit(solution)/shard_map/ppermute | solution.py:978
  18.7 10.5 %collective-permute-start.5 = (bf16[256,384]{1,0:T(8,128)(2,1)S(1)}, bf16[256,384]{1,0:T(8,128)(2,1)S(1)}, u32[]{:S(2)}, u32[]{:S(2)}) collective-permute-start(bf16[256,384]{1,0:T(8,128)(2,1)S(1)} %get-tuple-element.137), channel_id=1, source_target_pairs={{0,3},{1,2},{2,1},{3,0},{4,7},{5,6},{6,5},{7,4},{8,11},{9,10},{10,... | collective-permute-start | bytes 589832 | tf_op jit(solution)/shard_map/ppermute | solution.py:978
  30.0 12.3 %collective-permute-start.6 = (bf16[256,384]{1,0:T(8,128)(2,1)}, bf16[256,384]{1,0:T(8,128)(2,1)S(1)}, u32[]{:S(2)}, u32[]{:S(2)}) collective-permute-start(bf16[256,384]{1,0:T(8,128)(2,1)} %get-tuple-element.139), channel_id=1, source_target_pairs={{0,1},{1,0},{2,3},{3,2},{4,5},{5,4},{6,7},{7,6},{8,9},{9,8},{10,11... | collective-permute-start | bytes 589832 | tf_op jit(solution)/shard_map/ppermute | solution.py:978
  30.1 12.1 %collective-permute-start.7 = (bf16[256,384]{1,0:T(8,128)(2,1)}, bf16[256,384]{1,0:T(8,128)(2,1)S(1)}, u32[]{:S(2)}, u32[]{:S(2)}) collective-permute-start(bf16[256,384]{1,0:T(8,128)(2,1)} %get-tuple-element.140), channel_id=1, source_target_pairs={{0,2},{1,3},{2,0},{3,1},{4,6},{5,7},{6,4},{7,5},{8,10},{9,11},{10,... | collective-permute-start | bytes 589832 | tf_op jit(solution)/shard_map/ppermute | solution.py:978
  32.1 10.2 %collective-permute-start.8 = (bf16[256,384]{1,0:T(8,128)(2,1)}, bf16[256,384]{1,0:T(8,128)(2,1)S(1)}, u32[]{:S(2)}, u32[]{:S(2)}) collective-permute-start(bf16[256,384]{1,0:T(8,128)(2,1)} %get-tuple-element.141), channel_id=1, source_target_pairs={{0,3},{1,2},{2,1},{3,0},{4,7},{5,6},{6,5},{7,4},{8,11},{9,10},{10,... | collective-permute-start | bytes 589832 | tf_op jit(solution)/shard_map/ppermute | solution.py:978
  42.3 12.4 %collective-permute-start.9 = (bf16[256,384]{1,0:T(8,128)(2,1)}, bf16[256,384]{1,0:T(8,128)(2,1)S(1)}, u32[]{:S(2)}, u32[]{:S(2)}) collective-permute-start(bf16[256,384]{1,0:T(8,128)(2,1)} %get-tuple-element.143), channel_id=1, source_target_pairs={{0,1},{1,0},{2,3},{3,2},{4,5},{5,4},{6,7},{7,6},{8,9},{9,8},{10,11... | collective-permute-start | bytes 589832 | tf_op jit(solution)/shard_map/ppermute | solution.py:978
  42.5 12.2 %collective-permute-start.10 = (bf16[256,384]{1,0:T(8,128)(2,1)}, bf16[256,384]{1,0:T(8,128)(2,1)S(1)}, u32[]{:S(2)}, u32[]{:S(2)}) collective-permute-start(bf16[256,384]{1,0:T(8,128)(2,1)} %get-tuple-element.144), channel_id=1, source_target_pairs={{0,2},{1,3},{2,0},{3,1},{4,6},{5,7},{6,4},{7,5},{8,10},{9,11},{10,... | collective-permute-start | bytes 589832 | tf_op jit(solution)/shard_map/ppermute | solution.py:978
  44.5 10.3 %collective-permute-start.11 = (bf16[256,384]{1,0:T(8,128)(2,1)}, bf16[256,384]{1,0:T(8,128)(2,1)}, u32[]{:S(2)}, u32[]{:S(2)}) collective-permute-start(bf16[256,384]{1,0:T(8,128)(2,1)} %get-tuple-element.145), channel_id=1, source_target_pairs={{0,3},{1,2},{2,1},{3,0},{4,7},{5,6},{6,5},{7,4},{8,11},{9,10},{10,... | collective-permute-start | bytes 589832 | tf_op jit(solution)/shard_map/ppermute | solution.py:978
  180.3 14.0 %collective-permute-start.12 = (bf16[3072,384]{1,0:T(8,128)(2,1)}, bf16[3072,384]{1,0:T(8,128)(2,1)}, u32[]{:S(2)}, u32[]{:S(2)}) collective-permute-start(bf16[3072,384]{1,0:T(8,128)(2,1)} %slice.94), channel_id=1, source_target_pairs={{0,1},{1,0},{2,3},{3,2},{4,5},{5,4},{6,7},{7,6},{8,9},{9,8},{10,11... | collective-permute-start | bytes 7077896 | tf_op jit(solution)/shard_map/ppermute | solution.py:973
  199.9 33.0 %collective-permute-start.13 = (bf16[768,384]{1,0:T(8,128)(2,1)}, bf16[768,384]{1,0:T(8,128)(2,1)}, u32[]{:S(2)}, u32[]{:S(2)}) collective-permute-start(bf16[768,384]{1,0:T(8,128)(2,1)} %get-tuple-element.270), channel_id=1, source_target_pairs={{0,4},{1,5},{2,6},{3,7},{4,0},{5,1},{6,2},{7,3},{8,12},{9,13},{10,... | collective-permute-start | bytes 1769480 | tf_op jit(solution)/shard_map/ppermute | solution.py:973
  201.8 31.1 %collective-permute-start.15 = (bf16[768,384]{1,0:T(8,128)(2,1)}, bf16[768,384]{1,0:T(8,128)(2,1)}, u32[]{:S(2)}, u32[]{:S(2)}) collective-permute-start(bf16[768,384]{1,0:T(8,128)(2,1)} %get-tuple-element.271), channel_id=1, source_target_pairs={{0,6},{1,7},{2,4},{3,5},{4,2},{5,3},{6,0},{7,1},{8,14},{9,15},{10,... | collective-permute-start | bytes 1769480 | tf_op jit(solution)/shard_map/ppermute | solution.py:973
  203.3 29.6 %collective-permute-start.14 = (bf16[768,384]{1,0:T(8,128)(2,1)S(1)}, bf16[768,384]{1,0:T(8,128)(2,1)}, u32[]{:S(2)}, u32[]{:S(2)}) collective-permute-start(bf16[768,384]{1,0:T(8,128)(2,1)S(1)} %get-tuple-element.272), channel_id=1, source_target_pairs={{0,2},{1,3},{2,0},{3,1},{4,6},{5,7},{6,4},{7,5},{8,10},{9,11},{10,... | collective-permute-start | bytes 1769480 | tf_op jit(solution)/shard_map/ppermute | solution.py:973
  235.5 20.1 %collective-permute-start.16 = (bf16[192,384]{1,0:T(8,128)(2,1)}, bf16[192,384]{1,0:T(8,128)(2,1)}, u32[]{:S(2)}, u32[]{:S(2)}) collective-permute-start(bf16[192,384]{1,0:T(8,128)(2,1)} %get-tuple-element.276), channel_id=1, source_target_pairs={{0,16},{1,17},{2,18},{3,19},{4,20},{5,21},{6,22},{7,23},{8,24},{9,... | collective-permute-start | bytes 442376 | tf_op jit(solution)/shard_map/ppermute | solution.py:973
  238.5 17.1 %collective-permute-start.18 = (bf16[192,384]{1,0:T(8,128)(2,1)S(1)}, bf16[192,384]{1,0:T(8,128)(2,1)}, u32[]{:S(2)}, u32[]{:S(2)}) collective-permute-start(bf16[192,384]{1,0:T(8,128)(2,1)S(1)} %get-tuple-element.277), channel_id=1, source_target_pairs={{0,24},{1,25},{2,26},{3,27},{4,28},{5,29},{6,30},{7,31},{8,16},{9,... | collective-permute-start | bytes 442376 | tf_op jit(solution)/shard_map/ppermute | solution.py:973
  239.9 15.8 %collective-permute-start.17 = (bf16[192,384]{1,0:T(8,128)(2,1)S(1)}, bf16[192,384]{1,0:T(8,128)(2,1)}, u32[]{:S(2)}, u32[]{:S(2)}) collective-permute-start(bf16[192,384]{1,0:T(8,128)(2,1)S(1)} %get-tuple-element.278), channel_id=1, source_target_pairs={{0,8},{1,9},{2,10},{3,11},{4,12},{5,13},{6,14},{7,15},{8,0},{9,1},... | collective-permute-start | bytes 442376 | tf_op jit(solution)/shard_map/ppermute | solution.py:973
  256.8 21.3 %collective-permute-start.21 = (bf16[192,384]{1,0:T(8,128)(2,1)S(1)}, bf16[192,384]{1,0:T(8,128)(2,1)}, u32[]{:S(2)}, u32[]{:S(2)}) collective-permute-start(bf16[192,384]{1,0:T(8,128)(2,1)S(1)} %add_convert_fusion.5), channel_id=1, source_target_pairs={{0,24},{1,25},{2,26},{3,27},{4,28},{5,29},{6,30},{7,31},{8,16},{9,... | collective-permute-start | bytes 442376 | tf_op jit(solution)/shard_map/ppermute | solution.py:973
  259.8 18.4 %collective-permute-start.20 = (bf16[192,384]{1,0:T(8,128)(2,1)S(1)}, bf16[192,384]{1,0:T(8,128)(2,1)}, u32[]{:S(2)}, u32[]{:S(2)}) collective-permute-start(bf16[192,384]{1,0:T(8,128)(2,1)S(1)} %add_convert_fusion.5), channel_id=1, source_target_pairs={{0,8},{1,9},{2,10},{3,11},{4,12},{5,13},{6,14},{7,15},{8,0},{9,1},... | collective-permute-start | bytes 442376 | tf_op jit(solution)/shard_map/ppermute | solution.py:973
  260.2 17.9 %collective-permute-start.19 = (bf16[192,384]{1,0:T(8,128)(2,1)S(1)}, bf16[192,384]{1,0:T(8,128)(2,1)}, u32[]{:S(2)}, u32[]{:S(2)}) collective-permute-start(bf16[192,384]{1,0:T(8,128)(2,1)S(1)} %add_convert_fusion.5), channel_id=1, source_target_pairs={{0,16},{1,17},{2,18},{3,19},{4,20},{5,21},{6,22},{7,23},{8,24},{9,... | collective-permute-start | bytes 442376 | tf_op jit(solution)/shard_map/ppermute | solution.py:973
  262.4 17.6 %collective-permute-start.22 = (bf16[1024,384]{1,0:T(8,128)(2,1)S(1)}, bf16[1024,384]{1,0:T(8,128)(2,1)}, u32[]{:S(2)}, u32[]{:S(2)}) collective-permute-start(bf16[1024,384]{1,0:T(8,128)(2,1)S(1)} %slice.104), channel_id=1, source_target_pairs={{0,1},{1,0},{2,3},{3,2},{4,5},{5,4},{6,7},{7,6},{8,9},{9,8},{10,11... | collective-permute-start | bytes 2359304 | tf_op jit(solution)/shard_map/ppermute | solution.py:973
  282.4 7.7 %collective-permute-start.26 = (bf16[256,384]{1,0:T(8,128)(2,1)S(1)}, bf16[256,384]{1,0:T(8,128)(2,1)S(1)}, u32[]{:S(2)}, u32[]{:S(2)}) collective-permute-start(bf16[256,384]{1,0:T(8,128)(2,1)S(1)} %get-tuple-element.273), channel_id=1, source_target_pairs={{0,4},{1,5},{2,6},{3,7},{4,0},{5,1},{6,2},{7,3},{8,12},{9,13},{10,... | collective-permute-start | bytes 589832 | tf_op jit(solution)/shard_map/ppermute | solution.py:973
  283.9 39.3 %collective-permute-start.25 = (bf16[768,384]{1,0:T(8,128)(2,1)}, bf16[768,384]{1,0:T(8,128)(2,1)}, u32[]{:S(2)}, u32[]{:S(2)}) collective-permute-start(bf16[768,384]{1,0:T(8,128)(2,1)} %pad_maximum_fusion.4), channel_id=1, source_target_pairs={{0,6},{1,7},{2,4},{3,5},{4,2},{5,3},{6,0},{7,1},{8,14},{9,15},{10,... | collective-permute-start | bytes 1769480 | tf_op jit(solution)/shard_map/ppermute | solution.py:973
  285.4 37.8 %collective-permute-start.24 = (bf16[768,384]{1,0:T(8,128)(2,1)}, bf16[768,384]{1,0:T(8,128)(2,1)}, u32[]{:S(2)}, u32[]{:S(2)}) collective-permute-start(bf16[768,384]{1,0:T(8,128)(2,1)} %pad_maximum_fusion.4), channel_id=1, source_target_pairs={{0,2},{1,3},{2,0},{3,1},{4,6},{5,7},{6,4},{7,5},{8,10},{9,11},{10,... | collective-permute-start | bytes 1769480 | tf_op jit(solution)/shard_map/ppermute | solution.py:973
  285.9 37.4 %collective-permute-start.23 = (bf16[768,384]{1,0:T(8,128)(2,1)}, bf16[768,384]{1,0:T(8,128)(2,1)}, u32[]{:S(2)}, u32[]{:S(2)}) collective-permute-start(bf16[768,384]{1,0:T(8,128)(2,1)} %pad_maximum_fusion.4), channel_id=1, source_target_pairs={{0,4},{1,5},{2,6},{3,7},{4,0},{5,1},{6,2},{7,3},{8,12},{9,13},{10,... | collective-permute-start | bytes 1769480 | tf_op jit(solution)/shard_map/ppermute | solution.py:973
  287.3 33.1 %collective-permute-start.28 = (bf16[256,384]{1,0:T(8,128)(2,1)}, bf16[256,384]{1,0:T(8,128)(2,1)}, u32[]{:S(2)}, u32[]{:S(2)}) collective-permute-start(bf16[256,384]{1,0:T(8,128)(2,1)} %get-tuple-element.274), channel_id=1, source_target_pairs={{0,6},{1,7},{2,4},{3,5},{4,2},{5,3},{6,0},{7,1},{8,14},{9,15},{10,... | collective-permute-start | bytes 589832 | tf_op jit(solution)/shard_map/ppermute | solution.py:973
  290.1 31.9 %collective-permute-start.27 = (bf16[256,384]{1,0:T(8,128)(2,1)S(1)}, bf16[256,384]{1,0:T(8,128)(2,1)}, u32[]{:S(2)}, u32[]{:S(2)}) collective-permute-start(bf16[256,384]{1,0:T(8,128)(2,1)S(1)} %get-tuple-element.275), channel_id=1, source_target_pairs={{0,2},{1,3},{2,0},{3,1},{4,6},{5,7},{6,4},{7,5},{8,10},{9,11},{10,... | collective-permute-start | bytes 589832 | tf_op jit(solution)/shard_map/ppermute | solution.py:973
  325.1 9.6 %collective-permute-start.29 = (bf16[3072,384]{1,0:T(8,128)(2,1)S(1)}, bf16[3072,384]{1,0:T(8,128)(2,1)}, u32[]{:S(2)}, u32[]{:S(2)}) collective-permute-start(bf16[3072,384]{1,0:T(8,128)(2,1)S(1)} %pad_maximum_fusion.2), channel_id=1, source_target_pairs={{0,1},{1,0},{2,3},{3,2},{4,5},{5,4},{6,7},{7,6},{8,9},{9,8},{10,11... | collective-permute-start | bytes 7077896 | tf_op jit(solution)/shard_map/ppermute | solution.py:973
  326.0 13.0 %collective-permute-start.33 = (bf16[2,256,384]{2,1,0:T(8,128)(2,1)}, bf16[2,256,384]{2,1,0:T(8,128)(2,1)S(1)}, u32[]{:S(2)}, u32[]{:S(2)}) collective-permute-start(bf16[2,256,384]{2,1,0:T(8,128)(2,1)} %get-tuple-element.215), channel_id=1, source_target_pairs={{0,1},{1,0},{2,3},{3,2},{4,5},{5,4},{6,7},{7,6},{8,9},{9,8},{10,11... | collective-permute-start | bytes 1179656 | tf_op jit(solution)/shard_map/ppermute | solution.py:978
  326.6 6.0 %collective-permute-start.30 = (bf16[64,384]{1,0:T(8,128)(2,1)S(1)}, bf16[64,384]{1,0:T(8,128)(2,1)S(1)}, u32[]{:S(2)}, u32[]{:S(2)}) collective-permute-start(bf16[64,384]{1,0:T(8,128)(2,1)S(1)} %get-tuple-element.279), channel_id=1, source_target_pairs={{0,16},{1,17},{2,18},{3,19},{4,20},{5,21},{6,22},{7,23},{8,24},{9,... | collective-permute-start | bytes 147464 | tf_op jit(solution)/shard_map/ppermute | solution.py:973
  328.6 5.9 %collective-permute-start.32 = (bf16[64,384]{1,0:T(8,128)(2,1)S(1)}, bf16[64,384]{1,0:T(8,128)(2,1)S(1)}, u32[]{:S(2)}, u32[]{:S(2)}) collective-permute-start(bf16[64,384]{1,0:T(8,128)(2,1)S(1)} %get-tuple-element.280), channel_id=1, source_target_pairs={{0,24},{1,25},{2,26},{3,27},{4,28},{5,29},{6,30},{7,31},{8,16},{9,... | collective-permute-start | bytes 147464 | tf_op jit(solution)/shard_map/ppermute | solution.py:973
  329.9 4.6 %collective-permute-start.31 = (bf16[64,384]{1,0:T(8,128)(2,1)S(1)}, bf16[64,384]{1,0:T(8,128)(2,1)S(1)}, u32[]{:S(2)}, u32[]{:S(2)}) collective-permute-start(bf16[64,384]{1,0:T(8,128)(2,1)S(1)} %get-tuple-element.281), channel_id=1, source_target_pairs={{0,8},{1,9},{2,10},{3,11},{4,12},{5,13},{6,14},{7,15},{8,0},{9,1},... | collective-permute-start | bytes 147464 | tf_op jit(solution)/shard_map/ppermute | solution.py:973
  332.6 12.3 %collective-permute-start.34 = (bf16[2,256,384]{2,1,0:T(8,128)(2,1)}, bf16[2,256,384]{2,1,0:T(8,128)(2,1)S(1)}, u32[]{:S(2)}, u32[]{:S(2)}) collective-permute-start(bf16[2,256,384]{2,1,0:T(8,128)(2,1)} %get-tuple-element.216), channel_id=1, source_target_pairs={{0,2},{1,3},{2,0},{3,1},{4,6},{5,7},{6,4},{7,5},{8,10},{9,11},{10,... | collective-permute-start | bytes 1179656 | tf_op jit(solution)/shard_map/ppermute | solution.py:978
  334.6 14.7 %collective-permute-start.35 = (bf16[2,256,384]{2,1,0:T(8,128)(2,1)}, bf16[2,256,384]{2,1,0:T(8,128)(2,1)S(1)}, u32[]{:S(2)}, u32[]{:S(2)}) collective-permute-start(bf16[2,256,384]{2,1,0:T(8,128)(2,1)} %get-tuple-element.217), channel_id=1, source_target_pairs={{0,3},{1,2},{2,1},{3,0},{4,7},{5,6},{6,5},{7,4},{8,11},{9,10},{10,... | collective-permute-start | bytes 1179656 | tf_op jit(solution)/shard_map/ppermute | solution.py:978
  339.1 44.0 %copy-start.3 = (bf16[2,256,384]{2,1,0:T(8,128)(2,1)}, bf16[2,256,384]{2,1,0:T(8,128)(2,1)S(1)}, u32[]{:S(2)}) copy-start(bf16[2,256,384]{2,1,0:T(8,128)(2,1)S(1)} %collective-permute-done.33.refs_1_) | copy-start | bytes 1179652
  344.9 27.1 %copy-start.4 = (bf16[2,256,384]{2,1,0:T(8,128)(2,1)}, bf16[2,256,384]{2,1,0:T(8,128)(2,1)S(1)}, u32[]{:S(2)}) copy-start(bf16[2,256,384]{2,1,0:T(8,128)(2,1)S(1)} %collective-permute-done.34.refs_2_) | copy-start | bytes 1179652
  349.3 7.5 %collective-permute-start.36 = (bf16[112,384]{1,0:T(8,128)(2,1)S(1)}, bf16[112,384]{1,0:T(8,128)(2,1)S(1)}, u32[]{:S(2)}, u32[]{:S(2)}) collective-permute-start(bf16[112,384]{1,0:T(8,128)(2,1)S(1)} %pad_maximum_fusion.5), channel_id=1, source_target_pairs={{0,16},{1,17},{2,18},{3,19},{4,20},{5,21},{6,22},{7,23},{8,24},{9,... | collective-permute-start | bytes 258056 | tf_op jit(solution)/shard_map/ppermute | solution.py:973
  350.4 11.8 %collective-permute-start.39 = (bf16[2,256,384]{2,1,0:T(8,128)(2,1)S(1)}, bf16[2,256,384]{2,1,0:T(8,128)(2,1)S(1)}, u32[]{:S(2)}, u32[]{:S(2)}) collective-permute-start(bf16[2,256,384]{2,1,0:T(8,128)(2,1)S(1)} %copy-done.32), channel_id=1, source_target_pairs={{0,1},{1,0},{2,3},{3,2},{4,5},{5,4},{6,7},{7,6},{8,9},{9,8},{10,11... | collective-permute-start | bytes 1179656 | tf_op jit(solution)/shard_map/ppermute | solution.py:978
  351.8 12.0 %collective-permute-start.40 = (bf16[2,256,384]{2,1,0:T(8,128)(2,1)S(1)}, bf16[2,256,384]{2,1,0:T(8,128)(2,1)S(1)}, u32[]{:S(2)}, u32[]{:S(2)}) collective-permute-start(bf16[2,256,384]{2,1,0:T(8,128)(2,1)S(1)} %copy-done.31), channel_id=1, source_target_pairs={{0,2},{1,3},{2,0},{3,1},{4,6},{5,7},{6,4},{7,5},{8,10},{9,11},{10,... | collective-permute-start | bytes 1179656 | tf_op jit(solution)/shard_map/ppermute | solution.py:978
  352.3 18.2 %collective-permute-start.41 = (bf16[2,256,384]{2,1,0:T(8,128)(2,1)S(1)}, bf16[2,256,384]{2,1,0:T(8,128)(2,1)S(1)}, u32[]{:S(2)}, u32[]{:S(2)}) collective-permute-start(bf16[2,256,384]{2,1,0:T(8,128)(2,1)S(1)} %copy-done.30), channel_id=1, source_target_pairs={{0,3},{1,2},{2,1},{3,0},{4,7},{5,6},{6,5},{7,4},{8,11},{9,10},{10,... | collective-permute-start | bytes 1179656 | tf_op jit(solution)/shard_map/ppermute | solution.py:978
  353.3 8.9 %collective-permute-start.38 = (bf16[112,384]{1,0:T(8,128)(2,1)S(1)}, bf16[112,384]{1,0:T(8,128)(2,1)S(1)}, u32[]{:S(2)}, u32[]{:S(2)}) collective-permute-start(bf16[112,384]{1,0:T(8,128)(2,1)S(1)} %pad_maximum_fusion.5), channel_id=1, source_target_pairs={{0,24},{1,25},{2,26},{3,27},{4,28},{5,29},{6,30},{7,31},{8,16},{9,... | collective-permute-start | bytes 258056 | tf_op jit(solution)/shard_map/ppermute | solution.py:973
  356.8 5.3 %collective-permute-start.37 = (bf16[112,384]{1,0:T(8,128)(2,1)S(1)}, bf16[112,384]{1,0:T(8,128)(2,1)S(1)}, u32[]{:S(2)}, u32[]{:S(2)}) collective-permute-start(bf16[112,384]{1,0:T(8,128)(2,1)S(1)} %pad_maximum_fusion.5), channel_id=1, source_target_pairs={{0,8},{1,9},{2,10},{3,11},{4,12},{5,13},{6,14},{7,15},{8,0},{9,1},... | collective-permute-start | bytes 258056 | tf_op jit(solution)/shard_map/ppermute | solution.py:973
  370.5 12.6 %collective-permute-start.44 = (bf16[448,384]{1,0:T(8,128)(2,1)S(1)}, bf16[448,384]{1,0:T(8,128)(2,1)}, u32[]{:S(2)}, u32[]{:S(2)}) collective-permute-start(bf16[448,384]{1,0:T(8,128)(2,1)S(1)} %constant_dynamic-update-slice_fusion), channel_id=1, source_target_pairs={{0,6},{1,7},{2,4},{3,5},{4,2},{5,3},{6,0},{7,1},{8,14},{9,15},{10,... | collective-permute-start | bytes 1032200 | tf_op jit(solution)/shard_map/ppermute | solution.py:973
  372.0 17.5 %collective-permute-start.43 = (bf16[448,384]{1,0:T(8,128)(2,1)S(1)}, bf16[448,384]{1,0:T(8,128)(2,1)}, u32[]{:S(2)}, u32[]{:S(2)}) collective-permute-start(bf16[448,384]{1,0:T(8,128)(2,1)S(1)} %constant_dynamic-update-slice_fusion), channel_id=1, source_target_pairs={{0,2},{1,3},{2,0},{3,1},{4,6},{5,7},{6,4},{7,5},{8,10},{9,11},{10,... | collective-permute-start | bytes 1032200 | tf_op jit(solution)/shard_map/ppermute | solution.py:973
  373.4 16.1 %collective-permute-start.42 = (bf16[448,384]{1,0:T(8,128)(2,1)S(1)}, bf16[448,384]{1,0:T(8,128)(2,1)}, u32[]{:S(2)}, u32[]{:S(2)}) collective-permute-start(bf16[448,384]{1,0:T(8,128)(2,1)S(1)} %constant_dynamic-update-slice_fusion), channel_id=1, source_target_pairs={{0,4},{1,5},{2,6},{3,7},{4,0},{5,1},{6,2},{7,3},{8,12},{9,13},{10,... | collective-permute-start | bytes 1032200 | tf_op jit(solution)/shard_map/ppermute | solution.py:973
  391.9 7.4 %collective-permute-start.45 = (bf16[1792,384]{1,0:T(8,128)(2,1)}, bf16[1792,384]{1,0:T(8,128)(2,1)}, u32[]{:S(2)}, u32[]{:S(2)}) collective-permute-start(bf16[1792,384]{1,0:T(8,128)(2,1)} %pad_maximum_fusion.3), channel_id=1, source_target_pairs={{0,1},{1,0},{2,3},{3,2},{4,5},{5,4},{6,7},{7,6},{8,9},{9,8},{10,11... | collective-permute-start | bytes 4128776 | tf_op jit(solution)/shard_map/ppermute | solution.py:973
  (35 other events, 216.1 us)
where the time goes:
time: 422 us; the launch traced here: 417 us
  Pallas kernels  262 us (62%)
  waiting for transfers between devices  52.4 us (12%)
  starting transfers between devices  46.1 us (11%)
  local copies, waits for them, and re-layouts  26.3 us (6%)
  other arithmetic  25.5 us (6%)
    pallas_call x1, Pallas kernels, feed_forward_call(): pl.pallas_call(functools.partial(feed_forward_kernel, parts=parts), grid_...  111 us
    pallas_call x4, Pallas kernels, attention_back_call(): pl.pallas_call(functools.partial(attention_back_kernel, parts=parts, begi...  58.8 us
    pallas_call x4, Pallas kernels, attention_forward_call(): pl.pallas_call(functools.partial(attention_forward_kernel, strips, begin)...  40.9 us
    ppermute x28, starting transfers between devices, exchange(): return lax.ppermute(values, AXES, [(i, i ^ mask) for i in range(devices)])  32.3 us
    ppermute x28, waiting for transfers between devices, exchange(): return lax.ppermute(values, AXES, [(i, i ^ mask) for i in range(devices)])  32.2 us
    pallas_call x2, Pallas kernels, conv_attn_back_call(): pl.pallas_call(functools.partial(conv_attn_back_kernel, strips), grid_spe...  30.8 us
    ppermute x18, waiting for transfers between devices, swap_strips(): return lax.ppermute(values, 'narrow', [(i, i ^ mask) for i in range(count)])  20.2 us
    ppermute x18, starting transfers between devices, swap_strips(): return lax.ppermute(values, 'narrow', [(i, i ^ mask) for i in range(count)])  13.8 us
  transfers between devices with their start and end apart: 46, of which 13 were waited for; matrix products, arithmetic and copies ran while one was open for 4% of the time, Pallas kernels for 33%

commit v1 on v0

--- a/solution.py
+++ b/solution.py
@@ -167,7 +167,6 @@
     cols = tokens // 16
     width = xp_ref.shape[2]
     quarter = perm.shape[0] // 4
-    all_lanes = pl.ds(0, width)
     for ref in (plain_h, moved_h):
         zero_pads(ref, cols)
     shift_one, scale_one = (mod_ref[0, pl.ds(part, 1), :] for part in range(2))
@@ -182,7 +181,7 @@
     for plane in range(4):
         unit, _ = normed(xp_ref[0, pl.ds(plane * tokens, tokens), :].astype(F32))
         low = (unit * (1.0 + scale_one) + shift_one).astype(BF)
-        fill_planes(plain_h, moved_h, plane, moves[plane % 2], low, cols, all_lanes)
+        fill_planes(plain_h, moved_h, plane, moves[plane % 2], low, cols, pl.ds(0, width))
     for plane in range(4):
         for lane in range(0, width, LANES):
             for start in range(0, tokens, 128):
@@ -200,11 +199,12 @@
         qkv_ref[0, rows, :] = mm(co_ref[0, rows, :], qkv_w[...]).astype(BF)
         even = lax.broadcasted_iota(jnp.int32, (tokens, LANES), 1) < head_size
         scores = []
+        zero = jnp.zeros((tokens, LANES), BF)
         for pair in range(width // LANES):
             query = qkv_ref[0, rows, pl.ds(pair * LANES, LANES)]
             key = qkv_ref[0, rows, pl.ds(width + pair * LANES, LANES)] * jnp.asarray(factor, BF)
-            for mine in (even, ~even):
-                scores.append(mm(jnp.where(mine, key, jnp.zeros_like(key)), query, NT))
+            both = mm(jnp.concatenate([jnp.where(even, key, zero), jnp.where(even, zero, key)], axis=0), query, NT)
+            scores += [both[:tokens], both[tokens:]]
         tops = [jnp.max(score, axis=0, keepdims=True) for score in scores]
         grown = [jnp.exp(score - top) for score, top in zip(scores, tops)]
         totals = [col_sum(values) for values in grown]
@@ -461,20 +461,15 @@
     *rest,
     parts,
     begin,
-    fresh,
     last,
 ):
     image = pl.program_id(0)
     width = mix_ref.shape[2]
     tokens = mix_ref.shape[1] // 4
-    rest = list(rest)
-    before_ref = None if begin else rest.pop(0)
-    if not fresh:
-        rest.pop(0)
-    gqkv_ref = rest.pop(0)
-    sum_ref = rest.pop(0)
-    rows_ref = rest.pop(0) if last else None
-    gout_s, gmix_s = rest
+    before_ref = None if begin else rest[0]
+    gqkv_ref, sum_ref = rest[0 if begin else 1 :][:2]
+    rows_ref = rest[-3] if last else None
+    gout_s, gmix_s = rest[-2:]
 
     @pl.when(image == 0)
     def _():
@@ -499,26 +494,24 @@
             query_low = query * factor
             key_t = key.T
             grad_mixed = gmix_s[:, pl.ds(lane, LANES)]
-            masks = (even, ~even)
-            scores = [mm(jnp.where(mine, key, zero), query, NT) for mine in masks]
-            grad_probs = [mm(jnp.where(mine, value, zero), grad_mixed, NT) for mine in masks]
-            probs = [
-                jnp.exp(score - stat_ref[0, plane, pl.ds(2 * pair + half, 1), :])
-                for half, score in enumerate(scores)
-            ]
-            weighted = [a * b for a, b in zip(probs, grad_probs)]
-            inner = [col_sum(values) for values in weighted]
-            grad_scores = [
-                (values - prob * total).astype(BF)
-                for values, prob, total in zip(weighted, probs, inner)
-            ]
-            grad_value = sum(
-                mm(prob.astype(BF), jnp.where(mine, grad_mixed, zero))
-                for prob, mine in zip(probs, masks)
-            )
-            grad_key = sum(
-                mm(values, jnp.where(mine, query_low, zero)) for values, mine in zip(grad_scores, masks)
-            )
+
+            def heads(values):
+                return jnp.concatenate([jnp.where(even, values, zero), jnp.where(even, zero, values)], axis=0)
+
+            def joined(values):
+                return jnp.where(even, values[:tokens], values[tokens:])
+
+            scores = mm(heads(key), query, NT)
+            grad_probs = mm(heads(value), grad_mixed, NT)
+            probs, grad_scores = [], []
+            for half in range(2):
+                part = slice(half * tokens, (half + 1) * tokens)
+                prob = jnp.exp(scores[part] - stat_ref[0, plane, pl.ds(2 * pair + half, 1), :])
+                weighted = prob * grad_probs[part]
+                probs.append(prob.astype(BF))
+                grad_scores.append((weighted - prob * col_sum(weighted)).astype(BF))
+            grad_value = joined(mm(jnp.concatenate(probs, axis=0), grad_mixed))
+            grad_key = joined(mm(jnp.concatenate(grad_scores, axis=0), query_low))
             grad_query_t = jnp.concatenate(
                 [
                     mm(key_t[half * head_size : (half + 1) * head_size], grad_scores[half])
@@ -539,18 +532,19 @@
         lanes = pl.ds(part * width, width)
         sum_ref[:, lanes] += mm(conv_t, gqkv_ref[0, :, lanes])
 
-    if last:
-
-        @pl.when(image == pl.num_programs(0) - 1)
-        def _():
-            rank = rank_ref[0]
-            rows_ref[...] = jnp.zeros(rows_ref.shape, BF)
-            for part in range(4):
-                lanes = pl.ds(part * width, width)
-                place_rows(rows_ref, sum_ref[:, lanes].astype(BF), part * width, rank, parts)
-            for part in range(4):
-                lanes = pl.ds(part * width, width)
-                place_rows(rows_ref, small_ref[:, lanes].astype(BF), 4 * width + part * 16, rank, parts)
+    if not last:
+        return
+
+    @pl.when(image == pl.num_programs(0) - 1)
+    def _():
+        rank = rank_ref[0]
+        rows_ref[...] = jnp.zeros(rows_ref.shape, BF)
+        for part in range(4):
+            lanes = pl.ds(part * width, width)
+            place_rows(rows_ref, sum_ref[:, lanes].astype(BF), part * width, rank, parts)
+        for part in range(4):
+            lanes = pl.ds(part * width, width)
+            place_rows(rows_ref, small_ref[:, lanes].astype(BF), 4 * width + part * 16, rank, parts)
 
 
 def conv_attn_back_kernel(
@@ -573,7 +567,6 @@
     cols = tokens // 16
     width = xp_ref.shape[2]
     quarter = perm_back.shape[0] // 4
-    all_lanes = pl.ds(0, width)
 
     @pl.when(image == 0)
     def _():
@@ -587,7 +580,7 @@
     for plane in range(4):
         rows = pl.ds(plane * tokens, tokens)
         grad_conv = mm(gqkv_ref[0, rows, :], qkv_w[...], NT).astype(BF)
-        fill_planes(plain_g, moved_g, plane, moves[plane % 2], grad_conv, cols, all_lanes)
+        fill_planes(plain_g, moved_g, plane, moves[plane % 2], grad_conv, cols, pl.ds(0, width))
         unit, _ = normed(xp_ref[0, rows, :].astype(F32))
         low = (unit * (1.0 + scale_one) + shift_one).astype(BF)
         plain_h[rows, :] = low.astype(F32)
@@ -643,19 +636,15 @@
 FINISH_STEPS = 8
 
 
-def finish_big_kernel(rank_ref, rows_ref, fc1_ref, fc2_ref, down_ref):
+def finish_big_kernel(*refs):
+    rows, (fc1_ref, fc2_ref, down_ref) = refs[:-3], refs[-3:]
     step = pl.program_id(0)
-    count, share, width = rows_ref.shape
-    inner = rank_ref[0] % count
+    share, width = rows[0].shape
 
     def write(ref, flat):
-        for at in range(count):
-            values = rows_ref[at ^ inner].astype(F32)
-            if flat:
-                ref[pl.ds(at * share, share), :] = values
-            else:
-                block, row = divmod(at * share, width)
-                ref[pl.ds(row, share), pl.ds(block * width, width)] = values
+        for at, rows_ref in enumerate(rows):
+            block, row = (0, at * share) if flat else divmod(at * share, width)
+            ref[pl.ds(row, share), pl.ds(block * width, width)] = rows_ref[...].astype(F32)
 
     @pl.when(step < 2)
     def _():
@@ -670,11 +659,34 @@
         write(fc1_ref, False)
 
 
-def finish_rest_kernel(rank_ref, rows_ref, qkv_ref, proj_ref, small_ref, *, share):
+def finish_rest_kernel(
+    rank_ref,
+    own_ref,
+    other_ref,
+    qkv_ref,
+    proj_ref,
+    conv_ffn_ref,
+    fc1b_ref,
+    fc2b_ref,
+    downb_ref,
+    conv_ref,
+    ada_ref,
+    bias_ref,
+    *,
+    share,
+    images,
+    features,
+):
     width = proj_ref.shape[0]
     rank = rank_ref[0]
-    for part in range(rows_ref.shape[0]):
-        values = rows_ref[part ^ rank, pl.ds(0, share), :].astype(F32)
+    half = own_ref.shape[0]
+    near = rank < half
+    for part in range(2 * half):
+        at = (part ^ rank) % half
+        rows = pl.ds(0, share)
+        own, other = own_ref[at, rows, :], other_ref[at, rows, :]
+        is_own = near if part < half else ~near
+        values = jnp.where(is_own, own.astype(F32), other.astype(F32))
         block, row = divmod(part * share, width)
         if block < 3:
             qkv_ref[pl.ds(row, share), pl.ds(block * width, width)] = values
@@ -682,9 +694,40 @@
             proj_ref[pl.ds(row, share), :] = values
         elif block == 4 and row < 64:
             small = min(share, 16)
-            for at in range(0, share, small):
-                lanes = pl.ds((row + at) // 16 * width, width)
-                small_ref[:, lanes] = values[at : at + small]
+            for first in range(0, share, small):
+                block = (row + first) // 16
+                lanes = pl.ds(block * width, width)
+                for tap in range(9):
+                    conv_ffn_ref[tap // 3, pl.ds(tap % 3, 1), lanes] = values[first + tap : first + tap + 1]
+                fc1b_ref[lanes] = values[first + 9]
+                if block == 0:
+                    fc2b_ref[...] = values[first + 10]
+                elif block < 3:
+                    downb_ref[pl.ds((block - 1) * width, width)] = values[first + 10]
+    conv = jnp.zeros((16, width), F32)
+    for ref in (own_ref, other_ref):
+        for at in range(half):
+            conv += ref[at, pl.ds(share, 16), :].astype(F32)
+    for tap in range(9):
+        conv_ref[tap // 3, pl.ds(tap % 3, 1), :] = conv[tap : tap + 1]
+    per_tile = 8 // images
+    tiles = -(-6 // per_tile)
+
+    def tile(index, lanes):
+        rows = pl.ds(share + 16 + 8 * index, 8)
+        return jnp.concatenate(
+            [ref[:, rows, lanes].reshape(8 * half, lanes.size) for ref in (own_ref, other_ref)], axis=0
+        )
+
+    cond = tile(tiles, pl.ds(0, features))
+    slot = lax.broadcasted_iota(jnp.int32, cond.shape, 0) % 8 // images
+    for part in range(6):
+        chosen = jnp.where(slot == part % per_tile, cond, jnp.zeros_like(cond))
+        ones = jnp.where(slot == part % per_tile, jnp.ones_like(cond), jnp.zeros_like(cond))[:, :LANES]
+        grads = tile(part // per_tile, pl.ds(0, width))
+        lanes = pl.ds(part * width, width)
+        ada_ref[:, lanes] = mm(chosen, grads, TN)
+        bias_ref[lanes] = mm(ones, grads, TN)[0]
 
 
 def per_image(shape, first=0):
@@ -812,44 +855,38 @@
     )
 
 
-def attention_back_call(rank, parts, image, last, group, mod, gmid, co, qkv, mix, stat, proj_w, small, before, held):
-    width = mix.shape[2]
-    all_tokens = mix.shape[1]
+def attention_back_call(rank, parts, group, mod, gmid, co, qkv, mix, stat, proj_w, small, before):
+    images, all_tokens, width = mix.shape
     first, count = group
-    begin = before is None
-    fresh = held is None
+    begin, last = before is None, first + count == images
     per = (mod, gmid, co, qkv, mix, stat)
     shared = (proj_w, small) + (() if begin else (before,))
-    aliased = () if fresh else (held,)
+    share = 64 if parts <= 32 else 16
     outs = [((count,) + qkv.shape[1:], BF)]
-    share = 64 if parts <= 32 else 16
     sums = [((width, 4 * width), F32)] + ([((share * parts, width), BF)] if last else [])
     grid = pltpu.PrefetchScalarGridSpec(
         num_scalar_prefetch=1,
-        grid=(1,),
-        in_specs=[per_image(v.shape, image) for v in per]
-        + [resident(w.shape) for w in shared]
-        + [pl.BlockSpec(memory_space=pl.ANY)] * len(aliased),
-        out_specs=[per_image(s, image - first) for s, _ in outs] + [resident(s) for s, _ in sums],
+        grid=(count,),
+        in_specs=[per_image(v.shape, first) for v in per] + [resident(w.shape) for w in shared],
+        out_specs=[per_image(s) for s, _ in outs] + [resident(s) for s, _ in sums],
         scratch_shapes=[
             pltpu.VMEM((all_tokens, width), BF),
             pltpu.VMEM((all_tokens // 4, width), BF),
         ],
     )
     return pl.pallas_call(
-        functools.partial(attention_back_kernel, parts=parts, begin=begin, fresh=fresh, last=last),
+        functools.partial(attention_back_kernel, parts=parts, begin=begin, last=last),
         grid_spec=grid,
         out_shape=[out_of(s, d) for s, d in outs + sums],
-        input_output_aliases={} if fresh else {1 + len(per) + len(shared): 0},
         compiler_params=PARAMS,
-        cost_estimate=cost(1, 8e9, 10e6),
+        cost_estimate=cost(count, 8e9, 10e6),
         name="attention_back",
-    )(rank, *per, *shared, *aliased)
-
-
-def conv_attn_back_call(rank, strips, first, xp, mod, gmid, gqkv, weights, perm_back, moves):
+    )(rank, *per, *shared)
+
+
+def conv_attn_back_call(rank, strips, first, skip, images, xp, mod, gmid, gqkv, weights, perm_back, moves):
     qkv_w, conv_a = weights
-    images, all_tokens, width = gqkv.shape[0], xp.shape[1], xp.shape[2]
+    all_tokens, width = xp.shape[1:]
     tokens = moves.shape[1]
     padded = tokens + 32
     shared = (qkv_w, conv_a, perm_back, moves)
@@ -859,7 +896,7 @@
         num_scalar_prefetch=1,
         grid=(images,),
         in_specs=[per_image(v.shape, first) for v in (xp, mod, gmid)]
-        + [per_image(gqkv.shape)]
+        + [per_image(gqkv.shape, skip)]
         + [resident(w.shape) for w in shared],
         out_specs=[per_image(s) for s, _ in outs] + [resident(s) for s in sums],
         scratch_shapes=[
@@ -910,56 +947,68 @@
     )(rank, *pieces, *held)
 
 
-def finish_big_call(rank, rows, hidden, width):
-    parts, share, _ = rows.shape
-    count = parts // FINISH_STEPS
+def finish_big_call(rows, devices, order, hidden, width):
+    count = devices // FINISH_STEPS
+    share = rows.shape[0] // devices
     deep = count * share
-    grid = pltpu.PrefetchScalarGridSpec(
-        num_scalar_prefetch=1,
-        grid=(FINISH_STEPS,),
-        in_specs=[pl.BlockSpec((count, share, width), lambda i, rank: (i ^ (rank[0] // count), 0, 0))],
-        out_specs=[
-            pl.BlockSpec((width, deep), lambda i, rank: (0, jnp.maximum(i - 6, 0))),
-            pl.BlockSpec((deep, width), lambda i, rank: (jnp.minimum(i, 1), 0)),
-            pl.BlockSpec(
-                (deep, width), lambda i, rank: (jnp.clip(i - 2, 0, 3) % 2, jnp.clip(i - 2, 0, 3) // 2)
-            ),
-        ],
-    )
+    def owner(part):
+        return sum(((part >> at) & 1) << bit for at, bit in enumerate(reversed(order)))
+
     return pl.pallas_call(
         finish_big_kernel,
-        grid_spec=grid,
+        grid=(FINISH_STEPS,),
+        in_specs=[
+            pl.BlockSpec((share, width), lambda i, at=at: (owner(i * count + at), 0)) for at in range(count)
+        ],
+        out_specs=[
+            pl.BlockSpec((width, deep), lambda i: (0, jnp.maximum(i - 6, 0))),
+            pl.BlockSpec((deep, width), lambda i: (jnp.minimum(i, 1), 0)),
+            pl.BlockSpec((deep, width), lambda i: (jnp.clip(i - 2, 0, 3) % 2, jnp.clip(i - 2, 0, 3) // 2)),
+        ],
         out_shape=[out_of((width, hidden), F32), out_of((hidden, width), F32), out_of((hidden, 2 * width), F32)],
         compiler_params=PARAMS,
         cost_estimate=cost(1, 0, 15e6),
         name="finish_big",
-    )(rank, rows)
-
-
-def finish_rest_call(rank, rows, share, width):
-    shapes = [(width, 3 * width), (width, width), (16, 4 * width)]
+    )(*[rows] * count)
+
+
+def finish_rest_call(rank, own, other, share, width, images, features):
+    shapes = [
+        (width, 3 * width),
+        (width, width),
+        (3, 3, 4 * width),
+        (4 * width,),
+        (width,),
+        (2 * width,),
+        (3, 3, width),
+        (features, 6 * width),
+        (6 * width,),
+    ]
     grid = pltpu.PrefetchScalarGridSpec(
         num_scalar_prefetch=1,
         grid=(1,),
-        in_specs=[resident(rows.shape)],
+        in_specs=[resident(own.shape), resident(other.shape)],
         out_specs=[resident(shape) for shape in shapes],
     )
     return pl.pallas_call(
-        functools.partial(finish_rest_kernel, share=share),
+        functools.partial(finish_rest_kernel, share=share, images=images, features=features),
         grid_spec=grid,
         out_shape=[out_of(shape, F32) for shape in shapes],
         compiler_params=PARAMS,
-        cost_estimate=cost(1, 0, 5e6),
+        cost_estimate=cost(1, 0, 8e6),
         name="finish_rest",
-    )(rank, rows)
-
-
-def stages(devices):
-    bits = devices.bit_length() - 1
-    found = [[1]]
-    for at in range(1, bits, 2):
-        group = [1 << b for b in range(at, min(at + 2, bits))]
-        found.append(group)
+    )(rank, own, other)
+
+
+def bit_order(devices, narrow):
+    bits, near = devices.bit_length() - 1, narrow.bit_length() - 1
+    return [0, *range(near, bits), *range(1, near)]
+
+
+def stages(order):
+    found = [[1 << order[0]]]
+    for at in range(1, len(order), 2):
+        found.append([1 << bit for bit in order[at : at + 2]])
     return found
 
 
@@ -998,12 +1047,11 @@
     )
 
 
-def flat_rank(devices):
+def flat_rank(order):
     index = lax.axis_index("wide") * lax.axis_size("narrow") + lax.axis_index("narrow")
     rank = jnp.zeros((), jnp.int32)
-    bits = devices.bit_length() - 1
-    for bit in range(bits):
-        rank = rank | (((index >> bit) & 1) << (bits - 1 - bit))
+    for bit in order:
+        rank = 2 * rank + ((index >> bit) & 1)
     return jnp.stack([rank, lax.axis_index("narrow")])
 
 
@@ -1028,8 +1076,9 @@
     height = latents.shape[1] * lax.axis_size("narrow")
     hidden = fc1_weight.shape[1]
     devices = lax.axis_size("wide") * lax.axis_size("narrow")
-    rank = flat_rank(devices)
-    steps = stages(devices)
+    order = bit_order(devices, lax.axis_size("narrow"))
+    rank = flat_rank(order)
+    steps = stages(order)
     strips = lax.axis_size("narrow")
     strip_tokens = latents.shape[1] * cols
     place = lax.axis_index("narrow")
@@ -1085,125 +1134,111 @@
         ),
         moves,
     )
-    halves = [(0, images)] if images == 1 else [(0, images // 2), (images // 2, images - images // 2)]
-    calls = images + len(halves)
-    plan = [(0, 0), (1, 0), (1, 0), (2, 0), (3, 0), (4, 1)] if calls == 6 else [(min(at, 3), 0) for at in range(calls)]
-    large = [functools.partial(scatter_stage, group=group, devices=devices) for group in steps]
-    large += [functools.partial(gather_stage, group=group, devices=devices) for group in reversed(steps)]
-    little = [functools.partial(scatter_stage, group=group, devices=devices) for group in steps]
-    large_at = little_at = 0
-    rest = before = None
-    gqkv_parts = []
-
-    def advance(call):
-        nonlocal large_at, little_at, big, rest, mod
-        while large_at < plan[call][0]:
-            big = large[large_at](big)
-            large_at += 1
-        while little_at < plan[call][1]:
-            rest = little[little_at](rest)
-            little_at += 1
-        if large_at:
-            mod, big, rest = lax.optimization_barrier((mod, big, rest))
-
-    for group in halves:
-        gqkv = None
-        for image in range(group[0], sum(group)):
-            advance(image)
-            gqkv, before, *final = attention_back_call(
-                rank,
-                devices,
-                image,
-                image == images - 1,
-                group,
-                mod,
-                gmid,
-                co,
-                qkv,
-                mix,
-                stat,
-                proj_weight,
-                small,
-                before,
-                gqkv,
-            )
-        gqkv_parts.append(gqkv)
-    rest = final[0]
-    outs, mods, convs = [], [], []
-    made = ()
-    for at, ((first, count), gqkv) in enumerate(zip(halves, gqkv_parts)):
-        advance(images + at)
-        if at:
-            mod, big, rest, made = lax.optimization_barrier((mod, big, rest, made))
-            outs.append(sent_strips(made))
+    split = max(images // 2, 1)
+    groups = [(0, split)] + ([(split, images - split)] if images > split else [])
+    later = [(image, 1) for image in range(split, images)]
+    gqkvs = []
+    before = None
+
+    def attention_back(group):
+        nonlocal before
+        gqkv, before, *final = attention_back_call(
+            rank, devices, group, mod, gmid, co, qkv, mix, stat, proj_weight, small, before
+        )
+        gqkvs.append(gqkv)
+        return final
+
+    def conv_attn_back(group, skip):
         *made, gmod_one, d_ca = conv_attn_back_call(
-            rank, strips, first, xp, mod, gmid, gqkv, (qkv_weight, conv_a), perm_back, moves
+            rank, strips, group[0], skip, group[1], xp, mod, gmid, gqkvs[-1], (qkv_weight, conv_a), perm_back, moves
         )
         mods.append(gmod_one)
         convs.append(d_ca)
-    arrived = outs
-    while large_at < len(large) or little_at < len(little):
-        if large_at < len(large):
-            big = large[large_at](big)
-            large_at += 1
-        if little_at < len(little):
-            rest = little[little_at](rest)
-            little_at += 1
-        if made is not None:
-            big, rest, made = lax.optimization_barrier((big, rest, made))
-            sent, made = sent_strips(made), None
-        else:
-            big, rest, arrived = lax.optimization_barrier((big, rest, arrived))
-    outs = [*arrived, sent]
+        return made
+
+    mods, convs = [], []
+    big = scatter_stage(big, steps[0], devices)
+    mod, big = lax.optimization_barrier((mod, big))
+    final = attention_back(groups[0])
+    for group in steps[1:-1]:
+        big = scatter_stage(big, group, devices)
+    mod, big, gqkvs = lax.optimization_barrier((mod, big, gqkvs))
+    made = conv_attn_back(groups[0], 0)
+    big = scatter_stage(big, steps[-1], devices)
+    mod, big, made = lax.optimization_barrier((mod, big, made))
+    gathered = lax.all_gather(big, AXES, axis=0, tiled=True)
+    outs = [sent_strips(made)]
+    for group in groups[1:]:
+        final = attention_back(group)
+    rest, outs = lax.optimization_barrier((final[0], outs))
+    stage = 0
+    for at, group in enumerate(later):
+        made = conv_attn_back(group, at)
+        if stage < len(steps) - 1:
+            rest = scatter_stage(rest, steps[stage], devices)
+            stage += 1
+        mod, rest, made, outs = lax.optimization_barrier((mod, rest, made, outs))
+        outs.append(sent_strips(made))
+    for group in steps[stage:]:
+        rest = scatter_stage(rest, group, devices)
+    halves = [groups[0], *later]
     grad_mod = jnp.concatenate([jnp.concatenate(mods, axis=0)[:, :2], gmod_two[:, :4]], axis=1)
+    grad_mod = grad_mod.transpose(1, 0, 2).reshape(6 * images, width)
+    per_tile = 8 // images
     late = jnp.concatenate(
         [
             sum(convs),
-            grad_mod.reshape(images * 6, width),
-            jnp.pad(cond.astype(F32), ((0, 0), (0, width - cond.shape[1]))),
+            jnp.pad(grad_mod, ((0, -grad_mod.shape[0] % 8), (0, 0))),
+            jnp.pad(
+                jnp.concatenate([cond.astype(F32)] * per_tile, axis=0), ((0, 0), (0, width - cond.shape[1]))
+            ),
         ],
         axis=0,
-    )
-    late = jnp.pad(late, ((0, -late.shape[0] % 16), (0, 0))).astype(BF)
+    ).astype(BF)
     share = rest.shape[0]
     rest = jnp.concatenate([rest, late], axis=0)
-    finished = None
-    for at, group in enumerate(reversed(steps)):
+    grad_latents = None
+    for at, group in enumerate(steps[:0:-1]):
         rest = gather_stage(rest, group, devices)
         if at == 0:
-            rest, outs = lax.optimization_barrier((rest, outs))
-        if at == 1:
-            finished = finish_big_call(rank, big.reshape(devices, -1, width), hidden, width)
-            rest, finished = lax.optimization_barrier((rest, finished))
+            rest, outs, gathered = lax.optimization_barrier((rest, outs, gathered))
+        if at == len(steps) - 2:
+            finished = finish_big_call(gathered, devices, order, hidden, width)
+            for (first, count), pieces in zip(halves[:2], outs):
+                grad_latents = finish_latents_call(rank, images, first, pieces, grad_latents)
+            rest, grad_latents, finished = lax.optimization_barrier((rest, grad_latents, finished))
     grad_fc1, grad_fc2, grad_down = finished
-    grad_latents = None
-    for (first, count), pieces in zip(halves, outs):
+    for (first, count), pieces in zip(halves[2:], outs[2:]):
         grad_latents = finish_latents_call(rank, images, first, pieces, grad_latents)
-    rest = rest.reshape(devices, -1, width)
-    rest, grad_latents = lax.optimization_barrier((rest, grad_latents))
-    grad_qkv, grad_proj, small = finish_rest_call(rank, rest, share, width)
-    late = rest[:, share:]
-    grad_conv_attn = jnp.sum(late[:, :9].astype(F32), axis=0)
-    all_mod = late[:, 16 : 16 + 6 * images].reshape(devices * images, 6 * width)
-    all_cond = late[:, 16 + 6 * images : 16 + 7 * images, : cond.shape[1]]
-    all_cond = all_cond.reshape(devices * images, cond.shape[1])
-    grad_ada = lax.dot_general(all_cond, all_mod, (TN, ((), ())), preferred_element_type=F32)
-    grad_ada_bias = jnp.sum(all_mod.astype(F32), axis=0)
+    rest = rest.reshape(devices // 2, -1, width)
+    other = exchange(rest, steps[0][0], devices)
+    other, grad_latents = lax.optimization_barrier((other, grad_latents))
+    (
+        grad_qkv,
+        grad_proj,
+        grad_conv_ffn,
+        grad_fc1b,
+        grad_fc2b,
+        grad_downb,
+        grad_conv_attn,
+        grad_ada,
+        grad_ada_bias,
+    ) = finish_rest_call(rank, rest, other, share, width, images, cond.shape[1])
     return (
         res.reshape(out_grad.shape),
         grad_latents.reshape(latents.shape),
         grad_ada,
         grad_ada_bias,
-        grad_conv_attn.reshape(conv_attn.shape),
+        grad_conv_attn,
         grad_qkv,
         grad_proj,
         grad_fc1,
-        small[9],
-        small[:9].reshape(conv_ffn.shape),
+        grad_fc1b,
+        grad_conv_ffn,
         grad_fc2,
-        small[10, :width],
+        grad_fc2b,
         grad_down,
-        small[10, width : 3 * width],
+        grad_downb,
     )
 
 

time: 422 us -> 383 us (0.908)
  waiting for transfers between devices: 52.4 us -> 25.4 us
  between operations: 1.8 us -> 14.9 us
  other arithmetic: 25.5 us -> 17.6 us
  local copies, waits for them, and re-layouts: 26.3 us -> 19.2 us
  starting transfers between devices: 46.1 us -> 40.3 us
    ppermute x18 -> x21, waiting for transfers between devices: 20.2 us -> 5.26 us  [swap_strips(): return lax.ppermute(values, 'narrow', [(i, i ^ mask) for i in range(count)])]
    ppermute x28 -> x21, waiting for transfers between devices: 32.2 us -> 20.1 us  [exchange(): return lax.ppermute(values, AXES, [(i, i ^ mask) for i in range(devices)])]
    concatenate x5 -> x1, other arithmetic: 12.6 us -> 2.3 us  [gather_stage(): jnp.concatenate([values] + [exchange(values, mask, devices) for mask in m...]
    pallas_call x4 -> x2, Pallas kernels: 58.8 us -> 50.3 us  [attention_back_call(): pl.pallas_call(functools.partial(attention_back_kernel, parts=parts, begi...]
    ppermute x28 -> x21, starting transfers between devices: 32.3 us -> 25.3 us  [exchange(): return lax.ppermute(values, AXES, [(i, i ^ mask) for i in range(devices)])]
    pallas_call x2 -> x3, Pallas kernels: 7.32 us -> 9.92 us  [finish_latents_call(): pl.pallas_call(functools.partial(finish_latents_kernel, strips), grid_spe...]
    pallas_call x2 -> x3, Pallas kernels: 30.8 us -> 33.4 us  [conv_attn_back_call(): pl.pallas_call(functools.partial(conv_attn_back_kernel, strips), grid_spe...]
    convert_element_type x6 -> x5, other arithmetic: 8.82 us -> 7.08 us  [scatter_stage(): return total.astype(BF)]
  transfers between devices with their start and end apart: 46 -> 43, of which waited for: 13 -> 12; matrix products, arithmetic and copies ran while one was open for 4% -> 5% of each run, Pallas kernels for 33% -> 35%
where the time goes in v1:
time: 383 us; the launch traced here: 379 us
  Pallas kernels  261 us (68%)
  starting transfers between devices  40.3 us (11%)
  waiting for transfers between devices  25.4 us (7%)
  local copies, waits for them, and re-layouts  19.2 us (5%)
  other arithmetic  17.6 us (5%)
  between operations  14.9 us (4%)
    pallas_call x1, Pallas kernels, feed_forward_call(): pl.pallas_call(functools.partial(feed_forward_kernel, parts=parts), grid_...  111 us
    pallas_call x2, Pallas kernels, attention_back_call(): pl.pallas_call(functools.partial(attention_back_kernel, parts=parts, begi...  50.3 us
    pallas_call x4, Pallas kernels, attention_forward_call(): pl.pallas_call(functools.partial(attention_forward_kernel, strips, begin)...  42.1 us
    pallas_call x3, Pallas kernels, conv_attn_back_call(): pl.pallas_call(functools.partial(conv_attn_back_kernel, strips), grid_spe...  33.4 us
    ppermute x21, starting transfers between devices, exchange(): return lax.ppermute(values, AXES, [(i, i ^ mask) for i in range(devices)])  25.3 us
    ppermute x21, waiting for transfers between devices, exchange(): return lax.ppermute(values, AXES, [(i, i ^ mask) for i in range(devices)])  20.1 us
    ppermute x21, starting transfers between devices, swap_strips(): return lax.ppermute(values, 'narrow', [(i, i ^ mask) for i in range(count)])  15 us
    pallas_call x3, Pallas kernels, finish_latents_call(): pl.pallas_call(functools.partial(finish_latents_kernel, strips), grid_spe...  9.92 us
  transfers between devices with their start and end apart: 43, of which 12 were waited for; matrix products, arithmetic and copies ran while one was open for 5% of the time, Pallas kernels for 35%

profile of v1, /device:TPU:0, one launch (start us, length us, event | category | flops | bytes accessed | tf_op | source)
XLA Modules:
  0.0 378.9 jit_solution(9065705662097544811)
XLA Ops:
  7.3 3.4 dynamic-slice_bitcast_fusion
  11.2 2.6 collective-permute-start.1
  21.2 2.1 collective-permute-done.2.refs_3_
  23.4 1.7 collective-permute-start.4
  25.1 10.6 %attention_forward.4 = (bf16[4,1024,384]{2,1,0:T(8,128)(2,1)}, bf16[4,1024,384]{2,1,0:T(8,128)(2,1)}, bf16[4,1024,1152]{2,1,0:T(8,128)(2,1)}, bf16[4,1024,384]{2,1,0:T(8,128)(2,1)}, f32[4,4,8,256]{3,2,1,0:T(8,128)}) custom-call(s32[2]{0:T(128)} %pad_add_fusion.rank_ref, bf16[256,384]{1,0:T(8,128)(2,1)} %get-tuple-element.177.refs_0_, ...), custom_call_target="tpu_custom_call" | custom-call | flops 5000000000 | bytes 8000000 | tf_op jit(solution)/shard_map/attention_forward/pallas_call | solution.py:790
  37.0 1.7 collective-permute-start.7
  38.7 10.5 %attention_forward.5 = (bf16[4,1024,384]{2,1,0:T(8,128)(2,1)}, bf16[4,1024,384]{2,1,0:T(8,128)(2,1)}, bf16[4,1024,1152]{2,1,0:T(8,128)(2,1)}, bf16[4,1024,384]{2,1,0:T(8,128)(2,1)}, f32[4,4,8,256]{3,2,1,0:T(8,128)}) custom-call(s32[2]{0:T(128)} %pad_add_fusion.rank_ref, ...), custom_call_target="tpu_custom_call", output_to_operand_aliasing={{0}: (10, {}), {1}: (11, {}), {2}: (12, {}), {3}: (13, {}),... | custom-call | flops 5000000000 | bytes 8000000 | tf_op jit(solution)/shard_map/attention_forward/pallas_call | solution.py:790
  49.7 1.7 collective-permute-start.10
  51.4 10.5 %attention_forward.6 = (bf16[4,1024,384]{2,1,0:T(8,128)(2,1)}, bf16[4,1024,384]{2,1,0:T(8,128)(2,1)}, bf16[4,1024,1152]{2,1,0:T(8,128)(2,1)}, bf16[4,1024,384]{2,1,0:T(8,128)(2,1)}, f32[4,4,8,256]{3,2,1,0:T(8,128)}) custom-call(s32[2]{0:T(128)} %pad_add_fusion.rank_ref, ...), custom_call_target="tpu_custom_call", output_to_operand_aliasing={{0}: (10, {}), {1}: (11, {}), {2}: (12, {}), {3}: (13, {}),... | custom-call | flops 5000000000 | bytes 8000000 | tf_op jit(solution)/shard_map/attention_forward/pallas_call | solution.py:790
  62.7 10.4 %attention_forward.7 = (bf16[4,1024,384]{2,1,0:T(8,128)(2,1)}, bf16[4,1024,384]{2,1,0:T(8,128)(2,1)}, bf16[4,1024,1152]{2,1,0:T(8,128)(2,1)}, bf16[4,1024,384]{2,1,0:T(8,128)(2,1)}, f32[4,4,8,256]{3,2,1,0:T(8,128)}) custom-call(s32[2]{0:T(128)} %pad_add_fusion.rank_ref, ...), custom_call_target="tpu_custom_call", output_to_operand_aliasing={{0}: (10, {}), {1}: (11, {}), {2}: (12, {}), {3}: (13, {}),... | custom-call | flops 5000000000 | bytes 8000000 | tf_op jit(solution)/shard_map/attention_forward/pallas_call | solution.py:790
  73.2 111.4 %feed_forward.1 = (bf16[4,256,768]{2,1,0:T(8,128)(2,1)}, f32[4,1024,384]{2,1,0:T(8,128)}, f32[4,8,384]{2,1,0:T(8,128)}, bf16[6144,384]{1,0:T(8,128)(2,1)}, f32[16,1536]{1,0:T(8,128)}) custom-call(s32[2]{0:T(128)} %pad_add_fusion.rank_ref, bf16[4,1024,384]{2,1,0:T(8,128)(2,1)} %get-tuple-element.196.xp_ref, bf16[4,1024,384]{2,1,0:T(8,128)(2,1)} %get-tuple-element.197.mix_ref, ...), custom_call_target="tpu_custom_call" | custom-call | flops 56000000000 | bytes 80000000 | tf_op jit(solution)/shard_map/feed_forward/pallas_call | solution.py:842
  184.6 2.1 slice.69
  187.1 4.2 %collective-permute-done.12 = bf16[3072,384]{1,0:T(8,128)(2,1)S(1)} collective-permute-done((bf16[3072,384]{1,0:T(8,128)(2,1)S(1)}, bf16[3072,384]{1,0:T(8,128)(2,1)S(1)}, u32[]{:S(2)}, u32[]{:S(2)}) %collective-permute-start.12) | collective-permute-done | bytes 2359328 | tf_op jit(solution)/shard_map/ppermute | solution.py:1022
  191.9 1.4 copy-done
  194.5 2.7 collective-permute-start.15
  198.0 24.0 %attention_back.2 = (bf16[2,1024,1152]{2,1,0:T(8,128)(2,1)}, f32[384,1536]{1,0:T(8,128)}) custom-call(s32[2]{0:T(128)} %pad_add_fusion.rank_ref, f32[4,8,384]{2,1,0:T(8,128)} %pad.19.refs_4_.mod_ref, f32[4,1024,384]{2,1,0:T(8,128)} %get-tuple-element.202.gmid_ref, bf16[4,1024,384]{2,1,0:T(8,128)(2,1)} %get-tuple-element.203.co_ref, ...), custom_call_target="tpu_custom_call" | custom-call | flops 16000000000 | bytes 20000000 | tf_op jit(solution)/shard_map/attention_back/pallas_call | solution.py:877
  222.1 2.0 collective-permute-done.14
  224.2 1.9 add_convert_fusion.2
  226.8 3.5 collective-permute-start.18
  231.2 15.3 %conv_attn_back.3 = (bf16[2,256,384]{2,1,0:T(8,128)(2,1)}, bf16[2,256,384]{2,1,0:T(8,128)(2,1)}, bf16[2,256,384]{2,1,0:T(8,128)(2,1)}, bf16[2,256,384]{2,1,0:T(8...) custom-call(s32[2]{0:T(128)} %pad_add_fusion.rank_ref, bf16[4,1024,384]{2,1,0:T(8,128)(2,1)} %get-tuple-element.196.xp_ref, ...), custom_call_target="tpu_custom_call" | custom-call | flops 8000000000 | bytes 16000000 | tf_op jit(solution)/shard_map/conv_attn_back/pallas_call | solution.py:911
  246.5 1.8 add_convert_fusion.5
  248.4 1.6 collective-permute-start.20
  250.3 26.2 %attention_back.3 = (bf16[2,1024,1152]{2,1,0:T(8,128)(2,1)}, f32[384,1536]{1,0:T(8,128)}, bf16[2048,384]{1,0:T(8,128)(2,1)}) custom-call(s32[2]{0:T(128)} %pad_add_fusion.rank_ref, f32[4,8,384]{2,1,0:T(8,128)} %pad.19.refs_4_.mod_ref, f32[4,1024,384]{2,1,0:T(8,128)} %get-tuple-element.202.gmid_ref, bf16[4,1024,384]{2,1,0:T(8,128)(2,1)} %get-tuple-element.203.co_ref, ...), custom_call_target="tpu_custom_call" | custom-call | flops 16000000000 | bytes 20000000 | tf_op jit(solution)/shard_map/attention_back/pallas_call | solution.py:877
  279.1 1.4 slice.98
  281.1 9.1 %conv_attn_back.4 = (bf16[1,256,384]{2,1,0:T(8,128)(2,1)}, bf16[1,256,384]{2,1,0:T(8,128)(2,1)}, bf16[1,256,384]{2,1,0:T(8,128)(2,1)}, bf16[1,256,384]{2,1,0:T(8...) custom-call(s32[2]{0:T(128)} %pad_add_fusion.rank_ref, bf16[4,1024,384]{2,1,0:T(8,128)(2,1)} %get-tuple-element.196.xp_ref, ...), custom_call_target="tpu_custom_call" | custom-call | flops 4000000000 | bytes 8000000 | tf_op jit(solution)/shard_map/conv_attn_back/pallas_call | solution.py:911
  290.2 1.3 convert.34
  291.5 1.6 add_convert_fusion.1
  293.9 1.5 collective-permute-start.25
  295.4 1.5 collective-permute-start.24
  297.4 1.5 collective-permute-start.27
  298.9 9.0 %conv_attn_back.5 = (bf16[1,256,384]{2,1,0:T(8,128)(2,1)}, bf16[1,256,384]{2,1,0:T(8,128)(2,1)}, bf16[1,256,384]{2,1,0:T(8,128)(2,1)}, bf16[1,256,384]{2,1,0:T(8...) custom-call(s32[2]{0:T(128)} %pad_add_fusion.rank_ref, bf16[4,1024,384]{2,1,0:T(8,128)(2,1)} %get-tuple-element.196.xp_ref, ...), custom_call_target="tpu_custom_call" | custom-call | flops 4000000000 | bytes 8000000 | tf_op jit(solution)/shard_map/conv_attn_back/pallas_call | solution.py:911
  309.0 2.3 collective-permute-done.24
  312.5 3.2 collective-permute-done.28.refs_3_
  315.7 2.6 collective-permute-start.31
  318.7 1.4 collective-permute-start.29
  320.9 2.2 collective-permute-done.31
  326.0 1.6 collective-permute-start.32
  328.1 1.3 collective-permute-start.37
  330.5 2.5 collective-permute-start.34
  333.1 6.2 %collective-permute-done.33 = bf16[112,384]{1,0:T(8,128)(2,1)S(1)} collective-permute-done((bf16[112,384]{1,0:T(8,128)(2,1)S(1)}, bf16[112,384]{1,0:T(8,128)(2,1)S(1)}, u32[]{:S(2)}, u32[]{:S(2)}) %collective-permute-start.33) | collective-permute-done | bytes 86048 | tf_op jit(solution)/shard_map/ppermute | solution.py:1022
  339.3 1.4 collective-permute-done.34
  342.9 2.2 collective-permute-start.38
  345.1 8.5 %finish_big.1 = (f32[384,1536]{1,0:T(8,128)}, f32[1536,384]{1,0:T(8,128)}, f32[1536,768]{1,0:T(8,128)}) custom-call(bf16[6144,384]{1,0:T(8,128)(2,1)} %all-gather.2.cloned.1.call-done.refs_0_.refs_1_.refs_2_.refs_3_, bf16[6144,384]{1,0:T(8,128)(2,1)} %all-gather.2.cloned.1.call-done.refs_0_.refs_1_.refs_2_.refs_3_, ...), custom_call_target="tpu_custom_call" | custom-call | bytes 15000000 | tf_op jit(solution)/shard_map/finish_big/pallas_call | solution.py:957
  353.7 3.7 finish_latents.3.refs_4_
  357.3 3.1 finish_latents.4.refs_4_
  360.5 2.3 pad_maximum_fusion
  362.8 3.1 finish_latents.5
  366.2 5.6 %finish_rest.1 = (f32[384,1152]{1,0:T(8,128)}, f32[384,384]{1,0:T(8,128)}, f32[3,3,1536]{2,1,0:T(4,128)}, f32[1536]{0:T(1024)}, f32[384]{0:T(512)}, /*index=5*/f...) custom-call(s32[2]{0:T(128)} %pad_add_fusion.rank_ref, bf16[16,112,384]{2,1,0:T(8,128)(2,1)} %bitcast.22.own_ref, ...), custom_call_target="tpu_custom_call" | custom-call | bytes 8000000 | tf_op jit(solution)/shard_map/finish_rest/pallas_call | solution.py:993
  (161 shorter events, 30.6 us)
Async XLA Ops:
  7.2 334.5 %all-gather.2.cloned.1.call-start = ((), (), s32[]{:S(2)}) async-start(), calls=%async_computation | async-start | bytes 4866048 | tf_op jit(solution)/shard_map/all_gather | solution.py:1169
  7.3 9.0 %copy-start.23 = (bf16[384]{0:T(512)(128)(2,1)S(1)}, bf16[384]{0:T(512)(128)(2,1)}, u32[]{:S(2)}) copy-start(bf16[384]{0:T(512)(128)(2,1)} %param.27) | copy-start | bytes 2308
  7.3 9.6 %copy-start.22 = (bf16[768]{0:T(1024)(128)(2,1)S(1)}, bf16[768]{0:T(1024)(128)(2,1)}, u32[]{:S(2)}) copy-start(bf16[768]{0:T(1024)(128)(2,1)} %param.29) | copy-start | bytes 4612
  7.3 10.1 %copy-start.16 = (bf16[3,3,1536]{2,1,0:T(4,128)(2,1)S(1)}, bf16[3,3,1536]{2,1,0:T(4,128)(2,1)}, u32[]{:S(2)}) copy-start(bf16[3,3,1536]{2,1,0:T(4,128)(2,1)} %param.25) | copy-start | bytes 82948
  10.7 10.5 %collective-permute-start = (bf16[256,384]{1,0:T(8,128)(2,1)S(1)}, bf16[256,384]{1,0:T(8,128)(2,1)S(1)}, u32[]{:S(2)}, u32[]{:S(2)}) collective-permute-start(bf16[256,384]{1,0:T(8,128)(2,1)S(1)} %get-tuple-element.318), channel_id=1, source_target_pairs={{0,1},{1,0},{2,3},{3,2},{4,5},{5,4},{6,7},{7,6},{8,9},{9,8},{10,11... | collective-permute-start | bytes 589832 | tf_op jit(solution)/shard_map/ppermute | solution.py:1027
  11.2 10.0 %collective-permute-start.1 = (bf16[256,384]{1,0:T(8,128)(2,1)S(1)}, bf16[256,384]{1,0:T(8,128)(2,1)S(1)}, u32[]{:S(2)}, u32[]{:S(2)}) collective-permute-start(bf16[256,384]{1,0:T(8,128)(2,1)S(1)} %get-tuple-element.317), channel_id=1, source_target_pairs={{0,2},{1,3},{2,0},{3,1},{4,6},{5,7},{6,4},{7,5},{8,10},{9,11},{10,... | collective-permute-start | bytes 589832 | tf_op jit(solution)/shard_map/ppermute | solution.py:1027
  13.8 9.4 %collective-permute-start.2 = (bf16[256,384]{1,0:T(8,128)(2,1)S(1)}, bf16[256,384]{1,0:T(8,128)(2,1)S(1)}, u32[]{:S(2)}, u32[]{:S(2)}) collective-permute-start(bf16[256,384]{1,0:T(8,128)(2,1)S(1)} %get-tuple-element.316), channel_id=1, source_target_pairs={{0,3},{1,2},{2,1},{3,0},{4,7},{5,6},{6,5},{7,4},{8,11},{9,10},{10,... | collective-permute-start | bytes 589832 | tf_op jit(solution)/shard_map/ppermute | solution.py:1027
  23.2 12.5 %collective-permute-start.3 = (bf16[256,384]{1,0:T(8,128)(2,1)}, bf16[256,384]{1,0:T(8,128)(2,1)S(1)}, u32[]{:S(2)}, u32[]{:S(2)}) collective-permute-start(bf16[256,384]{1,0:T(8,128)(2,1)} %get-tuple-element.158), channel_id=1, source_target_pairs={{0,1},{1,0},{2,3},{3,2},{4,5},{5,4},{6,7},{7,6},{8,9},{9,8},{10,11... | collective-permute-start | bytes 589832 | tf_op jit(solution)/shard_map/ppermute | solution.py:1027
  23.4 12.4 %collective-permute-start.4 = (bf16[256,384]{1,0:T(8,128)(2,1)S(1)}, bf16[256,384]{1,0:T(8,128)(2,1)S(1)}, u32[]{:S(2)}, u32[]{:S(2)}) collective-permute-start(bf16[256,384]{1,0:T(8,128)(2,1)S(1)} %get-tuple-element.159), channel_id=1, source_target_pairs={{0,2},{1,3},{2,0},{3,1},{4,6},{5,7},{6,4},{7,5},{8,10},{9,11},{10,... | collective-permute-start | bytes 589832 | tf_op jit(solution)/shard_map/ppermute | solution.py:1027
  25.1 10.7 %collective-permute-start.5 = (bf16[256,384]{1,0:T(8,128)(2,1)S(1)}, bf16[256,384]{1,0:T(8,128)(2,1)S(1)}, u32[]{:S(2)}, u32[]{:S(2)}) collective-permute-start(bf16[256,384]{1,0:T(8,128)(2,1)S(1)} %get-tuple-element.160), channel_id=1, source_target_pairs={{0,3},{1,2},{2,1},{3,0},{4,7},{5,6},{6,5},{7,4},{8,11},{9,10},{10,... | collective-permute-start | bytes 589832 | tf_op jit(solution)/shard_map/ppermute | solution.py:1027
  36.6 12.6 %collective-permute-start.6 = (bf16[256,384]{1,0:T(8,128)(2,1)}, bf16[256,384]{1,0:T(8,128)(2,1)S(1)}, u32[]{:S(2)}, u32[]{:S(2)}) collective-permute-start(bf16[256,384]{1,0:T(8,128)(2,1)} %get-tuple-element.162), channel_id=1, source_target_pairs={{0,1},{1,0},{2,3},{3,2},{4,5},{5,4},{6,7},{7,6},{8,9},{9,8},{10,11... | collective-permute-start | bytes 589832 | tf_op jit(solution)/shard_map/ppermute | solution.py:1027
  37.0 12.2 %collective-permute-start.7 = (bf16[256,384]{1,0:T(8,128)(2,1)}, bf16[256,384]{1,0:T(8,128)(2,1)S(1)}, u32[]{:S(2)}, u32[]{:S(2)}) collective-permute-start(bf16[256,384]{1,0:T(8,128)(2,1)} %get-tuple-element.163), channel_id=1, source_target_pairs={{0,2},{1,3},{2,0},{3,1},{4,6},{5,7},{6,4},{7,5},{8,10},{9,11},{10,... | collective-permute-start | bytes 589832 | tf_op jit(solution)/shard_map/ppermute | solution.py:1027
  38.7 10.5 %collective-permute-start.8 = (bf16[256,384]{1,0:T(8,128)(2,1)}, bf16[256,384]{1,0:T(8,128)(2,1)S(1)}, u32[]{:S(2)}, u32[]{:S(2)}) collective-permute-start(bf16[256,384]{1,0:T(8,128)(2,1)} %get-tuple-element.164), channel_id=1, source_target_pairs={{0,3},{1,2},{2,1},{3,0},{4,7},{5,6},{6,5},{7,4},{8,11},{9,10},{10,... | collective-permute-start | bytes 589832 | tf_op jit(solution)/shard_map/ppermute | solution.py:1027
  49.2 12.8 %collective-permute-start.9 = (bf16[256,384]{1,0:T(8,128)(2,1)}, bf16[256,384]{1,0:T(8,128)(2,1)S(1)}, u32[]{:S(2)}, u32[]{:S(2)}) collective-permute-start(bf16[256,384]{1,0:T(8,128)(2,1)} %get-tuple-element.166), channel_id=1, source_target_pairs={{0,1},{1,0},{2,3},{3,2},{4,5},{5,4},{6,7},{7,6},{8,9},{9,8},{10,11... | collective-permute-start | bytes 589832 | tf_op jit(solution)/shard_map/ppermute | solution.py:1027
  49.7 12.3 %collective-permute-start.10 = (bf16[256,384]{1,0:T(8,128)(2,1)}, bf16[256,384]{1,0:T(8,128)(2,1)S(1)}, u32[]{:S(2)}, u32[]{:S(2)}) collective-permute-start(bf16[256,384]{1,0:T(8,128)(2,1)} %get-tuple-element.167), channel_id=1, source_target_pairs={{0,2},{1,3},{2,0},{3,1},{4,6},{5,7},{6,4},{7,5},{8,10},{9,11},{10,... | collective-permute-start | bytes 589832 | tf_op jit(solution)/shard_map/ppermute | solution.py:1027
  51.4 10.6 %collective-permute-start.11 = (bf16[256,384]{1,0:T(8,128)(2,1)}, bf16[256,384]{1,0:T(8,128)(2,1)}, u32[]{:S(2)}, u32[]{:S(2)}) collective-permute-start(bf16[256,384]{1,0:T(8,128)(2,1)} %get-tuple-element.168), channel_id=1, source_target_pairs={{0,3},{1,2},{2,1},{3,0},{4,7},{5,6},{6,5},{7,4},{8,11},{9,10},{10,... | collective-permute-start | bytes 589832 | tf_op jit(solution)/shard_map/ppermute | solution.py:1027
  186.7 4.6 %collective-permute-start.12 = (bf16[3072,384]{1,0:T(8,128)(2,1)S(1)}, bf16[3072,384]{1,0:T(8,128)(2,1)S(1)}, u32[]{:S(2)}, u32[]{:S(2)}) collective-permute-start(bf16[3072,384]{1,0:T(8,128)(2,1)S(1)} %slice.69), channel_id=1, source_target_pairs={{0,1},{1,0},{2,3},{3,2},{4,5},{5,4},{6,7},{7,6},{8,9},{9,8},{10,11... | collective-permute-start | bytes 7077896 | tf_op jit(solution)/shard_map/ppermute | solution.py:1022
  194.5 27.5 %collective-permute-start.15 = (bf16[768,384]{1,0:T(8,128)(2,1)}, bf16[768,384]{1,0:T(8,128)(2,1)}, u32[]{:S(2)}, u32[]{:S(2)}) collective-permute-start(bf16[768,384]{1,0:T(8,128)(2,1)} %get-tuple-element.321), channel_id=1, source_target_pairs={{0,12},{1,13},{2,14},{3,15},{4,8},{5,9},{6,10},{7,11},{8,4},{9,5},... | collective-permute-start | bytes 1769480 | tf_op jit(solution)/shard_map/ppermute | solution.py:1022
  197.2 26.8 %collective-permute-start.14 = (bf16[768,384]{1,0:T(8,128)(2,1)}, bf16[768,384]{1,0:T(8,128)(2,1)}, u32[]{:S(2)}, u32[]{:S(2)}) collective-permute-start(bf16[768,384]{1,0:T(8,128)(2,1)} %get-tuple-element.322), channel_id=1, source_target_pairs={{0,4},{1,5},{2,6},{3,7},{4,0},{5,1},{6,2},{7,3},{8,12},{9,13},{10,... | collective-permute-start | bytes 1769480 | tf_op jit(solution)/shard_map/ppermute | solution.py:1022
  197.8 26.5 %collective-permute-start.13 = (bf16[768,384]{1,0:T(8,128)(2,1)S(1)}, bf16[768,384]{1,0:T(8,128)(2,1)}, u32[]{:S(2)}, u32[]{:S(2)}) collective-permute-start(bf16[768,384]{1,0:T(8,128)(2,1)S(1)} %get-tuple-element.320), channel_id=1, source_target_pairs={{0,8},{1,9},{2,10},{3,11},{4,12},{5,13},{6,14},{7,15},{8,0},{9,1},... | collective-permute-start | bytes 1769480 | tf_op jit(solution)/shard_map/ppermute | solution.py:1022
  226.8 19.7 %collective-permute-start.18 = (bf16[192,384]{1,0:T(8,128)(2,1)}, bf16[192,384]{1,0:T(8,128)(2,1)}, u32[]{:S(2)}, u32[]{:S(2)}) collective-permute-start(bf16[192,384]{1,0:T(8,128)(2,1)} %get-tuple-element.327), channel_id=1, source_target_pairs={{0,18},{1,19},{2,16},{3,17},{4,22},{5,23},{6,20},{7,21},{8,26},{9,... | collective-permute-start | bytes 442376 | tf_op jit(solution)/shard_map/ppermute | solution.py:1022
  230.4 16.1 %collective-permute-start.17 = (bf16[192,384]{1,0:T(8,128)(2,1)S(1)}, bf16[192,384]{1,0:T(8,128)(2,1)}, u32[]{:S(2)}, u32[]{:S(2)}) collective-permute-start(bf16[192,384]{1,0:T(8,128)(2,1)S(1)} %get-tuple-element.328), channel_id=1, source_target_pairs={{0,16},{1,17},{2,18},{3,19},{4,20},{5,21},{6,22},{7,23},{8,24},{9,... | collective-permute-start | bytes 442376 | tf_op jit(solution)/shard_map/ppermute | solution.py:1022
  230.7 15.8 %collective-permute-start.16 = (bf16[192,384]{1,0:T(8,128)(2,1)S(1)}, bf16[192,384]{1,0:T(8,128)(2,1)}, u32[]{:S(2)}, u32[]{:S(2)}) collective-permute-start(bf16[192,384]{1,0:T(8,128)(2,1)S(1)} %get-tuple-element.326), channel_id=1, source_target_pairs={{0,2},{1,3},{2,0},{3,1},{4,6},{5,7},{6,4},{7,5},{8,10},{9,11},{10,... | collective-permute-start | bytes 442376 | tf_op jit(solution)/shard_map/ppermute | solution.py:1022
  248.3 28.2 %collective-permute-start.19 = (bf16[2,256,384]{2,1,0:T(8,128)(2,1)}, bf16[2,256,384]{2,1,0:T(8,128)(2,1)S(1)}, u32[]{:S(2)}, u32[]{:S(2)}) collective-permute-start(bf16[2,256,384]{2,1,0:T(8,128)(2,1)} %get-tuple-element.219), channel_id=1, source_target_pairs={{0,1},{1,0},{2,3},{3,2},{4,5},{5,4},{6,7},{7,6},{8,9},{9,8},{10,11... | collective-permute-start | bytes 1179656 | tf_op jit(solution)/shard_map/ppermute | solution.py:1027
  248.4 28.1 %collective-permute-start.20 = (bf16[2,256,384]{2,1,0:T(8,128)(2,1)}, bf16[2,256,384]{2,1,0:T(8,128)(2,1)S(1)}, u32[]{:S(2)}, u32[]{:S(2)}) collective-permute-start(bf16[2,256,384]{2,1,0:T(8,128)(2,1)} %get-tuple-element.220), channel_id=1, source_target_pairs={{0,2},{1,3},{2,0},{3,1},{4,6},{5,7},{6,4},{7,5},{8,10},{9,11},{10,... | collective-permute-start | bytes 1179656 | tf_op jit(solution)/shard_map/ppermute | solution.py:1027
  250.0 26.6 %collective-permute-start.21 = (bf16[2,256,384]{2,1,0:T(8,128)(2,1)}, bf16[2,256,384]{2,1,0:T(8,128)(2,1)}, u32[]{:S(2)}, u32[]{:S(2)}) collective-permute-start(bf16[2,256,384]{2,1,0:T(8,128)(2,1)} %get-tuple-element.221), channel_id=1, source_target_pairs={{0,3},{1,2},{2,1},{3,0},{4,7},{5,6},{6,5},{7,4},{8,11},{9,10},{10,... | collective-permute-start | bytes 1179656 | tf_op jit(solution)/shard_map/ppermute | solution.py:1027
  250.3 30.2 %copy-start.17 = (f32[2,8,384]{2,1,0:T(8,128)S(1)}, f32[2,8,384]{2,1,0:T(8,128)}, u32[]{:S(2)}) copy-start(f32[2,8,384]{2,1,0:T(8,128)} %get-tuple-element.250) | copy-start | bytes 73732
  278.7 12.8 %collective-permute-start.22 = (bf16[1024,384]{1,0:T(8,128)(2,1)S(1)}, bf16[1024,384]{1,0:T(8,128)(2,1)}, u32[]{:S(2)}, u32[]{:S(2)}) collective-permute-start(bf16[1024,384]{1,0:T(8,128)(2,1)S(1)} %slice.79), channel_id=1, source_target_pairs={{0,1},{1,0},{2,3},{3,2},{4,5},{5,4},{6,7},{7,6},{8,9},{9,8},{10,11... | collective-permute-start | bytes 2359304 | tf_op jit(solution)/shard_map/ppermute | solution.py:1022
  293.9 14.8 %collective-permute-start.25 = (bf16[256,384]{1,0:T(8,128)(2,1)}, bf16[256,384]{1,0:T(8,128)(2,1)}, u32[]{:S(2)}, u32[]{:S(2)}) collective-permute-start(bf16[256,384]{1,0:T(8,128)(2,1)} %get-tuple-element.324), channel_id=1, source_target_pairs={{0,12},{1,13},{2,14},{3,15},{4,8},{5,9},{6,10},{7,11},{8,4},{9,5},... | collective-permute-start | bytes 589832 | tf_op jit(solution)/shard_map/ppermute | solution.py:1022
  295.4 15.9 %collective-permute-start.24 = (bf16[256,384]{1,0:T(8,128)(2,1)}, bf16[256,384]{1,0:T(8,128)(2,1)}, u32[]{:S(2)}, u32[]{:S(2)}) collective-permute-start(bf16[256,384]{1,0:T(8,128)(2,1)} %get-tuple-element.325), channel_id=1, source_target_pairs={{0,4},{1,5},{2,6},{3,7},{4,0},{5,1},{6,2},{7,3},{8,12},{9,13},{10,... | collective-permute-start | bytes 589832 | tf_op jit(solution)/shard_map/ppermute | solution.py:1022
  296.9 14.4 %collective-permute-start.23 = (bf16[256,384]{1,0:T(8,128)(2,1)S(1)}, bf16[256,384]{1,0:T(8,128)(2,1)}, u32[]{:S(2)}, u32[]{:S(2)}) collective-permute-start(bf16[256,384]{1,0:T(8,128)(2,1)S(1)} %get-tuple-element.323), channel_id=1, source_target_pairs={{0,8},{1,9},{2,10},{3,11},{4,12},{5,13},{6,14},{7,15},{8,0},{9,1},... | collective-permute-start | bytes 589832 | tf_op jit(solution)/shard_map/ppermute | solution.py:1022
  297.4 15.1 %collective-permute-start.26 = (bf16[1,256,384]{2,1,0:T(8,128)(2,1)}, bf16[1,256,384]{2,1,0:T(8,128)(2,1)}, u32[]{:S(2)}, u32[]{:S(2)}) collective-permute-start(bf16[1,256,384]{2,1,0:T(8,128)(2,1)} %get-tuple-element.243), channel_id=1, source_target_pairs={{0,1},{1,0},{2,3},{3,2},{4,5},{5,4},{6,7},{7,6},{8,9},{9,8},{10,11... | collective-permute-start | bytes 589832 | tf_op jit(solution)/shard_map/ppermute | solution.py:1027
  297.4 15.2 %collective-permute-start.27 = (bf16[1,256,384]{2,1,0:T(8,128)(2,1)}, bf16[1,256,384]{2,1,0:T(8,128)(2,1)}, u32[]{:S(2)}, u32[]{:S(2)}) collective-permute-start(bf16[1,256,384]{2,1,0:T(8,128)(2,1)} %get-tuple-element.244), channel_id=1, source_target_pairs={{0,2},{1,3},{2,0},{3,1},{4,6},{5,7},{6,4},{7,5},{8,10},{9,11},{10,... | collective-permute-start | bytes 589832 | tf_op jit(solution)/shard_map/ppermute | solution.py:1027
  308.6 7.0 %collective-permute-start.28 = (bf16[1,256,384]{2,1,0:T(8,128)(2,1)}, bf16[1,256,384]{2,1,0:T(8,128)(2,1)S(1)}, u32[]{:S(2)}, u32[]{:S(2)}) collective-permute-start(bf16[1,256,384]{2,1,0:T(8,128)(2,1)} %get-tuple-element.245), channel_id=1, source_target_pairs={{0,3},{1,2},{2,1},{3,0},{4,7},{5,6},{6,5},{7,4},{8,11},{9,10},{10,... | collective-permute-start | bytes 589832 | tf_op jit(solution)/shard_map/ppermute | solution.py:1027
  315.7 7.4 %collective-permute-start.31 = (bf16[64,384]{1,0:T(8,128)(2,1)S(1)}, bf16[64,384]{1,0:T(8,128)(2,1)S(1)}, u32[]{:S(2)}, u32[]{:S(2)}) collective-permute-start(bf16[64,384]{1,0:T(8,128)(2,1)S(1)} %get-tuple-element.330), channel_id=1, source_target_pairs={{0,18},{1,19},{2,16},{3,17},{4,22},{5,23},{6,20},{7,21},{8,26},{9,... | collective-permute-start | bytes 147464 | tf_op jit(solution)/shard_map/ppermute | solution.py:1022
  318.3 6.0 %collective-permute-start.30 = (bf16[64,384]{1,0:T(8,128)(2,1)S(1)}, bf16[64,384]{1,0:T(8,128)(2,1)S(1)}, u32[]{:S(2)}, u32[]{:S(2)}) collective-permute-start(bf16[64,384]{1,0:T(8,128)(2,1)S(1)} %get-tuple-element.331), channel_id=1, source_target_pairs={{0,16},{1,17},{2,18},{3,19},{4,20},{5,21},{6,22},{7,23},{8,24},{9,... | collective-permute-start | bytes 147464 | tf_op jit(solution)/shard_map/ppermute | solution.py:1022
  318.7 5.6 %collective-permute-start.29 = (bf16[64,384]{1,0:T(8,128)(2,1)S(1)}, bf16[64,384]{1,0:T(8,128)(2,1)S(1)}, u32[]{:S(2)}, u32[]{:S(2)}) collective-permute-start(bf16[64,384]{1,0:T(8,128)(2,1)S(1)} %get-tuple-element.329), channel_id=1, source_target_pairs={{0,2},{1,3},{2,0},{3,1},{4,6},{5,7},{6,4},{7,5},{8,10},{9,11},{10,... | collective-permute-start | bytes 147464 | tf_op jit(solution)/shard_map/ppermute | solution.py:1022
  326.0 4.6 %collective-permute-start.32 = (bf16[112,384]{1,0:T(8,128)(2,1)S(1)}, bf16[112,384]{1,0:T(8,128)(2,1)S(1)}, u32[]{:S(2)}, u32[]{:S(2)}) collective-permute-start(bf16[112,384]{1,0:T(8,128)(2,1)S(1)} %pad_maximum_fusion.1), channel_id=1, source_target_pairs={{0,2},{1,3},{2,0},{3,1},{4,6},{5,7},{6,4},{7,5},{8,10},{9,11},{10,... | collective-permute-start | bytes 258056 | tf_op jit(solution)/shard_map/ppermute | solution.py:1022
  327.6 13.1 %collective-permute-start.35 = (bf16[1,256,384]{2,1,0:T(8,128)(2,1)}, bf16[1,256,384]{2,1,0:T(8,128)(2,1)S(1)}, u32[]{:S(2)}, u32[]{:S(2)}) collective-permute-start(bf16[1,256,384]{2,1,0:T(8,128)(2,1)} %get-tuple-element.263), channel_id=1, source_target_pairs={{0,1},{1,0},{2,3},{3,2},{4,5},{5,4},{6,7},{7,6},{8,9},{9,8},{10,11... | collective-permute-start | bytes 589832 | tf_op jit(solution)/shard_map/ppermute | solution.py:1027
  327.6 13.1 %collective-permute-start.36 = (bf16[1,256,384]{2,1,0:T(8,128)(2,1)}, bf16[1,256,384]{2,1,0:T(8,128)(2,1)S(1)}, u32[]{:S(2)}, u32[]{:S(2)}) collective-permute-start(bf16[1,256,384]{2,1,0:T(8,128)(2,1)} %get-tuple-element.264), channel_id=1, source_target_pairs={{0,2},{1,3},{2,0},{3,1},{4,6},{5,7},{6,4},{7,5},{8,10},{9,11},{10,... | collective-permute-start | bytes 589832 | tf_op jit(solution)/shard_map/ppermute | solution.py:1027
  328.1 12.9 %collective-permute-start.37 = (bf16[1,256,384]{2,1,0:T(8,128)(2,1)}, bf16[1,256,384]{2,1,0:T(8,128)(2,1)}, u32[]{:S(2)}, u32[]{:S(2)}) collective-permute-start(bf16[1,256,384]{2,1,0:T(8,128)(2,1)} %get-tuple-element.265), channel_id=1, source_target_pairs={{0,3},{1,2},{2,1},{3,0},{4,7},{5,6},{6,5},{7,4},{8,11},{9,10},{10,... | collective-permute-start | bytes 589832 | tf_op jit(solution)/shard_map/ppermute | solution.py:1027
  329.4 9.9 %collective-permute-start.33 = (bf16[112,384]{1,0:T(8,128)(2,1)S(1)}, bf16[112,384]{1,0:T(8,128)(2,1)S(1)}, u32[]{:S(2)}, u32[]{:S(2)}) collective-permute-start(bf16[112,384]{1,0:T(8,128)(2,1)S(1)} %pad_maximum_fusion.1), channel_id=1, source_target_pairs={{0,16},{1,17},{2,18},{3,19},{4,20},{5,21},{6,22},{7,23},{8,24},{9,... | collective-permute-start | bytes 258056 | tf_op jit(solution)/shard_map/ppermute | solution.py:1022
  330.5 10.1 %collective-permute-start.34 = (bf16[112,384]{1,0:T(8,128)(2,1)S(1)}, bf16[112,384]{1,0:T(8,128)(2,1)S(1)}, u32[]{:S(2)}, u32[]{:S(2)}) collective-permute-start(bf16[112,384]{1,0:T(8,128)(2,1)S(1)} %pad_maximum_fusion.1), channel_id=1, source_target_pairs={{0,18},{1,19},{2,16},{3,17},{4,22},{5,23},{6,20},{7,21},{8,26},{9,... | collective-permute-start | bytes 258056 | tf_op jit(solution)/shard_map/ppermute | solution.py:1022
  340.7 13.0 %copy-start.14 = (bf16[1,256,384]{2,1,0:T(8,128)(2,1)}, bf16[1,256,384]{2,1,0:T(8,128)(2,1)S(1)}, u32[]{:S(2)}) copy-start(bf16[1,256,384]{2,1,0:T(8,128)(2,1)S(1)} %collective-permute-done.35.refs_1_) | copy-start | bytes 589828
  341.6 18.8 %collective-permute-start.40 = (bf16[448,384]{1,0:T(8,128)(2,1)S(1)}, bf16[448,384]{1,0:T(8,128)(2,1)S(1)}, u32[]{:S(2)}, u32[]{:S(2)}) collective-permute-start(bf16[448,384]{1,0:T(8,128)(2,1)S(1)} %constant_dynamic-update-slice_fusion), channel_id=1, source_target_pairs={{0,12},{1,13},{2,14},{3,15},{4,8},{5,9},{6,10},{7,11},{8,4},{9,5},... | collective-permute-start | bytes 1032200 | tf_op jit(solution)/shard_map/ppermute | solution.py:1022
  341.6 18.8 %collective-permute-start.39 = (bf16[448,384]{1,0:T(8,128)(2,1)S(1)}, bf16[448,384]{1,0:T(8,128)(2,1)}, u32[]{:S(2)}, u32[]{:S(2)}) collective-permute-start(bf16[448,384]{1,0:T(8,128)(2,1)S(1)} %constant_dynamic-update-slice_fusion), channel_id=1, source_target_pairs={{0,4},{1,5},{2,6},{3,7},{4,0},{5,1},{6,2},{7,3},{8,12},{9,13},{10,... | collective-permute-start | bytes 1032200 | tf_op jit(solution)/shard_map/ppermute | solution.py:1022
  342.9 17.5 %collective-permute-start.38 = (bf16[448,384]{1,0:T(8,128)(2,1)S(1)}, bf16[448,384]{1,0:T(8,128)(2,1)}, u32[]{:S(2)}, u32[]{:S(2)}) collective-permute-start(bf16[448,384]{1,0:T(8,128)(2,1)S(1)} %constant_dynamic-update-slice_fusion), channel_id=1, source_target_pairs={{0,8},{1,9},{2,10},{3,11},{4,12},{5,13},{6,14},{7,15},{8,0},{9,1},... | collective-permute-start | bytes 1032200 | tf_op jit(solution)/shard_map/ppermute | solution.py:1022
  362.8 3.5 collective-permute-start.41
  (23 other events, 81.5 us)
Sparse Core Ops, SparseCore 0:
  248.5 72.3 all-gather.1

commit v2 on v1

--- a/solution.py
+++ b/solution.py
@@ -136,10 +136,18 @@
     return total, sums
 
 
-def fill_packed(plain, moved, plane, matrix, values_low, cols):
-    tokens = values_low.shape[0]
-    plain[plane, pl.ds(cols, tokens), :] = values_low
-    moved[plane, pl.ds(cols, tokens), :] = mm(matrix, values_low).astype(BF)
+def column_moved(values, col_phase, cols):
+    tokens, lanes = values.shape
+    turned = pltpu.roll(values, 1 if col_phase else tokens - 1, 0).reshape(tokens // cols, cols, lanes)
+    spot = lax.broadcasted_iota(jnp.int32, (1, cols, lanes), 1)
+    edge = 0 if col_phase else cols - 1
+    return jnp.where(spot == edge, 0.0, turned).reshape(tokens, lanes)
+
+
+def fill_packed(plain, moved, plane, values, cols):
+    rows = pl.ds(cols, values.shape[0])
+    plain[plane, rows, :] = values.astype(BF)
+    moved[plane, rows, :] = column_moved(values, plane % 2, cols).astype(BF)
 
 
 def place_rows(ref, values, first_row, rank, parts):
@@ -278,6 +286,7 @@
     def _():
         for ref in (fc1_sum, fc2_sum, down_sum, small_ref, dconv_s):
             ref[...] = jnp.zeros(ref.shape, F32)
+        hid_t[pl.ds(width, 16), :] = jnp.ones((16, hid_t.shape[1]), BF)
         for ref in (plain_g, moved_g):
             zero_pads(ref, cols)
         for ref in (plain_p, moved_p):
@@ -290,9 +299,10 @@
 
     grad_low = og_ref[0]
     small_ref[pl.ds(10, 1), pl.ds(width, 2 * width)] += col_sum(grad_low.astype(F32))
+    grad_all = mm(grad_low, down_w[...], NT)
     for plane in range(4):
         rows = pl.ds(plane * tokens, tokens)
-        grad_after = mm(grad_low, down_w[pl.ds(plane * width, width), :], NT)
+        grad_after = grad_all[:, plane * width : (plane + 1) * width]
         gmid_ref[0, rows, :] = grad_after
         grad_out = (gate_two * grad_after).astype(BF)
         gffn_s[rows, :] = grad_out
@@ -301,7 +311,7 @@
         unit, _ = normed(after)
         hid_s[rows, :] = (unit * (1.0 + scale_two) + shift_two).astype(BF)
 
-    hid_t[...] = hid_s[...].T
+    hid_t[pl.ds(0, width), :] = hid_s[...].T
     gffn_t[...] = gffn_s[...].T
     chunks = hidden // CHUNK
 
@@ -310,13 +320,12 @@
 
     def prepare(chunk, slot):
         units = units_of(chunk)
-        pre = (mm(hid_s[...], fc1_w[:, units]) + fc1_b[:, units]).astype(BF)
+        pre = mm(hid_s[...], fc1_w[:, units]) + fc1_b[:, units]
         for plane in range(4):
             fill_packed(
                 plain_p.at[slot],
                 moved_p.at[slot],
                 plane,
-                moves[plane % 2],
                 pre[plane * tokens : (plane + 1) * tokens],
                 cols,
             )
@@ -324,11 +333,11 @@
 
     def collect(chunk, slot):
         units = units_of(chunk)
-        ones = jnp.ones((16, act_s.shape[1]), BF)
         grad_pre = gpre_s[slot]
         active = act_s[slot]
-        fc1_sum[:, units] += mm(hid_t[...], grad_pre)
-        small_ref[pl.ds(9, 1), units] += mm(ones, grad_pre)[:1]
+        sums = mm(hid_t[...], grad_pre)
+        fc1_sum[:, units] += sums[:width]
+        small_ref[pl.ds(9, 1), units] += sums[width : width + 1]
         fc2_sum[:, units] += mm(gffn_t[...], active)
         out = mm(active, fc2_w[units, :])
         grad_hid = mm(grad_pre, fc1_w[:, units], NT)
@@ -423,7 +432,7 @@
         down_sum[:, units] += mm(grad_low_t, low_s[:, units])
         return carry
 
-    lax.fori_loop(0, low_s.shape[1] // CHUNK, down_weights, 0)
+    lax.fori_loop(0, low_s.shape[1] // CHUNK, down_weights, 0, unroll=True)
 
     @pl.when(image == pl.num_programs(0) - 1)
     def _():
@@ -479,11 +488,11 @@
     head_size = width // HEADS
     factor = jnp.asarray(head_size ** (-0.5), BF)
 
+    gout_s[...] = (gate_one * gmid_ref[0]).astype(BF)
+    gmix_s[...] = mm(gout_s[...], proj_w[...], NT).astype(BF)
+
     def attend(plane, carry):
         rows = pl.ds(pl.multiple_of(plane * tokens, tokens), tokens)
-        grad_out = (gate_one * gmid_ref[0, rows, :]).astype(BF)
-        gout_s[rows, :] = grad_out
-        gmix_s[...] = mm(grad_out, proj_w[...], NT).astype(BF)
         even = lax.broadcasted_iota(jnp.int32, (tokens, LANES), 1) < head_size
         zero = jnp.zeros((tokens, LANES), BF)
         for pair in range(width // LANES):
@@ -493,7 +502,7 @@
             value = qkv_ref[0, rows, pl.ds(2 * width + lane, LANES)]
             query_low = query * factor
             key_t = key.T
-            grad_mixed = gmix_s[:, pl.ds(lane, LANES)]
+            grad_mixed = gmix_s[rows, pl.ds(lane, LANES)]
 
             def heads(values):
                 return jnp.concatenate([jnp.where(even, values, zero), jnp.where(even, zero, values)], axis=0)
@@ -524,7 +533,7 @@
             gqkv_ref[0, rows, pl.ds(2 * width + lane, LANES)] = grad_value.astype(BF)
         return carry
 
-    lax.fori_loop(0, 4, attend, 0)
+    lax.fori_loop(0, 4, attend, 0, unroll=2)
 
     sum_ref[:, pl.ds(3 * width, width)] += mm(mix_ref[0].T, gout_s[...])
     conv_t = co_ref[0].T
@@ -830,7 +839,7 @@
             pltpu.VMEM((2, all_tokens, CHUNK), BF),
             pltpu.VMEM((2, all_tokens, CHUNK), BF),
             pltpu.VMEM((2, all_tokens, CHUNK), BF),
-            pltpu.VMEM((width, all_tokens), BF),
+            pltpu.VMEM((width + 16, all_tokens), BF),
             pltpu.VMEM((width, all_tokens), BF),
             pltpu.VMEM((tokens, 4 * width), BF),
             pltpu.VMEM((9, 8, hidden), F32),
@@ -871,7 +880,7 @@
         out_specs=[per_image(s) for s, _ in outs] + [resident(s) for s, _ in sums],
         scratch_shapes=[
             pltpu.VMEM((all_tokens, width), BF),
-            pltpu.VMEM((all_tokens // 4, width), BF),
+            pltpu.VMEM((all_tokens, width), BF),
         ],
     )
     return pl.pallas_call(

time: 383 us -> 371 us (0.969)
  Pallas kernels: 261 us -> 246 us
  waiting for transfers between devices: 25.4 us -> 29.8 us
    pallas_call x1, Pallas kernels: 111 us -> 99.8 us  [feed_forward_call(): pl.pallas_call(functools.partial(feed_forward_kernel, parts=parts), grid_...]
    ppermute x21, waiting for transfers between devices: 20.1 us -> 24.6 us  [exchange(): return lax.ppermute(values, AXES, [(i, i ^ mask) for i in range(devices)])]
  transfers between devices with their start and end apart: 43 -> 43, of which waited for: 12 -> 14; matrix products, arithmetic and copies ran while one was open for 5% -> 5% of each run, Pallas kernels for 35% -> 36%
where the time goes in v2:
time: 371 us; the launch traced here: 366 us
  Pallas kernels  246 us (66%)
  starting transfers between devices  39 us (11%)
  waiting for transfers between devices  29.8 us (8%)
  local copies, waits for them, and re-layouts  18.5 us (5%)
  other arithmetic  17.6 us (5%)
  between operations  15.1 us (4%)
    pallas_call x1, Pallas kernels, feed_forward_call(): pl.pallas_call(functools.partial(feed_forward_kernel, parts=parts), grid_...  99.8 us
    pallas_call x2, Pallas kernels, attention_back_call(): pl.pallas_call(functools.partial(attention_back_kernel, parts=parts, begi...  46.6 us
    pallas_call x4, Pallas kernels, attention_forward_call(): pl.pallas_call(functools.partial(attention_forward_kernel, strips, begin)...  42.1 us
    pallas_call x3, Pallas kernels, conv_attn_back_call(): pl.pallas_call(functools.partial(conv_attn_back_kernel, strips), grid_spe...  33.4 us
    ppermute x21, waiting for transfers between devices, exchange(): return lax.ppermute(values, AXES, [(i, i ^ mask) for i in range(devices)])  24.6 us
    ppermute x21, starting transfers between devices, exchange(): return lax.ppermute(values, AXES, [(i, i ^ mask) for i in range(devices)])  23.6 us
    ppermute x21, starting transfers between devices, swap_strips(): return lax.ppermute(values, 'narrow', [(i, i ^ mask) for i in range(count)])  15.4 us
    pallas_call x3, Pallas kernels, finish_latents_call(): pl.pallas_call(functools.partial(finish_latents_kernel, strips), grid_spe...  9.92 us
  transfers between devices with their start and end apart: 43, of which 14 were waited for; matrix products, arithmetic and copies ran while one was open for 5% of the time, Pallas kernels for 36%

profile of v2, /device:TPU:0, one launch (start us, length us, event | category | flops | bytes accessed | tf_op | source)
XLA Modules:
  0.0 366.3 jit_solution(2564604313008106699)
XLA Ops:
  7.3 3.4 dynamic-slice_bitcast_fusion
  11.2 2.6 collective-permute-start.1
  21.2 2.1 collective-permute-done.2.refs_3_
  23.4 1.7 collective-permute-start.4
  25.1 10.7 %attention_forward.4 = (bf16[4,1024,384]{2,1,0:T(8,128)(2,1)}, bf16[4,1024,384]{2,1,0:T(8,128)(2,1)}, bf16[4,1024,1152]{2,1,0:T(8,128)(2,1)}, bf16[4,1024,384]{2,1,0:T(8,128)(2,1)}, f32[4,4,8,256]{3,2,1,0:T(8,128)}) custom-call(s32[2]{0:T(128)} %pad_add_fusion.rank_ref, bf16[256,384]{1,0:T(8,128)(2,1)} %get-tuple-element.177.refs_0_, ...), custom_call_target="tpu_custom_call" | custom-call | flops 5000000000 | bytes 8000000 | tf_op jit(solution)/shard_map/attention_forward/pallas_call | solution.py:799
  37.0 1.7 collective-permute-start.7
  38.7 10.5 %attention_forward.5 = (bf16[4,1024,384]{2,1,0:T(8,128)(2,1)}, bf16[4,1024,384]{2,1,0:T(8,128)(2,1)}, bf16[4,1024,1152]{2,1,0:T(8,128)(2,1)}, bf16[4,1024,384]{2,1,0:T(8,128)(2,1)}, f32[4,4,8,256]{3,2,1,0:T(8,128)}) custom-call(s32[2]{0:T(128)} %pad_add_fusion.rank_ref, ...), custom_call_target="tpu_custom_call", output_to_operand_aliasing={{0}: (10, {}), {1}: (11, {}), {2}: (12, {}), {3}: (13, {}),... | custom-call | flops 5000000000 | bytes 8000000 | tf_op jit(solution)/shard_map/attention_forward/pallas_call | solution.py:799
  49.8 1.7 collective-permute-start.10
  51.5 10.5 %attention_forward.6 = (bf16[4,1024,384]{2,1,0:T(8,128)(2,1)}, bf16[4,1024,384]{2,1,0:T(8,128)(2,1)}, bf16[4,1024,1152]{2,1,0:T(8,128)(2,1)}, bf16[4,1024,384]{2,1,0:T(8,128)(2,1)}, f32[4,4,8,256]{3,2,1,0:T(8,128)}) custom-call(s32[2]{0:T(128)} %pad_add_fusion.rank_ref, ...), custom_call_target="tpu_custom_call", output_to_operand_aliasing={{0}: (10, {}), {1}: (11, {}), {2}: (12, {}), {3}: (13, {}),... | custom-call | flops 5000000000 | bytes 8000000 | tf_op jit(solution)/shard_map/attention_forward/pallas_call | solution.py:799
  62.7 10.4 %attention_forward.7 = (bf16[4,1024,384]{2,1,0:T(8,128)(2,1)}, bf16[4,1024,384]{2,1,0:T(8,128)(2,1)}, bf16[4,1024,1152]{2,1,0:T(8,128)(2,1)}, bf16[4,1024,384]{2,1,0:T(8,128)(2,1)}, f32[4,4,8,256]{3,2,1,0:T(8,128)}) custom-call(s32[2]{0:T(128)} %pad_add_fusion.rank_ref, ...), custom_call_target="tpu_custom_call", output_to_operand_aliasing={{0}: (10, {}), {1}: (11, {}), {2}: (12, {}), {3}: (13, {}),... | custom-call | flops 5000000000 | bytes 8000000 | tf_op jit(solution)/shard_map/attention_forward/pallas_call | solution.py:799
  73.2 99.8 %feed_forward.1 = (bf16[4,256,768]{2,1,0:T(8,128)(2,1)}, f32[4,1024,384]{2,1,0:T(8,128)}, f32[4,8,384]{2,1,0:T(8,128)}, bf16[6144,384]{1,0:T(8,128)(2,1)}, f32[16,1536]{1,0:T(8,128)}) custom-call(s32[2]{0:T(128)} %pad_add_fusion.rank_ref, bf16[4,1024,384]{2,1,0:T(8,128)(2,1)} %get-tuple-element.196.xp_ref, bf16[4,1024,384]{2,1,0:T(8,128)(2,1)} %get-tuple-element.197.mix_ref, ...), custom_call_target="tpu_custom_call" | custom-call | flops 56000000000 | bytes 80000000 | tf_op jit(solution)/shard_map/feed_forward/pallas_call | solution.py:851
  173.0 2.1 slice.69
  175.5 4.2 %collective-permute-done.12 = bf16[3072,384]{1,0:T(8,128)(2,1)S(1)} collective-permute-done((bf16[3072,384]{1,0:T(8,128)(2,1)S(1)}, bf16[3072,384]{1,0:T(8,128)(2,1)S(1)}, u32[]{:S(2)}, u32[]{:S(2)}) %collective-permute-start.12) | collective-permute-done | bytes 2359328 | tf_op jit(solution)/shard_map/ppermute | solution.py:1031
  180.3 1.4 copy-done
  182.9 2.7 collective-permute-start.15
  186.4 22.2 %attention_back.2 = (bf16[2,1024,1152]{2,1,0:T(8,128)(2,1)}, f32[384,1536]{1,0:T(8,128)}) custom-call(s32[2]{0:T(128)} %pad_add_fusion.rank_ref, f32[4,8,384]{2,1,0:T(8,128)} %pad.19.refs_4_.mod_ref, f32[4,1024,384]{2,1,0:T(8,128)} %get-tuple-element.202.gmid_ref, bf16[4,1024,384]{2,1,0:T(8,128)(2,1)} %get-tuple-element.203.co_ref, ...), custom_call_target="tpu_custom_call" | custom-call | flops 16000000000 | bytes 20000000 | tf_op jit(solution)/shard_map/attention_back/pallas_call | solution.py:886
  208.6 3.8 %collective-permute-done.14 = bf16[768,384]{1,0:T(8,128)(2,1)} collective-permute-done((bf16[768,384]{1,0:T(8,128)(2,1)}, bf16[768,384]{1,0:T(8,128)(2,1)}, u32[]{:S(2)}, u32[]{:S(2)}) %collective-permute-start.14) | collective-permute-done | bytes 589856 | tf_op jit(solution)/shard_map/ppermute | solution.py:1031
  212.6 1.9 add_convert_fusion.2
  215.2 3.5 collective-permute-start.18
  219.6 15.3 %conv_attn_back.3 = (bf16[2,256,384]{2,1,0:T(8,128)(2,1)}, bf16[2,256,384]{2,1,0:T(8,128)(2,1)}, bf16[2,256,384]{2,1,0:T(8,128)(2,1)}, bf16[2,256,384]{2,1,0:T(8...) custom-call(s32[2]{0:T(128)} %pad_add_fusion.rank_ref, bf16[4,1024,384]{2,1,0:T(8,128)(2,1)} %get-tuple-element.196.xp_ref, ...), custom_call_target="tpu_custom_call" | custom-call | flops 8000000000 | bytes 16000000 | tf_op jit(solution)/shard_map/conv_attn_back/pallas_call | solution.py:920
  234.9 1.8 add_convert_fusion.5
  236.8 1.6 collective-permute-start.20
  238.7 24.4 %attention_back.3 = (bf16[2,1024,1152]{2,1,0:T(8,128)(2,1)}, f32[384,1536]{1,0:T(8,128)}, bf16[2048,384]{1,0:T(8,128)(2,1)}) custom-call(s32[2]{0:T(128)} %pad_add_fusion.rank_ref, f32[4,8,384]{2,1,0:T(8,128)} %pad.19.refs_4_.mod_ref, f32[4,1024,384]{2,1,0:T(8,128)} %get-tuple-element.202.gmid_ref, bf16[4,1024,384]{2,1,0:T(8,128)(2,1)} %get-tuple-element.203.co_ref, ...), custom_call_target="tpu_custom_call" | custom-call | flops 16000000000 | bytes 20000000 | tf_op jit(solution)/shard_map/attention_back/pallas_call | solution.py:886
  265.7 1.4 slice.98
  267.7 9.1 %conv_attn_back.4 = (bf16[1,256,384]{2,1,0:T(8,128)(2,1)}, bf16[1,256,384]{2,1,0:T(8,128)(2,1)}, bf16[1,256,384]{2,1,0:T(8,128)(2,1)}, bf16[1,256,384]{2,1,0:T(8...) custom-call(s32[2]{0:T(128)} %pad_add_fusion.rank_ref, bf16[4,1024,384]{2,1,0:T(8,128)(2,1)} %get-tuple-element.196.xp_ref, ...), custom_call_target="tpu_custom_call" | custom-call | flops 4000000000 | bytes 8000000 | tf_op jit(solution)/shard_map/conv_attn_back/pallas_call | solution.py:920
  276.8 1.3 convert.34
  278.1 1.6 add_convert_fusion.1
  280.4 1.5 collective-permute-start.25
  282.0 1.5 collective-permute-start.24
  283.9 1.5 collective-permute-start.27
  285.4 9.0 %conv_attn_back.5 = (bf16[1,256,384]{2,1,0:T(8,128)(2,1)}, bf16[1,256,384]{2,1,0:T(8,128)(2,1)}, bf16[1,256,384]{2,1,0:T(8,128)(2,1)}, bf16[1,256,384]{2,1,0:T(8...) custom-call(s32[2]{0:T(128)} %pad_add_fusion.rank_ref, bf16[4,1024,384]{2,1,0:T(8,128)(2,1)} %get-tuple-element.196.xp_ref, ...), custom_call_target="tpu_custom_call" | custom-call | flops 4000000000 | bytes 8000000 | tf_op jit(solution)/shard_map/conv_attn_back/pallas_call | solution.py:920
  296.0 1.7 collective-permute-done.24
  300.0 2.3 collective-permute-done.28.refs_3_
  302.3 2.6 collective-permute-start.31
  304.9 1.4 collective-permute-start.30
  307.5 4.7 %collective-permute-done.31 = bf16[64,384]{1,0:T(8,128)(2,1)S(1)} collective-permute-done((bf16[64,384]{1,0:T(8,128)(2,1)S(1)}, bf16[64,384]{1,0:T(8,128)(2,1)S(1)}, u32[]{:S(2)}, u32[]{:S(2)}) %collective-permute-start.31) | collective-permute-done | bytes 49184 | tf_op jit(solution)/shard_map/ppermute | solution.py:1031
  314.0 1.5 collective-permute-start.32
  316.1 1.3 collective-permute-start.37
  318.5 1.8 collective-permute-start.34
  320.3 5.6 %collective-permute-done.33 = bf16[112,384]{1,0:T(8,128)(2,1)S(1)} collective-permute-done((bf16[112,384]{1,0:T(8,128)(2,1)S(1)}, bf16[112,384]{1,0:T(8,128)(2,1)S(1)}, u32[]{:S(2)}, u32[]{:S(2)}) %collective-permute-start.33) | collective-permute-done | bytes 86048 | tf_op jit(solution)/shard_map/ppermute | solution.py:1031
  325.9 1.8 collective-permute-done.34
  329.7 2.6 collective-permute-start.38
  332.3 8.5 %finish_big.1 = (f32[384,1536]{1,0:T(8,128)}, f32[1536,384]{1,0:T(8,128)}, f32[1536,768]{1,0:T(8,128)}) custom-call(bf16[6144,384]{1,0:T(8,128)(2,1)} %all-gather.2.cloned.1.call-done.refs_0_.refs_1_.refs_2_.refs_3_, bf16[6144,384]{1,0:T(8,128)(2,1)} %all-gather.2.cloned.1.call-done.refs_0_.refs_1_.refs_2_.refs_3_, ...), custom_call_target="tpu_custom_call" | custom-call | bytes 15000000 | tf_op jit(solution)/shard_map/finish_big/pallas_call | solution.py:966
  340.8 3.7 finish_latents.3.refs_4_
  344.5 3.1 finish_latents.4.refs_4_
  347.6 2.3 pad_maximum_fusion
  349.9 3.1 finish_latents.5
  353.4 5.6 %finish_rest.1 = (f32[384,1152]{1,0:T(8,128)}, f32[384,384]{1,0:T(8,128)}, f32[3,3,1536]{2,1,0:T(4,128)}, f32[1536]{0:T(1024)}, f32[384]{0:T(512)}, /*index=5*/f...) custom-call(s32[2]{0:T(128)} %pad_add_fusion.rank_ref, bf16[16,112,384]{2,1,0:T(8,128)(2,1)} %bitcast.22.own_ref, ...), custom_call_target="tpu_custom_call" | custom-call | bytes 8000000 | tf_op jit(solution)/shard_map/finish_rest/pallas_call | solution.py:1002
  (161 shorter events, 30.9 us)
Async XLA Ops:
  7.2 321.6 %all-gather.2.cloned.1.call-start = ((), (), s32[]{:S(2)}) async-start(), calls=%async_computation | async-start | bytes 4866048 | tf_op jit(solution)/shard_map/all_gather | solution.py:1178
  7.3 9.6 %copy-start.22 = (bf16[768]{0:T(1024)(128)(2,1)S(1)}, bf16[768]{0:T(1024)(128)(2,1)}, u32[]{:S(2)}) copy-start(bf16[768]{0:T(1024)(128)(2,1)} %param.29) | copy-start | bytes 4612
  7.3 10.1 %copy-start.16 = (bf16[3,3,1536]{2,1,0:T(4,128)(2,1)S(1)}, bf16[3,3,1536]{2,1,0:T(4,128)(2,1)}, u32[]{:S(2)}) copy-start(bf16[3,3,1536]{2,1,0:T(4,128)(2,1)} %param.25) | copy-start | bytes 82948
  10.7 10.5 %collective-permute-start = (bf16[256,384]{1,0:T(8,128)(2,1)S(1)}, bf16[256,384]{1,0:T(8,128)(2,1)S(1)}, u32[]{:S(2)}, u32[]{:S(2)}) collective-permute-start(bf16[256,384]{1,0:T(8,128)(2,1)S(1)} %get-tuple-element.318), channel_id=1, source_target_pairs={{0,1},{1,0},{2,3},{3,2},{4,5},{5,4},{6,7},{7,6},{8,9},{9,8},{10,11... | collective-permute-start | bytes 589832 | tf_op jit(solution)/shard_map/ppermute | solution.py:1036
  11.2 10.0 %collective-permute-start.1 = (bf16[256,384]{1,0:T(8,128)(2,1)S(1)}, bf16[256,384]{1,0:T(8,128)(2,1)S(1)}, u32[]{:S(2)}, u32[]{:S(2)}) collective-permute-start(bf16[256,384]{1,0:T(8,128)(2,1)S(1)} %get-tuple-element.317), channel_id=1, source_target_pairs={{0,2},{1,3},{2,0},{3,1},{4,6},{5,7},{6,4},{7,5},{8,10},{9,11},{10,... | collective-permute-start | bytes 589832 | tf_op jit(solution)/shard_map/ppermute | solution.py:1036
  13.8 9.4 %collective-permute-start.2 = (bf16[256,384]{1,0:T(8,128)(2,1)S(1)}, bf16[256,384]{1,0:T(8,128)(2,1)S(1)}, u32[]{:S(2)}, u32[]{:S(2)}) collective-permute-start(bf16[256,384]{1,0:T(8,128)(2,1)S(1)} %get-tuple-element.316), channel_id=1, source_target_pairs={{0,3},{1,2},{2,1},{3,0},{4,7},{5,6},{6,5},{7,4},{8,11},{9,10},{10,... | collective-permute-start | bytes 589832 | tf_op jit(solution)/shard_map/ppermute | solution.py:1036
  23.2 12.6 %collective-permute-start.3 = (bf16[256,384]{1,0:T(8,128)(2,1)}, bf16[256,384]{1,0:T(8,128)(2,1)S(1)}, u32[]{:S(2)}, u32[]{:S(2)}) collective-permute-start(bf16[256,384]{1,0:T(8,128)(2,1)} %get-tuple-element.158), channel_id=1, source_target_pairs={{0,1},{1,0},{2,3},{3,2},{4,5},{5,4},{6,7},{7,6},{8,9},{9,8},{10,11... | collective-permute-start | bytes 589832 | tf_op jit(solution)/shard_map/ppermute | solution.py:1036
  23.4 12.5 %collective-permute-start.4 = (bf16[256,384]{1,0:T(8,128)(2,1)S(1)}, bf16[256,384]{1,0:T(8,128)(2,1)S(1)}, u32[]{:S(2)}, u32[]{:S(2)}) collective-permute-start(bf16[256,384]{1,0:T(8,128)(2,1)S(1)} %get-tuple-element.159), channel_id=1, source_target_pairs={{0,2},{1,3},{2,0},{3,1},{4,6},{5,7},{6,4},{7,5},{8,10},{9,11},{10,... | collective-permute-start | bytes 589832 | tf_op jit(solution)/shard_map/ppermute | solution.py:1036
  25.1 10.8 %collective-permute-start.5 = (bf16[256,384]{1,0:T(8,128)(2,1)S(1)}, bf16[256,384]{1,0:T(8,128)(2,1)S(1)}, u32[]{:S(2)}, u32[]{:S(2)}) collective-permute-start(bf16[256,384]{1,0:T(8,128)(2,1)S(1)} %get-tuple-element.160), channel_id=1, source_target_pairs={{0,3},{1,2},{2,1},{3,0},{4,7},{5,6},{6,5},{7,4},{8,11},{9,10},{10,... | collective-permute-start | bytes 589832 | tf_op jit(solution)/shard_map/ppermute | solution.py:1036
  36.6 12.6 %collective-permute-start.6 = (bf16[256,384]{1,0:T(8,128)(2,1)}, bf16[256,384]{1,0:T(8,128)(2,1)S(1)}, u32[]{:S(2)}, u32[]{:S(2)}) collective-permute-start(bf16[256,384]{1,0:T(8,128)(2,1)} %get-tuple-element.162), channel_id=1, source_target_pairs={{0,1},{1,0},{2,3},{3,2},{4,5},{5,4},{6,7},{7,6},{8,9},{9,8},{10,11... | collective-permute-start | bytes 589832 | tf_op jit(solution)/shard_map/ppermute | solution.py:1036
  37.0 12.2 %collective-permute-start.7 = (bf16[256,384]{1,0:T(8,128)(2,1)}, bf16[256,384]{1,0:T(8,128)(2,1)S(1)}, u32[]{:S(2)}, u32[]{:S(2)}) collective-permute-start(bf16[256,384]{1,0:T(8,128)(2,1)} %get-tuple-element.163), channel_id=1, source_target_pairs={{0,2},{1,3},{2,0},{3,1},{4,6},{5,7},{6,4},{7,5},{8,10},{9,11},{10,... | collective-permute-start | bytes 589832 | tf_op jit(solution)/shard_map/ppermute | solution.py:1036
  38.7 10.5 %collective-permute-start.8 = (bf16[256,384]{1,0:T(8,128)(2,1)}, bf16[256,384]{1,0:T(8,128)(2,1)S(1)}, u32[]{:S(2)}, u32[]{:S(2)}) collective-permute-start(bf16[256,384]{1,0:T(8,128)(2,1)} %get-tuple-element.164), channel_id=1, source_target_pairs={{0,3},{1,2},{2,1},{3,0},{4,7},{5,6},{6,5},{7,4},{8,11},{9,10},{10,... | collective-permute-start | bytes 589832 | tf_op jit(solution)/shard_map/ppermute | solution.py:1036
  49.2 12.7 %collective-permute-start.9 = (bf16[256,384]{1,0:T(8,128)(2,1)}, bf16[256,384]{1,0:T(8,128)(2,1)S(1)}, u32[]{:S(2)}, u32[]{:S(2)}) collective-permute-start(bf16[256,384]{1,0:T(8,128)(2,1)} %get-tuple-element.166), channel_id=1, source_target_pairs={{0,1},{1,0},{2,3},{3,2},{4,5},{5,4},{6,7},{7,6},{8,9},{9,8},{10,11... | collective-permute-start | bytes 589832 | tf_op jit(solution)/shard_map/ppermute | solution.py:1036
  49.8 12.2 %collective-permute-start.10 = (bf16[256,384]{1,0:T(8,128)(2,1)}, bf16[256,384]{1,0:T(8,128)(2,1)S(1)}, u32[]{:S(2)}, u32[]{:S(2)}) collective-permute-start(bf16[256,384]{1,0:T(8,128)(2,1)} %get-tuple-element.167), channel_id=1, source_target_pairs={{0,2},{1,3},{2,0},{3,1},{4,6},{5,7},{6,4},{7,5},{8,10},{9,11},{10,... | collective-permute-start | bytes 589832 | tf_op jit(solution)/shard_map/ppermute | solution.py:1036
  51.4 10.6 %collective-permute-start.11 = (bf16[256,384]{1,0:T(8,128)(2,1)}, bf16[256,384]{1,0:T(8,128)(2,1)}, u32[]{:S(2)}, u32[]{:S(2)}) collective-permute-start(bf16[256,384]{1,0:T(8,128)(2,1)} %get-tuple-element.168), channel_id=1, source_target_pairs={{0,3},{1,2},{2,1},{3,0},{4,7},{5,6},{6,5},{7,4},{8,11},{9,10},{10,... | collective-permute-start | bytes 589832 | tf_op jit(solution)/shard_map/ppermute | solution.py:1036
  175.0 4.7 %collective-permute-start.12 = (bf16[3072,384]{1,0:T(8,128)(2,1)S(1)}, bf16[3072,384]{1,0:T(8,128)(2,1)S(1)}, u32[]{:S(2)}, u32[]{:S(2)}) collective-permute-start(bf16[3072,384]{1,0:T(8,128)(2,1)S(1)} %slice.69), channel_id=1, source_target_pairs={{0,1},{1,0},{2,3},{3,2},{4,5},{5,4},{6,7},{7,6},{8,9},{9,8},{10,11... | collective-permute-start | bytes 7077896 | tf_op jit(solution)/shard_map/ppermute | solution.py:1031
  182.9 25.7 %collective-permute-start.15 = (bf16[768,384]{1,0:T(8,128)(2,1)}, bf16[768,384]{1,0:T(8,128)(2,1)}, u32[]{:S(2)}, u32[]{:S(2)}) collective-permute-start(bf16[768,384]{1,0:T(8,128)(2,1)} %get-tuple-element.321), channel_id=1, source_target_pairs={{0,12},{1,13},{2,14},{3,15},{4,8},{5,9},{6,10},{7,11},{8,4},{9,5},... | collective-permute-start | bytes 1769480 | tf_op jit(solution)/shard_map/ppermute | solution.py:1031
  185.6 26.8 %collective-permute-start.14 = (bf16[768,384]{1,0:T(8,128)(2,1)}, bf16[768,384]{1,0:T(8,128)(2,1)}, u32[]{:S(2)}, u32[]{:S(2)}) collective-permute-start(bf16[768,384]{1,0:T(8,128)(2,1)} %get-tuple-element.322), channel_id=1, source_target_pairs={{0,4},{1,5},{2,6},{3,7},{4,0},{5,1},{6,2},{7,3},{8,12},{9,13},{10,... | collective-permute-start | bytes 1769480 | tf_op jit(solution)/shard_map/ppermute | solution.py:1031
  186.1 26.5 %collective-permute-start.13 = (bf16[768,384]{1,0:T(8,128)(2,1)S(1)}, bf16[768,384]{1,0:T(8,128)(2,1)}, u32[]{:S(2)}, u32[]{:S(2)}) collective-permute-start(bf16[768,384]{1,0:T(8,128)(2,1)S(1)} %get-tuple-element.320), channel_id=1, source_target_pairs={{0,8},{1,9},{2,10},{3,11},{4,12},{5,13},{6,14},{7,15},{8,0},{9,1},... | collective-permute-start | bytes 1769480 | tf_op jit(solution)/shard_map/ppermute | solution.py:1031
  215.2 19.7 %collective-permute-start.18 = (bf16[192,384]{1,0:T(8,128)(2,1)}, bf16[192,384]{1,0:T(8,128)(2,1)}, u32[]{:S(2)}, u32[]{:S(2)}) collective-permute-start(bf16[192,384]{1,0:T(8,128)(2,1)} %get-tuple-element.327), channel_id=1, source_target_pairs={{0,18},{1,19},{2,16},{3,17},{4,22},{5,23},{6,20},{7,21},{8,26},{9,... | collective-permute-start | bytes 442376 | tf_op jit(solution)/shard_map/ppermute | solution.py:1031
  218.8 16.2 %collective-permute-start.17 = (bf16[192,384]{1,0:T(8,128)(2,1)S(1)}, bf16[192,384]{1,0:T(8,128)(2,1)}, u32[]{:S(2)}, u32[]{:S(2)}) collective-permute-start(bf16[192,384]{1,0:T(8,128)(2,1)S(1)} %get-tuple-element.328), channel_id=1, source_target_pairs={{0,16},{1,17},{2,18},{3,19},{4,20},{5,21},{6,22},{7,23},{8,24},{9,... | collective-permute-start | bytes 442376 | tf_op jit(solution)/shard_map/ppermute | solution.py:1031
  219.1 15.8 %collective-permute-start.16 = (bf16[192,384]{1,0:T(8,128)(2,1)S(1)}, bf16[192,384]{1,0:T(8,128)(2,1)}, u32[]{:S(2)}, u32[]{:S(2)}) collective-permute-start(bf16[192,384]{1,0:T(8,128)(2,1)S(1)} %get-tuple-element.326), channel_id=1, source_target_pairs={{0,2},{1,3},{2,0},{3,1},{4,6},{5,7},{6,4},{7,5},{8,10},{9,11},{10,... | collective-permute-start | bytes 442376 | tf_op jit(solution)/shard_map/ppermute | solution.py:1031
  236.7 26.4 %collective-permute-start.19 = (bf16[2,256,384]{2,1,0:T(8,128)(2,1)}, bf16[2,256,384]{2,1,0:T(8,128)(2,1)S(1)}, u32[]{:S(2)}, u32[]{:S(2)}) collective-permute-start(bf16[2,256,384]{2,1,0:T(8,128)(2,1)} %get-tuple-element.219), channel_id=1, source_target_pairs={{0,1},{1,0},{2,3},{3,2},{4,5},{5,4},{6,7},{7,6},{8,9},{9,8},{10,11... | collective-permute-start | bytes 1179656 | tf_op jit(solution)/shard_map/ppermute | solution.py:1036
  236.8 26.3 %collective-permute-start.20 = (bf16[2,256,384]{2,1,0:T(8,128)(2,1)}, bf16[2,256,384]{2,1,0:T(8,128)(2,1)S(1)}, u32[]{:S(2)}, u32[]{:S(2)}) collective-permute-start(bf16[2,256,384]{2,1,0:T(8,128)(2,1)} %get-tuple-element.220), channel_id=1, source_target_pairs={{0,2},{1,3},{2,0},{3,1},{4,6},{5,7},{6,4},{7,5},{8,10},{9,11},{10,... | collective-permute-start | bytes 1179656 | tf_op jit(solution)/shard_map/ppermute | solution.py:1036
  238.4 24.8 %collective-permute-start.21 = (bf16[2,256,384]{2,1,0:T(8,128)(2,1)}, bf16[2,256,384]{2,1,0:T(8,128)(2,1)}, u32[]{:S(2)}, u32[]{:S(2)}) collective-permute-start(bf16[2,256,384]{2,1,0:T(8,128)(2,1)} %get-tuple-element.221), channel_id=1, source_target_pairs={{0,3},{1,2},{2,1},{3,0},{4,7},{5,6},{6,5},{7,4},{8,11},{9,10},{10,... | collective-permute-start | bytes 1179656 | tf_op jit(solution)/shard_map/ppermute | solution.py:1036
  238.7 28.4 %copy-start.17 = (f32[2,8,384]{2,1,0:T(8,128)S(1)}, f32[2,8,384]{2,1,0:T(8,128)}, u32[]{:S(2)}) copy-start(f32[2,8,384]{2,1,0:T(8,128)} %get-tuple-element.250) | copy-start | bytes 73732
  265.2 12.8 %collective-permute-start.22 = (bf16[1024,384]{1,0:T(8,128)(2,1)S(1)}, bf16[1024,384]{1,0:T(8,128)(2,1)}, u32[]{:S(2)}, u32[]{:S(2)}) collective-permute-start(bf16[1024,384]{1,0:T(8,128)(2,1)S(1)} %slice.79), channel_id=1, source_target_pairs={{0,1},{1,0},{2,3},{3,2},{4,5},{5,4},{6,7},{7,6},{8,9},{9,8},{10,11... | collective-permute-start | bytes 2359304 | tf_op jit(solution)/shard_map/ppermute | solution.py:1031
  280.4 14.8 %collective-permute-start.25 = (bf16[256,384]{1,0:T(8,128)(2,1)}, bf16[256,384]{1,0:T(8,128)(2,1)}, u32[]{:S(2)}, u32[]{:S(2)}) collective-permute-start(bf16[256,384]{1,0:T(8,128)(2,1)} %get-tuple-element.324), channel_id=1, source_target_pairs={{0,12},{1,13},{2,14},{3,15},{4,8},{5,9},{6,10},{7,11},{8,4},{9,5},... | collective-permute-start | bytes 589832 | tf_op jit(solution)/shard_map/ppermute | solution.py:1031
  282.0 15.7 %collective-permute-start.24 = (bf16[256,384]{1,0:T(8,128)(2,1)}, bf16[256,384]{1,0:T(8,128)(2,1)}, u32[]{:S(2)}, u32[]{:S(2)}) collective-permute-start(bf16[256,384]{1,0:T(8,128)(2,1)} %get-tuple-element.325), channel_id=1, source_target_pairs={{0,4},{1,5},{2,6},{3,7},{4,0},{5,1},{6,2},{7,3},{8,12},{9,13},{10,... | collective-permute-start | bytes 589832 | tf_op jit(solution)/shard_map/ppermute | solution.py:1031
  283.5 15.3 %collective-permute-start.23 = (bf16[256,384]{1,0:T(8,128)(2,1)S(1)}, bf16[256,384]{1,0:T(8,128)(2,1)}, u32[]{:S(2)}, u32[]{:S(2)}) collective-permute-start(bf16[256,384]{1,0:T(8,128)(2,1)S(1)} %get-tuple-element.323), channel_id=1, source_target_pairs={{0,8},{1,9},{2,10},{3,11},{4,12},{5,13},{6,14},{7,15},{8,0},{9,1},... | collective-permute-start | bytes 589832 | tf_op jit(solution)/shard_map/ppermute | solution.py:1031
  283.9 16.0 %collective-permute-start.26 = (bf16[1,256,384]{2,1,0:T(8,128)(2,1)}, bf16[1,256,384]{2,1,0:T(8,128)(2,1)}, u32[]{:S(2)}, u32[]{:S(2)}) collective-permute-start(bf16[1,256,384]{2,1,0:T(8,128)(2,1)} %get-tuple-element.243), channel_id=1, source_target_pairs={{0,1},{1,0},{2,3},{3,2},{4,5},{5,4},{6,7},{7,6},{8,9},{9,8},{10,11... | collective-permute-start | bytes 589832 | tf_op jit(solution)/shard_map/ppermute | solution.py:1036
  283.9 16.0 %collective-permute-start.27 = (bf16[1,256,384]{2,1,0:T(8,128)(2,1)}, bf16[1,256,384]{2,1,0:T(8,128)(2,1)}, u32[]{:S(2)}, u32[]{:S(2)}) collective-permute-start(bf16[1,256,384]{2,1,0:T(8,128)(2,1)} %get-tuple-element.244), channel_id=1, source_target_pairs={{0,2},{1,3},{2,0},{3,1},{4,6},{5,7},{6,4},{7,5},{8,10},{9,11},{10,... | collective-permute-start | bytes 589832 | tf_op jit(solution)/shard_map/ppermute | solution.py:1036
  295.2 7.0 %collective-permute-start.28 = (bf16[1,256,384]{2,1,0:T(8,128)(2,1)}, bf16[1,256,384]{2,1,0:T(8,128)(2,1)S(1)}, u32[]{:S(2)}, u32[]{:S(2)}) collective-permute-start(bf16[1,256,384]{2,1,0:T(8,128)(2,1)} %get-tuple-element.245), channel_id=1, source_target_pairs={{0,3},{1,2},{2,1},{3,0},{4,7},{5,6},{6,5},{7,4},{8,11},{9,10},{10,... | collective-permute-start | bytes 589832 | tf_op jit(solution)/shard_map/ppermute | solution.py:1036
  302.2 10.1 %copy-start.13 = (bf16[1,256,384]{2,1,0:T(8,128)(2,1)}, bf16[1,256,384]{2,1,0:T(8,128)(2,1)S(1)}, u32[]{:S(2)}) copy-start(bf16[1,256,384]{2,1,0:T(8,128)(2,1)S(1)} %collective-permute-done.28.refs_3_) | copy-start | bytes 589828
  302.3 10.0 %collective-permute-start.31 = (bf16[64,384]{1,0:T(8,128)(2,1)S(1)}, bf16[64,384]{1,0:T(8,128)(2,1)S(1)}, u32[]{:S(2)}, u32[]{:S(2)}) collective-permute-start(bf16[64,384]{1,0:T(8,128)(2,1)S(1)} %get-tuple-element.330), channel_id=1, source_target_pairs={{0,18},{1,19},{2,16},{3,17},{4,22},{5,23},{6,20},{7,21},{8,26},{9,... | collective-permute-start | bytes 147464 | tf_op jit(solution)/shard_map/ppermute | solution.py:1031
  304.9 7.4 %collective-permute-start.30 = (bf16[64,384]{1,0:T(8,128)(2,1)S(1)}, bf16[64,384]{1,0:T(8,128)(2,1)S(1)}, u32[]{:S(2)}, u32[]{:S(2)}) collective-permute-start(bf16[64,384]{1,0:T(8,128)(2,1)S(1)} %get-tuple-element.331), channel_id=1, source_target_pairs={{0,16},{1,17},{2,18},{3,19},{4,20},{5,21},{6,22},{7,23},{8,24},{9,... | collective-permute-start | bytes 147464 | tf_op jit(solution)/shard_map/ppermute | solution.py:1031
  306.3 6.0 %collective-permute-start.29 = (bf16[64,384]{1,0:T(8,128)(2,1)S(1)}, bf16[64,384]{1,0:T(8,128)(2,1)S(1)}, u32[]{:S(2)}, u32[]{:S(2)}) collective-permute-start(bf16[64,384]{1,0:T(8,128)(2,1)S(1)} %get-tuple-element.329), channel_id=1, source_target_pairs={{0,2},{1,3},{2,0},{3,1},{4,6},{5,7},{6,4},{7,5},{8,10},{9,11},{10,... | collective-permute-start | bytes 147464 | tf_op jit(solution)/shard_map/ppermute | solution.py:1031
  314.0 4.6 %collective-permute-start.32 = (bf16[112,384]{1,0:T(8,128)(2,1)S(1)}, bf16[112,384]{1,0:T(8,128)(2,1)S(1)}, u32[]{:S(2)}, u32[]{:S(2)}) collective-permute-start(bf16[112,384]{1,0:T(8,128)(2,1)S(1)} %pad_maximum_fusion.1), channel_id=1, source_target_pairs={{0,2},{1,3},{2,0},{3,1},{4,6},{5,7},{6,4},{7,5},{8,10},{9,11},{10,... | collective-permute-start | bytes 258056 | tf_op jit(solution)/shard_map/ppermute | solution.py:1031
  315.5 12.2 %collective-permute-start.35 = (bf16[1,256,384]{2,1,0:T(8,128)(2,1)}, bf16[1,256,384]{2,1,0:T(8,128)(2,1)S(1)}, u32[]{:S(2)}, u32[]{:S(2)}) collective-permute-start(bf16[1,256,384]{2,1,0:T(8,128)(2,1)} %get-tuple-element.263), channel_id=1, source_target_pairs={{0,1},{1,0},{2,3},{3,2},{4,5},{5,4},{6,7},{7,6},{8,9},{9,8},{10,11... | collective-permute-start | bytes 589832 | tf_op jit(solution)/shard_map/ppermute | solution.py:1036
  315.5 12.2 %collective-permute-start.36 = (bf16[1,256,384]{2,1,0:T(8,128)(2,1)}, bf16[1,256,384]{2,1,0:T(8,128)(2,1)S(1)}, u32[]{:S(2)}, u32[]{:S(2)}) collective-permute-start(bf16[1,256,384]{2,1,0:T(8,128)(2,1)} %get-tuple-element.264), channel_id=1, source_target_pairs={{0,2},{1,3},{2,0},{3,1},{4,6},{5,7},{6,4},{7,5},{8,10},{9,11},{10,... | collective-permute-start | bytes 589832 | tf_op jit(solution)/shard_map/ppermute | solution.py:1036
  316.1 12.7 %collective-permute-start.37 = (bf16[1,256,384]{2,1,0:T(8,128)(2,1)}, bf16[1,256,384]{2,1,0:T(8,128)(2,1)}, u32[]{:S(2)}, u32[]{:S(2)}) collective-permute-start(bf16[1,256,384]{2,1,0:T(8,128)(2,1)} %get-tuple-element.265), channel_id=1, source_target_pairs={{0,3},{1,2},{2,1},{3,0},{4,7},{5,6},{6,5},{7,4},{8,11},{9,10},{10,... | collective-permute-start | bytes 589832 | tf_op jit(solution)/shard_map/ppermute | solution.py:1036
  317.4 8.5 %collective-permute-start.33 = (bf16[112,384]{1,0:T(8,128)(2,1)S(1)}, bf16[112,384]{1,0:T(8,128)(2,1)S(1)}, u32[]{:S(2)}, u32[]{:S(2)}) collective-permute-start(bf16[112,384]{1,0:T(8,128)(2,1)S(1)} %pad_maximum_fusion.1), channel_id=1, source_target_pairs={{0,16},{1,17},{2,18},{3,19},{4,20},{5,21},{6,22},{7,23},{8,24},{9,... | collective-permute-start | bytes 258056 | tf_op jit(solution)/shard_map/ppermute | solution.py:1031
  318.5 9.1 %collective-permute-start.34 = (bf16[112,384]{1,0:T(8,128)(2,1)S(1)}, bf16[112,384]{1,0:T(8,128)(2,1)S(1)}, u32[]{:S(2)}, u32[]{:S(2)}) collective-permute-start(bf16[112,384]{1,0:T(8,128)(2,1)S(1)} %pad_maximum_fusion.1), channel_id=1, source_target_pairs={{0,18},{1,19},{2,16},{3,17},{4,22},{5,23},{6,20},{7,21},{8,26},{9,... | collective-permute-start | bytes 258056 | tf_op jit(solution)/shard_map/ppermute | solution.py:1031
  327.7 13.1 %copy-start.14 = (bf16[1,256,384]{2,1,0:T(8,128)(2,1)}, bf16[1,256,384]{2,1,0:T(8,128)(2,1)S(1)}, u32[]{:S(2)}) copy-start(bf16[1,256,384]{2,1,0:T(8,128)(2,1)S(1)} %collective-permute-done.35.refs_1_) | copy-start | bytes 589828
  328.8 18.8 %collective-permute-start.40 = (bf16[448,384]{1,0:T(8,128)(2,1)S(1)}, bf16[448,384]{1,0:T(8,128)(2,1)S(1)}, u32[]{:S(2)}, u32[]{:S(2)}) collective-permute-start(bf16[448,384]{1,0:T(8,128)(2,1)S(1)} %constant_dynamic-update-slice_fusion), channel_id=1, source_target_pairs={{0,12},{1,13},{2,14},{3,15},{4,8},{5,9},{6,10},{7,11},{8,4},{9,5},... | collective-permute-start | bytes 1032200 | tf_op jit(solution)/shard_map/ppermute | solution.py:1031
  328.8 18.8 %collective-permute-start.39 = (bf16[448,384]{1,0:T(8,128)(2,1)S(1)}, bf16[448,384]{1,0:T(8,128)(2,1)}, u32[]{:S(2)}, u32[]{:S(2)}) collective-permute-start(bf16[448,384]{1,0:T(8,128)(2,1)S(1)} %constant_dynamic-update-slice_fusion), channel_id=1, source_target_pairs={{0,4},{1,5},{2,6},{3,7},{4,0},{5,1},{6,2},{7,3},{8,12},{9,13},{10,... | collective-permute-start | bytes 1032200 | tf_op jit(solution)/shard_map/ppermute | solution.py:1031
  329.7 17.9 %collective-permute-start.38 = (bf16[448,384]{1,0:T(8,128)(2,1)S(1)}, bf16[448,384]{1,0:T(8,128)(2,1)}, u32[]{:S(2)}, u32[]{:S(2)}) collective-permute-start(bf16[448,384]{1,0:T(8,128)(2,1)S(1)} %constant_dynamic-update-slice_fusion), channel_id=1, source_target_pairs={{0,8},{1,9},{2,10},{3,11},{4,12},{5,13},{6,14},{7,15},{8,0},{9,1},... | collective-permute-start | bytes 1032200 | tf_op jit(solution)/shard_map/ppermute | solution.py:1031
  349.9 3.5 collective-permute-start.41
  (23 other events, 81.9 us)
Sparse Core Ops, SparseCore 0:
  236.9 73.7 all-gather.1

commit v3 on v2

--- a/solution.py
+++ b/solution.py
@@ -30,6 +30,11 @@
 
 def col_sum(values):
     return jnp.sum(values, axis=0, keepdims=True)
+
+
+def rows_of(*rows):
+    blank = jnp.zeros((8 - len(rows), rows[0].shape[1]), F32)
+    return jnp.concatenate([*rows, blank], axis=0).astype(BF)
 
 
 def row_mean(values):
@@ -293,7 +298,6 @@
             for slot in range(2):
                 zero_pads(ref.at[slot], cols)
 
-    gmod_ref[...] = jnp.zeros(gmod_ref.shape, F32)
     gate_one, shift_two, scale_two, gate_two = (mod_ref[0, pl.ds(part, 1), :] for part in range(2, 6))
     attn_s[...] = mm(mix_ref[0], proj_w[...])
 
@@ -419,10 +423,7 @@
         grad_mid = grad_after + norm_back(grad_hid * (1.0 + scale_two), unit, inverse)
         gmid_ref[0, rows, :] = grad_mid
         grad_gate_one += col_sum(attn * grad_mid)
-    gmod_ref[0, pl.ds(0, 1), :] = grad_gate_one
-    gmod_ref[0, pl.ds(1, 1), :] = grad_shift_two
-    gmod_ref[0, pl.ds(2, 1), :] = grad_scale_two
-    gmod_ref[0, pl.ds(3, 1), :] = grad_gate_two
+    gmod_ref[0] = rows_of(grad_gate_one, grad_shift_two, grad_scale_two, grad_gate_two)
 
     res_ref[0] = (mm(low_s[...], down_w[...]) + down_b[...]).astype(BF)
     grad_low_t = grad_low.T
@@ -584,7 +585,6 @@
         for ref in (plain_g, moved_g):
             zero_pads(ref, cols)
 
-    gmod_ref[...] = jnp.zeros(gmod_ref.shape, F32)
     shift_one, scale_one = (mod_ref[0, pl.ds(part, 1), :] for part in range(2))
     for plane in range(4):
         rows = pl.ds(plane * tokens, tokens)
@@ -623,8 +623,7 @@
         gout_s[rows, :] = (
             gmid_ref[0, rows, :] + norm_back(grad_hid * (1.0 + scale_one), unit, inverse)
         ).astype(BF)
-    gmod_ref[0, pl.ds(0, 1), :] = grad_shift
-    gmod_ref[0, pl.ds(1, 1), :] = grad_scale
+    gmod_ref[0] = rows_of(grad_shift, grad_scale)
     for at, piece in enumerate(pieces):
         strip = at ^ rank_ref[1]
         gathered = jnp.concatenate(
@@ -818,7 +817,7 @@
     outs = [
         (og.shape[:2] + (down_w.shape[1],), BF),
         (xp.shape, F32),
-        ((images, 8, width), F32),
+        ((images, 8, width), BF),
     ]
     sums = [((4 * hidden, width), BF), ((16, hidden), F32)]
     grid = pltpu.PrefetchScalarGridSpec(
@@ -899,7 +898,7 @@
     tokens = moves.shape[1]
     padded = tokens + 32
     shared = (qkv_w, conv_a, perm_back, moves)
-    outs = [((images, all_tokens // strips, width), BF)] * strips + [((images, 8, width), F32)]
+    outs = [((images, all_tokens // strips, width), BF)] * strips + [((images, 8, width), BF)]
     sums = [(16, width)]
     grid = pltpu.PrefetchScalarGridSpec(
         num_scalar_prefetch=1,
@@ -1196,14 +1195,14 @@
     per_tile = 8 // images
     late = jnp.concatenate(
         [
-            sum(convs),
+            sum(convs).astype(BF),
             jnp.pad(grad_mod, ((0, -grad_mod.shape[0] % 8), (0, 0))),
             jnp.pad(
-                jnp.concatenate([cond.astype(F32)] * per_tile, axis=0), ((0, 0), (0, width - cond.shape[1]))
+                jnp.concatenate([cond] * per_tile, axis=0), ((0, 0), (0, width - cond.shape[1]))
             ),
         ],
         axis=0,
-    ).astype(BF)
+    )
     share = rest.shape[0]
     rest = jnp.concatenate([rest, late], axis=0)
     grad_latents = None

time: 371 us -> 370 us (level)
  transfers between devices with their start and end apart: 43 -> 43, of which waited for: 14 -> 14; matrix products, arithmetic and copies ran while one was open for 5% -> 4% of each run, Pallas kernels for 36% -> 36%
where the time goes in v3:
time: 370 us; the launch traced here: 365 us
  Pallas kernels  246 us (66%)
  starting transfers between devices  39 us (11%)
  waiting for transfers between devices  32.5 us (9%)
  local copies, waits for them, and re-layouts  17.5 us (5%)
  between operations  15.1 us (4%)
  other arithmetic  15 us (4%)
    pallas_call x1, Pallas kernels, feed_forward_call(): pl.pallas_call(functools.partial(feed_forward_kernel, parts=parts), grid_...  100 us
    pallas_call x2, Pallas kernels, attention_back_call(): pl.pallas_call(functools.partial(attention_back_kernel, parts=parts, begi...  46.6 us
    pallas_call x4, Pallas kernels, attention_forward_call(): pl.pallas_call(functools.partial(attention_forward_kernel, strips, begin)...  42.1 us
    pallas_call x3, Pallas kernels, conv_attn_back_call(): pl.pallas_call(functools.partial(conv_attn_back_kernel, strips), grid_spe...  33.3 us
    ppermute x21, waiting for transfers between devices, exchange(): return lax.ppermute(values, AXES, [(i, i ^ mask) for i in range(devices)])  26.3 us
    ppermute x21, starting transfers between devices, exchange(): return lax.ppermute(values, AXES, [(i, i ^ mask) for i in range(devices)])  23.9 us
    ppermute x21, starting transfers between devices, swap_strips(): return lax.ppermute(values, 'narrow', [(i, i ^ mask) for i in range(count)])  15 us
    pallas_call x3, Pallas kernels, finish_latents_call(): pl.pallas_call(functools.partial(finish_latents_kernel, strips), grid_spe...  9.92 us
  transfers between devices with their start and end apart: 43, of which 14 were waited for; matrix products, arithmetic and copies ran while one was open for 4% of the time, Pallas kernels for 36%

profile of v3, /device:TPU:0, one launch (start us, length us, event | category | flops | bytes accessed | tf_op | source)
XLA Modules:
  0.0 365.4 jit_solution(4416787401777727843)
XLA Ops:
  7.3 3.4 dynamic-slice_bitcast_fusion
  11.2 2.6 collective-permute-start.1
  21.2 2.1 collective-permute-done.2.refs_3_
  23.4 1.7 collective-permute-start.4
  25.1 10.7 %attention_forward.4 = (bf16[4,1024,384]{2,1,0:T(8,128)(2,1)}, bf16[4,1024,384]{2,1,0:T(8,128)(2,1)}, bf16[4,1024,1152]{2,1,0:T(8,128)(2,1)}, bf16[4,1024,384]{2,1,0:T(8,128)(2,1)}, f32[4,4,8,256]{3,2,1,0:T(8,128)}) custom-call(s32[2]{0:T(128)} %pad_add_fusion.rank_ref, bf16[256,384]{1,0:T(8,128)(2,1)} %get-tuple-element.177.refs_0_, ...), custom_call_target="tpu_custom_call" | custom-call | flops 5000000000 | bytes 8000000 | tf_op jit(solution)/shard_map/attention_forward/pallas_call | solution.py:798
  37.0 1.7 collective-permute-start.7
  38.7 10.5 %attention_forward.5 = (bf16[4,1024,384]{2,1,0:T(8,128)(2,1)}, bf16[4,1024,384]{2,1,0:T(8,128)(2,1)}, bf16[4,1024,1152]{2,1,0:T(8,128)(2,1)}, bf16[4,1024,384]{2,1,0:T(8,128)(2,1)}, f32[4,4,8,256]{3,2,1,0:T(8,128)}) custom-call(s32[2]{0:T(128)} %pad_add_fusion.rank_ref, ...), custom_call_target="tpu_custom_call", output_to_operand_aliasing={{0}: (10, {}), {1}: (11, {}), {2}: (12, {}), {3}: (13, {}),... | custom-call | flops 5000000000 | bytes 8000000 | tf_op jit(solution)/shard_map/attention_forward/pallas_call | solution.py:798
  49.8 1.7 collective-permute-start.10
  51.5 10.5 %attention_forward.6 = (bf16[4,1024,384]{2,1,0:T(8,128)(2,1)}, bf16[4,1024,384]{2,1,0:T(8,128)(2,1)}, bf16[4,1024,1152]{2,1,0:T(8,128)(2,1)}, bf16[4,1024,384]{2,1,0:T(8,128)(2,1)}, f32[4,4,8,256]{3,2,1,0:T(8,128)}) custom-call(s32[2]{0:T(128)} %pad_add_fusion.rank_ref, ...), custom_call_target="tpu_custom_call", output_to_operand_aliasing={{0}: (10, {}), {1}: (11, {}), {2}: (12, {}), {3}: (13, {}),... | custom-call | flops 5000000000 | bytes 8000000 | tf_op jit(solution)/shard_map/attention_forward/pallas_call | solution.py:798
  62.7 10.4 %attention_forward.7 = (bf16[4,1024,384]{2,1,0:T(8,128)(2,1)}, bf16[4,1024,384]{2,1,0:T(8,128)(2,1)}, bf16[4,1024,1152]{2,1,0:T(8,128)(2,1)}, bf16[4,1024,384]{2,1,0:T(8,128)(2,1)}, f32[4,4,8,256]{3,2,1,0:T(8,128)}) custom-call(s32[2]{0:T(128)} %pad_add_fusion.rank_ref, ...), custom_call_target="tpu_custom_call", output_to_operand_aliasing={{0}: (10, {}), {1}: (11, {}), {2}: (12, {}), {3}: (13, {}),... | custom-call | flops 5000000000 | bytes 8000000 | tf_op jit(solution)/shard_map/attention_forward/pallas_call | solution.py:798
  73.2 100.1 %feed_forward.1 = (bf16[4,256,768]{2,1,0:T(8,128)(2,1)}, f32[4,1024,384]{2,1,0:T(8,128)}, bf16[4,8,384]{2,1,0:T(8,128)(2,1)}, bf16[6144,384]{1,0:T(8,128)(2,1)}, f32[16,1536]{1,0:T(8,128)}) custom-call(s32[2]{0:T(128)} %pad_add_fusion.rank_ref, bf16[4,1024,384]{2,1,0:T(8,128)(2,1)} %get-tuple-element.196.xp_ref, ...), custom_call_target="tpu_custom_call" | custom-call | flops 56000000000 | bytes 80000000 | tf_op jit(solution)/shard_map/feed_forward/pallas_call | solution.py:850
  173.3 2.1 slice.67
  175.9 4.2 %collective-permute-done.12 = bf16[3072,384]{1,0:T(8,128)(2,1)S(1)} collective-permute-done((bf16[3072,384]{1,0:T(8,128)(2,1)S(1)}, bf16[3072,384]{1,0:T(8,128)(2,1)S(1)}, u32[]{:S(2)}, u32[]{:S(2)}) %collective-permute-start.12) | collective-permute-done | bytes 2359328 | tf_op jit(solution)/shard_map/ppermute | solution.py:1030
  180.6 1.4 copy-done
  183.2 2.7 collective-permute-start.15
  186.7 22.2 %attention_back.2 = (bf16[2,1024,1152]{2,1,0:T(8,128)(2,1)}, f32[384,1536]{1,0:T(8,128)}) custom-call(s32[2]{0:T(128)} %pad_add_fusion.rank_ref, f32[4,8,384]{2,1,0:T(8,128)} %pad.18.refs_4_.mod_ref, f32[4,1024,384]{2,1,0:T(8,128)} %get-tuple-element.202.gmid_ref, bf16[4,1024,384]{2,1,0:T(8,128)(2,1)} %get-tuple-element.203.co_ref, ...), custom_call_target="tpu_custom_call" | custom-call | flops 16000000000 | bytes 20000000 | tf_op jit(solution)/shard_map/attention_back/pallas_call | solution.py:885
  208.9 3.8 %collective-permute-done.14 = bf16[768,384]{1,0:T(8,128)(2,1)} collective-permute-done((bf16[768,384]{1,0:T(8,128)(2,1)}, bf16[768,384]{1,0:T(8,128)(2,1)}, u32[]{:S(2)}, u32[]{:S(2)}) %collective-permute-start.14) | collective-permute-done | bytes 589856 | tf_op jit(solution)/shard_map/ppermute | solution.py:1030
  212.9 1.9 add_convert_fusion.2
  215.5 3.5 collective-permute-start.18
  219.9 15.3 %conv_attn_back.3 = (bf16[2,256,384]{2,1,0:T(8,128)(2,1)}, bf16[2,256,384]{2,1,0:T(8,128)(2,1)}, bf16[2,256,384]{2,1,0:T(8,128)(2,1)}, bf16[2,256,384]{2,1,0:T(8...) custom-call(s32[2]{0:T(128)} %pad_add_fusion.rank_ref, bf16[4,1024,384]{2,1,0:T(8,128)(2,1)} %get-tuple-element.196.xp_ref, ...), custom_call_target="tpu_custom_call" | custom-call | flops 8000000000 | bytes 16000000 | tf_op jit(solution)/shard_map/conv_attn_back/pallas_call | solution.py:919
  235.2 1.8 add_convert_fusion.5
  237.1 1.6 collective-permute-start.20
  239.0 24.4 %attention_back.3 = (bf16[2,1024,1152]{2,1,0:T(8,128)(2,1)}, f32[384,1536]{1,0:T(8,128)}, bf16[2048,384]{1,0:T(8,128)(2,1)}) custom-call(s32[2]{0:T(128)} %pad_add_fusion.rank_ref, f32[4,8,384]{2,1,0:T(8,128)} %pad.18.refs_4_.mod_ref, f32[4,1024,384]{2,1,0:T(8,128)} %get-tuple-element.202.gmid_ref, bf16[4,1024,384]{2,1,0:T(8,128)(2,1)} %get-tuple-element.203.co_ref, ...), custom_call_target="tpu_custom_call" | custom-call | flops 16000000000 | bytes 20000000 | tf_op jit(solution)/shard_map/attention_back/pallas_call | solution.py:885
  266.6 9.0 %conv_attn_back.4 = (bf16[1,256,384]{2,1,0:T(8,128)(2,1)}, bf16[1,256,384]{2,1,0:T(8,128)(2,1)}, bf16[1,256,384]{2,1,0:T(8,128)(2,1)}, bf16[1,256,384]{2,1,0:T(8...) custom-call(s32[2]{0:T(128)} %pad_add_fusion.rank_ref, bf16[4,1024,384]{2,1,0:T(8,128)(2,1)} %get-tuple-element.196.xp_ref, ...), custom_call_target="tpu_custom_call" | custom-call | flops 4000000000 | bytes 8000000 | tf_op jit(solution)/shard_map/conv_attn_back/pallas_call | solution.py:919
  275.6 1.6 add_convert_fusion.1
  278.0 1.5 collective-permute-start.25
  279.5 1.5 collective-permute-start.24
  281.5 1.5 collective-permute-start.27
  283.0 9.0 %conv_attn_back.5 = (bf16[1,256,384]{2,1,0:T(8,128)(2,1)}, bf16[1,256,384]{2,1,0:T(8,128)(2,1)}, bf16[1,256,384]{2,1,0:T(8,128)(2,1)}, bf16[1,256,384]{2,1,0:T(8...) custom-call(s32[2]{0:T(128)} %pad_add_fusion.rank_ref, bf16[4,1024,384]{2,1,0:T(8,128)(2,1)} %get-tuple-element.196.xp_ref, ...), custom_call_target="tpu_custom_call" | custom-call | flops 4000000000 | bytes 8000000 | tf_op jit(solution)/shard_map/conv_attn_back/pallas_call | solution.py:919
  292.4 2.2 collective-permute-done.24
  294.5 2.1 collective-permute-done.23
  297.9 2.6 collective-permute-done.28.refs_3_
  300.4 2.5 collective-permute-start.31
  303.3 1.6 collective-permute-start.29
  305.7 5.4 %collective-permute-done.31 = bf16[64,384]{1,0:T(8,128)(2,1)S(1)} collective-permute-done((bf16[64,384]{1,0:T(8,128)(2,1)S(1)}, bf16[64,384]{1,0:T(8,128)(2,1)S(1)}, u32[]{:S(2)}, u32[]{:S(2)}) %collective-permute-start.31) | collective-permute-done | bytes 49184 | tf_op jit(solution)/shard_map/ppermute | solution.py:1030
  312.8 1.6 collective-permute-start.32
  317.3 1.8 collective-permute-start.34
  319.1 5.2 %collective-permute-done.33 = bf16[112,384]{1,0:T(8,128)(2,1)S(1)} collective-permute-done((bf16[112,384]{1,0:T(8,128)(2,1)S(1)}, bf16[112,384]{1,0:T(8,128)(2,1)S(1)}, u32[]{:S(2)}, u32[]{:S(2)}) %collective-permute-start.33) | collective-permute-done | bytes 86048 | tf_op jit(solution)/shard_map/ppermute | solution.py:1030
  324.4 1.7 collective-permute-done.34
  326.2 1.5 collective-permute-done.37.refs_3_
  327.9 1.5 collective-permute-start.39
  329.5 2.0 collective-permute-start.38
  331.4 8.5 %finish_big.1 = (f32[384,1536]{1,0:T(8,128)}, f32[1536,384]{1,0:T(8,128)}, f32[1536,768]{1,0:T(8,128)}) custom-call(bf16[6144,384]{1,0:T(8,128)(2,1)} %all-gather.2.cloned.1.call-done.refs_0_.refs_1_.refs_2_.refs_3_, bf16[6144,384]{1,0:T(8,128)(2,1)} %all-gather.2.cloned.1.call-done.refs_0_.refs_1_.refs_2_.refs_3_, ...), custom_call_target="tpu_custom_call" | custom-call | bytes 15000000 | tf_op jit(solution)/shard_map/finish_big/pallas_call | solution.py:965
  340.0 3.7 %finish_latents.3.refs_4_ = f32[4,4,256,384]{3,2,1,0:T(8,128)} custom-call(s32[2]{0:T(128)} %pad_add_fusion.rank_ref, bf16[2,256,384]{2,1,0:T(8,128)(2,1)} %get-tuple-element.272.refs_0_, bf16[2,256,384]{2,1,0:T(8,128)(2,1)} %copy-done.3, bf16[2,256,384]{2,1,0:T(8,128)(2,1)} %copy-done.4, bf16[2,256,384]{2,1,0:T(8,128)(2,1)} %collective-permute-done.21.refs_3_), custom_call_target="tpu_custom_call" | custom-call | bytes 6000000 | tf_op jit(solution)/shard_map/finish_latents/pallas_call | solution.py:947
  343.6 3.1 finish_latents.4.refs_4_
  346.8 2.3 pad_maximum_fusion
  349.1 3.1 finish_latents.5
  352.5 5.6 %finish_rest.1 = (f32[384,1152]{1,0:T(8,128)}, f32[384,384]{1,0:T(8,128)}, f32[3,3,1536]{2,1,0:T(4,128)}, f32[1536]{0:T(1024)}, f32[384]{0:T(512)}, /*index=5*/f...) custom-call(s32[2]{0:T(128)} %pad_add_fusion.rank_ref, bf16[16,112,384]{2,1,0:T(8,128)(2,1)} %bitcast.22.own_ref, ...), custom_call_target="tpu_custom_call" | custom-call | bytes 8000000 | tf_op jit(solution)/shard_map/finish_rest/pallas_call | solution.py:1001
  (158 shorter events, 28.4 us)
Async XLA Ops:
  7.2 320.5 %all-gather.2.cloned.1.call-start = ((), (), s32[]{:S(2)}) async-start(), calls=%async_computation | async-start | bytes 4866048 | tf_op jit(solution)/shard_map/all_gather | solution.py:1177
  7.3 9.6 %copy-start.22 = (bf16[768]{0:T(1024)(128)(2,1)S(1)}, bf16[768]{0:T(1024)(128)(2,1)}, u32[]{:S(2)}) copy-start(bf16[768]{0:T(1024)(128)(2,1)} %param.29) | copy-start | bytes 4612
  7.3 10.1 %copy-start.16 = (bf16[3,3,1536]{2,1,0:T(4,128)(2,1)S(1)}, bf16[3,3,1536]{2,1,0:T(4,128)(2,1)}, u32[]{:S(2)}) copy-start(bf16[3,3,1536]{2,1,0:T(4,128)(2,1)} %param.25) | copy-start | bytes 82948
  10.7 10.5 %collective-permute-start = (bf16[256,384]{1,0:T(8,128)(2,1)S(1)}, bf16[256,384]{1,0:T(8,128)(2,1)S(1)}, u32[]{:S(2)}, u32[]{:S(2)}) collective-permute-start(bf16[256,384]{1,0:T(8,128)(2,1)S(1)} %get-tuple-element.318), channel_id=1, source_target_pairs={{0,1},{1,0},{2,3},{3,2},{4,5},{5,4},{6,7},{7,6},{8,9},{9,8},{10,11... | collective-permute-start | bytes 589832 | tf_op jit(solution)/shard_map/ppermute | solution.py:1035
  11.2 10.0 %collective-permute-start.1 = (bf16[256,384]{1,0:T(8,128)(2,1)S(1)}, bf16[256,384]{1,0:T(8,128)(2,1)S(1)}, u32[]{:S(2)}, u32[]{:S(2)}) collective-permute-start(bf16[256,384]{1,0:T(8,128)(2,1)S(1)} %get-tuple-element.317), channel_id=1, source_target_pairs={{0,2},{1,3},{2,0},{3,1},{4,6},{5,7},{6,4},{7,5},{8,10},{9,11},{10,... | collective-permute-start | bytes 589832 | tf_op jit(solution)/shard_map/ppermute | solution.py:1035
  13.8 9.4 %collective-permute-start.2 = (bf16[256,384]{1,0:T(8,128)(2,1)S(1)}, bf16[256,384]{1,0:T(8,128)(2,1)S(1)}, u32[]{:S(2)}, u32[]{:S(2)}) collective-permute-start(bf16[256,384]{1,0:T(8,128)(2,1)S(1)} %get-tuple-element.316), channel_id=1, source_target_pairs={{0,3},{1,2},{2,1},{3,0},{4,7},{5,6},{6,5},{7,4},{8,11},{9,10},{10,... | collective-permute-start | bytes 589832 | tf_op jit(solution)/shard_map/ppermute | solution.py:1035
  23.2 12.6 %collective-permute-start.3 = (bf16[256,384]{1,0:T(8,128)(2,1)}, bf16[256,384]{1,0:T(8,128)(2,1)S(1)}, u32[]{:S(2)}, u32[]{:S(2)}) collective-permute-start(bf16[256,384]{1,0:T(8,128)(2,1)} %get-tuple-element.158), channel_id=1, source_target_pairs={{0,1},{1,0},{2,3},{3,2},{4,5},{5,4},{6,7},{7,6},{8,9},{9,8},{10,11... | collective-permute-start | bytes 589832 | tf_op jit(solution)/shard_map/ppermute | solution.py:1035
  23.4 12.5 %collective-permute-start.4 = (bf16[256,384]{1,0:T(8,128)(2,1)S(1)}, bf16[256,384]{1,0:T(8,128)(2,1)S(1)}, u32[]{:S(2)}, u32[]{:S(2)}) collective-permute-start(bf16[256,384]{1,0:T(8,128)(2,1)S(1)} %get-tuple-element.159), channel_id=1, source_target_pairs={{0,2},{1,3},{2,0},{3,1},{4,6},{5,7},{6,4},{7,5},{8,10},{9,11},{10,... | collective-permute-start | bytes 589832 | tf_op jit(solution)/shard_map/ppermute | solution.py:1035
  25.1 10.8 %collective-permute-start.5 = (bf16[256,384]{1,0:T(8,128)(2,1)S(1)}, bf16[256,384]{1,0:T(8,128)(2,1)S(1)}, u32[]{:S(2)}, u32[]{:S(2)}) collective-permute-start(bf16[256,384]{1,0:T(8,128)(2,1)S(1)} %get-tuple-element.160), channel_id=1, source_target_pairs={{0,3},{1,2},{2,1},{3,0},{4,7},{5,6},{6,5},{7,4},{8,11},{9,10},{10,... | collective-permute-start | bytes 589832 | tf_op jit(solution)/shard_map/ppermute | solution.py:1035
  36.6 12.6 %collective-permute-start.6 = (bf16[256,384]{1,0:T(8,128)(2,1)}, bf16[256,384]{1,0:T(8,128)(2,1)S(1)}, u32[]{:S(2)}, u32[]{:S(2)}) collective-permute-start(bf16[256,384]{1,0:T(8,128)(2,1)} %get-tuple-element.162), channel_id=1, source_target_pairs={{0,1},{1,0},{2,3},{3,2},{4,5},{5,4},{6,7},{7,6},{8,9},{9,8},{10,11... | collective-permute-start | bytes 589832 | tf_op jit(solution)/shard_map/ppermute | solution.py:1035
  37.0 12.2 %collective-permute-start.7 = (bf16[256,384]{1,0:T(8,128)(2,1)}, bf16[256,384]{1,0:T(8,128)(2,1)S(1)}, u32[]{:S(2)}, u32[]{:S(2)}) collective-permute-start(bf16[256,384]{1,0:T(8,128)(2,1)} %get-tuple-element.163), channel_id=1, source_target_pairs={{0,2},{1,3},{2,0},{3,1},{4,6},{5,7},{6,4},{7,5},{8,10},{9,11},{10,... | collective-permute-start | bytes 589832 | tf_op jit(solution)/shard_map/ppermute | solution.py:1035
  38.7 10.5 %collective-permute-start.8 = (bf16[256,384]{1,0:T(8,128)(2,1)}, bf16[256,384]{1,0:T(8,128)(2,1)S(1)}, u32[]{:S(2)}, u32[]{:S(2)}) collective-permute-start(bf16[256,384]{1,0:T(8,128)(2,1)} %get-tuple-element.164), channel_id=1, source_target_pairs={{0,3},{1,2},{2,1},{3,0},{4,7},{5,6},{6,5},{7,4},{8,11},{9,10},{10,... | collective-permute-start | bytes 589832 | tf_op jit(solution)/shard_map/ppermute | solution.py:1035
  49.2 12.7 %collective-permute-start.9 = (bf16[256,384]{1,0:T(8,128)(2,1)}, bf16[256,384]{1,0:T(8,128)(2,1)S(1)}, u32[]{:S(2)}, u32[]{:S(2)}) collective-permute-start(bf16[256,384]{1,0:T(8,128)(2,1)} %get-tuple-element.166), channel_id=1, source_target_pairs={{0,1},{1,0},{2,3},{3,2},{4,5},{5,4},{6,7},{7,6},{8,9},{9,8},{10,11... | collective-permute-start | bytes 589832 | tf_op jit(solution)/shard_map/ppermute | solution.py:1035
  49.8 12.2 %collective-permute-start.10 = (bf16[256,384]{1,0:T(8,128)(2,1)}, bf16[256,384]{1,0:T(8,128)(2,1)S(1)}, u32[]{:S(2)}, u32[]{:S(2)}) collective-permute-start(bf16[256,384]{1,0:T(8,128)(2,1)} %get-tuple-element.167), channel_id=1, source_target_pairs={{0,2},{1,3},{2,0},{3,1},{4,6},{5,7},{6,4},{7,5},{8,10},{9,11},{10,... | collective-permute-start | bytes 589832 | tf_op jit(solution)/shard_map/ppermute | solution.py:1035
  51.4 10.6 %collective-permute-start.11 = (bf16[256,384]{1,0:T(8,128)(2,1)}, bf16[256,384]{1,0:T(8,128)(2,1)}, u32[]{:S(2)}, u32[]{:S(2)}) collective-permute-start(bf16[256,384]{1,0:T(8,128)(2,1)} %get-tuple-element.168), channel_id=1, source_target_pairs={{0,3},{1,2},{2,1},{3,0},{4,7},{5,6},{6,5},{7,4},{8,11},{9,10},{10,... | collective-permute-start | bytes 589832 | tf_op jit(solution)/shard_map/ppermute | solution.py:1035
  175.3 4.7 %collective-permute-start.12 = (bf16[3072,384]{1,0:T(8,128)(2,1)S(1)}, bf16[3072,384]{1,0:T(8,128)(2,1)S(1)}, u32[]{:S(2)}, u32[]{:S(2)}) collective-permute-start(bf16[3072,384]{1,0:T(8,128)(2,1)S(1)} %slice.67), channel_id=1, source_target_pairs={{0,1},{1,0},{2,3},{3,2},{4,5},{5,4},{6,7},{7,6},{8,9},{9,8},{10,11... | collective-permute-start | bytes 7077896 | tf_op jit(solution)/shard_map/ppermute | solution.py:1030
  183.2 25.7 %collective-permute-start.15 = (bf16[768,384]{1,0:T(8,128)(2,1)}, bf16[768,384]{1,0:T(8,128)(2,1)}, u32[]{:S(2)}, u32[]{:S(2)}) collective-permute-start(bf16[768,384]{1,0:T(8,128)(2,1)} %get-tuple-element.321), channel_id=1, source_target_pairs={{0,12},{1,13},{2,14},{3,15},{4,8},{5,9},{6,10},{7,11},{8,4},{9,5},... | collective-permute-start | bytes 1769480 | tf_op jit(solution)/shard_map/ppermute | solution.py:1030
  185.9 26.8 %collective-permute-start.14 = (bf16[768,384]{1,0:T(8,128)(2,1)}, bf16[768,384]{1,0:T(8,128)(2,1)}, u32[]{:S(2)}, u32[]{:S(2)}) collective-permute-start(bf16[768,384]{1,0:T(8,128)(2,1)} %get-tuple-element.322), channel_id=1, source_target_pairs={{0,4},{1,5},{2,6},{3,7},{4,0},{5,1},{6,2},{7,3},{8,12},{9,13},{10,... | collective-permute-start | bytes 1769480 | tf_op jit(solution)/shard_map/ppermute | solution.py:1030
  186.4 26.5 %collective-permute-start.13 = (bf16[768,384]{1,0:T(8,128)(2,1)S(1)}, bf16[768,384]{1,0:T(8,128)(2,1)}, u32[]{:S(2)}, u32[]{:S(2)}) collective-permute-start(bf16[768,384]{1,0:T(8,128)(2,1)S(1)} %get-tuple-element.320), channel_id=1, source_target_pairs={{0,8},{1,9},{2,10},{3,11},{4,12},{5,13},{6,14},{7,15},{8,0},{9,1},... | collective-permute-start | bytes 1769480 | tf_op jit(solution)/shard_map/ppermute | solution.py:1030
  215.5 19.7 %collective-permute-start.18 = (bf16[192,384]{1,0:T(8,128)(2,1)}, bf16[192,384]{1,0:T(8,128)(2,1)}, u32[]{:S(2)}, u32[]{:S(2)}) collective-permute-start(bf16[192,384]{1,0:T(8,128)(2,1)} %get-tuple-element.327), channel_id=1, source_target_pairs={{0,18},{1,19},{2,16},{3,17},{4,22},{5,23},{6,20},{7,21},{8,26},{9,... | collective-permute-start | bytes 442376 | tf_op jit(solution)/shard_map/ppermute | solution.py:1030
  219.1 16.1 %collective-permute-start.17 = (bf16[192,384]{1,0:T(8,128)(2,1)S(1)}, bf16[192,384]{1,0:T(8,128)(2,1)}, u32[]{:S(2)}, u32[]{:S(2)}) collective-permute-start(bf16[192,384]{1,0:T(8,128)(2,1)S(1)} %get-tuple-element.328), channel_id=1, source_target_pairs={{0,16},{1,17},{2,18},{3,19},{4,20},{5,21},{6,22},{7,23},{8,24},{9,... | collective-permute-start | bytes 442376 | tf_op jit(solution)/shard_map/ppermute | solution.py:1030
  219.4 15.8 %collective-permute-start.16 = (bf16[192,384]{1,0:T(8,128)(2,1)S(1)}, bf16[192,384]{1,0:T(8,128)(2,1)}, u32[]{:S(2)}, u32[]{:S(2)}) collective-permute-start(bf16[192,384]{1,0:T(8,128)(2,1)S(1)} %get-tuple-element.326), channel_id=1, source_target_pairs={{0,2},{1,3},{2,0},{3,1},{4,6},{5,7},{6,4},{7,5},{8,10},{9,11},{10,... | collective-permute-start | bytes 442376 | tf_op jit(solution)/shard_map/ppermute | solution.py:1030
  237.0 26.4 %collective-permute-start.19 = (bf16[2,256,384]{2,1,0:T(8,128)(2,1)}, bf16[2,256,384]{2,1,0:T(8,128)(2,1)S(1)}, u32[]{:S(2)}, u32[]{:S(2)}) collective-permute-start(bf16[2,256,384]{2,1,0:T(8,128)(2,1)} %get-tuple-element.219), channel_id=1, source_target_pairs={{0,1},{1,0},{2,3},{3,2},{4,5},{5,4},{6,7},{7,6},{8,9},{9,8},{10,11... | collective-permute-start | bytes 1179656 | tf_op jit(solution)/shard_map/ppermute | solution.py:1035
  237.1 26.3 %collective-permute-start.20 = (bf16[2,256,384]{2,1,0:T(8,128)(2,1)}, bf16[2,256,384]{2,1,0:T(8,128)(2,1)S(1)}, u32[]{:S(2)}, u32[]{:S(2)}) collective-permute-start(bf16[2,256,384]{2,1,0:T(8,128)(2,1)} %get-tuple-element.220), channel_id=1, source_target_pairs={{0,2},{1,3},{2,0},{3,1},{4,6},{5,7},{6,4},{7,5},{8,10},{9,11},{10,... | collective-permute-start | bytes 1179656 | tf_op jit(solution)/shard_map/ppermute | solution.py:1035
  238.7 24.8 %collective-permute-start.21 = (bf16[2,256,384]{2,1,0:T(8,128)(2,1)}, bf16[2,256,384]{2,1,0:T(8,128)(2,1)}, u32[]{:S(2)}, u32[]{:S(2)}) collective-permute-start(bf16[2,256,384]{2,1,0:T(8,128)(2,1)} %get-tuple-element.221), channel_id=1, source_target_pairs={{0,3},{1,2},{2,1},{3,0},{4,7},{5,6},{6,5},{7,4},{8,11},{9,10},{10,... | collective-permute-start | bytes 1179656 | tf_op jit(solution)/shard_map/ppermute | solution.py:1035
  239.0 27.0 %copy-start.19 = (bf16[4,8,384]{2,1,0:T(8,128)(2,1)S(1)}, bf16[4,8,384]{2,1,0:T(8,128)(2,1)}, u32[]{:S(2)}) copy-start(bf16[4,8,384]{2,1,0:T(8,128)(2,1)} %get-tuple-element.253) | copy-start | bytes 73732
  265.5 10.1 %collective-permute-start.22 = (bf16[1024,384]{1,0:T(8,128)(2,1)S(1)}, bf16[1024,384]{1,0:T(8,128)(2,1)}, u32[]{:S(2)}, u32[]{:S(2)}) collective-permute-start(bf16[1024,384]{1,0:T(8,128)(2,1)S(1)} %slice.77), channel_id=1, source_target_pairs={{0,1},{1,0},{2,3},{3,2},{4,5},{5,4},{6,7},{7,6},{8,9},{9,8},{10,11... | collective-permute-start | bytes 2359304 | tf_op jit(solution)/shard_map/ppermute | solution.py:1030
  278.0 14.0 %collective-permute-start.25 = (bf16[256,384]{1,0:T(8,128)(2,1)}, bf16[256,384]{1,0:T(8,128)(2,1)}, u32[]{:S(2)}, u32[]{:S(2)}) collective-permute-start(bf16[256,384]{1,0:T(8,128)(2,1)} %get-tuple-element.324), channel_id=1, source_target_pairs={{0,12},{1,13},{2,14},{3,15},{4,8},{5,9},{6,10},{7,11},{8,4},{9,5},... | collective-permute-start | bytes 589832 | tf_op jit(solution)/shard_map/ppermute | solution.py:1030
  279.5 15.0 %collective-permute-start.24 = (bf16[256,384]{1,0:T(8,128)(2,1)}, bf16[256,384]{1,0:T(8,128)(2,1)}, u32[]{:S(2)}, u32[]{:S(2)}) collective-permute-start(bf16[256,384]{1,0:T(8,128)(2,1)} %get-tuple-element.325), channel_id=1, source_target_pairs={{0,4},{1,5},{2,6},{3,7},{4,0},{5,1},{6,2},{7,3},{8,12},{9,13},{10,... | collective-permute-start | bytes 589832 | tf_op jit(solution)/shard_map/ppermute | solution.py:1030
  281.0 15.6 %collective-permute-start.23 = (bf16[256,384]{1,0:T(8,128)(2,1)S(1)}, bf16[256,384]{1,0:T(8,128)(2,1)}, u32[]{:S(2)}, u32[]{:S(2)}) collective-permute-start(bf16[256,384]{1,0:T(8,128)(2,1)S(1)} %get-tuple-element.323), channel_id=1, source_target_pairs={{0,8},{1,9},{2,10},{3,11},{4,12},{5,13},{6,14},{7,15},{8,0},{9,1},... | collective-permute-start | bytes 589832 | tf_op jit(solution)/shard_map/ppermute | solution.py:1030
  281.5 16.4 %collective-permute-start.26 = (bf16[1,256,384]{2,1,0:T(8,128)(2,1)}, bf16[1,256,384]{2,1,0:T(8,128)(2,1)}, u32[]{:S(2)}, u32[]{:S(2)}) collective-permute-start(bf16[1,256,384]{2,1,0:T(8,128)(2,1)} %get-tuple-element.243), channel_id=1, source_target_pairs={{0,1},{1,0},{2,3},{3,2},{4,5},{5,4},{6,7},{7,6},{8,9},{9,8},{10,11... | collective-permute-start | bytes 589832 | tf_op jit(solution)/shard_map/ppermute | solution.py:1035
  281.5 16.4 %collective-permute-start.27 = (bf16[1,256,384]{2,1,0:T(8,128)(2,1)}, bf16[1,256,384]{2,1,0:T(8,128)(2,1)}, u32[]{:S(2)}, u32[]{:S(2)}) collective-permute-start(bf16[1,256,384]{2,1,0:T(8,128)(2,1)} %get-tuple-element.244), channel_id=1, source_target_pairs={{0,2},{1,3},{2,0},{3,1},{4,6},{5,7},{6,4},{7,5},{8,10},{9,11},{10,... | collective-permute-start | bytes 589832 | tf_op jit(solution)/shard_map/ppermute | solution.py:1035
  292.0 8.4 %collective-permute-start.28 = (bf16[1,256,384]{2,1,0:T(8,128)(2,1)}, bf16[1,256,384]{2,1,0:T(8,128)(2,1)S(1)}, u32[]{:S(2)}, u32[]{:S(2)}) collective-permute-start(bf16[1,256,384]{2,1,0:T(8,128)(2,1)} %get-tuple-element.245), channel_id=1, source_target_pairs={{0,3},{1,2},{2,1},{3,0},{4,7},{5,6},{6,5},{7,4},{8,11},{9,10},{10,... | collective-permute-start | bytes 589832 | tf_op jit(solution)/shard_map/ppermute | solution.py:1035
  300.4 10.8 %copy-start.13 = (bf16[1,256,384]{2,1,0:T(8,128)(2,1)}, bf16[1,256,384]{2,1,0:T(8,128)(2,1)S(1)}, u32[]{:S(2)}) copy-start(bf16[1,256,384]{2,1,0:T(8,128)(2,1)S(1)} %collective-permute-done.28.refs_3_) | copy-start | bytes 589828
  300.4 10.6 %collective-permute-start.31 = (bf16[64,384]{1,0:T(8,128)(2,1)S(1)}, bf16[64,384]{1,0:T(8,128)(2,1)S(1)}, u32[]{:S(2)}, u32[]{:S(2)}) collective-permute-start(bf16[64,384]{1,0:T(8,128)(2,1)S(1)} %get-tuple-element.330), channel_id=1, source_target_pairs={{0,18},{1,19},{2,16},{3,17},{4,22},{5,23},{6,20},{7,21},{8,26},{9,... | collective-permute-start | bytes 147464 | tf_op jit(solution)/shard_map/ppermute | solution.py:1030
  302.9 8.3 %collective-permute-start.30 = (bf16[64,384]{1,0:T(8,128)(2,1)S(1)}, bf16[64,384]{1,0:T(8,128)(2,1)S(1)}, u32[]{:S(2)}, u32[]{:S(2)}) collective-permute-start(bf16[64,384]{1,0:T(8,128)(2,1)S(1)} %get-tuple-element.331), channel_id=1, source_target_pairs={{0,16},{1,17},{2,18},{3,19},{4,20},{5,21},{6,22},{7,23},{8,24},{9,... | collective-permute-start | bytes 147464 | tf_op jit(solution)/shard_map/ppermute | solution.py:1030
  303.3 7.9 %collective-permute-start.29 = (bf16[64,384]{1,0:T(8,128)(2,1)S(1)}, bf16[64,384]{1,0:T(8,128)(2,1)S(1)}, u32[]{:S(2)}, u32[]{:S(2)}) collective-permute-start(bf16[64,384]{1,0:T(8,128)(2,1)S(1)} %get-tuple-element.329), channel_id=1, source_target_pairs={{0,2},{1,3},{2,0},{3,1},{4,6},{5,7},{6,4},{7,5},{8,10},{9,11},{10,... | collective-permute-start | bytes 147464 | tf_op jit(solution)/shard_map/ppermute | solution.py:1030
  312.8 4.6 %collective-permute-start.32 = (bf16[112,384]{1,0:T(8,128)(2,1)S(1)}, bf16[112,384]{1,0:T(8,128)(2,1)S(1)}, u32[]{:S(2)}, u32[]{:S(2)}) collective-permute-start(bf16[112,384]{1,0:T(8,128)(2,1)S(1)} %pad_maximum_fusion.1), channel_id=1, source_target_pairs={{0,2},{1,3},{2,0},{3,1},{4,6},{5,7},{6,4},{7,5},{8,10},{9,11},{10,... | collective-permute-start | bytes 258056 | tf_op jit(solution)/shard_map/ppermute | solution.py:1030
  314.4 11.8 %collective-permute-start.35 = (bf16[1,256,384]{2,1,0:T(8,128)(2,1)}, bf16[1,256,384]{2,1,0:T(8,128)(2,1)S(1)}, u32[]{:S(2)}, u32[]{:S(2)}) collective-permute-start(bf16[1,256,384]{2,1,0:T(8,128)(2,1)} %get-tuple-element.263), channel_id=1, source_target_pairs={{0,1},{1,0},{2,3},{3,2},{4,5},{5,4},{6,7},{7,6},{8,9},{9,8},{10,11... | collective-permute-start | bytes 589832 | tf_op jit(solution)/shard_map/ppermute | solution.py:1035
  314.4 11.8 %collective-permute-start.36 = (bf16[1,256,384]{2,1,0:T(8,128)(2,1)}, bf16[1,256,384]{2,1,0:T(8,128)(2,1)S(1)}, u32[]{:S(2)}, u32[]{:S(2)}) collective-permute-start(bf16[1,256,384]{2,1,0:T(8,128)(2,1)} %get-tuple-element.264), channel_id=1, source_target_pairs={{0,2},{1,3},{2,0},{3,1},{4,6},{5,7},{6,4},{7,5},{8,10},{9,11},{10,... | collective-permute-start | bytes 589832 | tf_op jit(solution)/shard_map/ppermute | solution.py:1035
  314.9 12.8 %collective-permute-start.37 = (bf16[1,256,384]{2,1,0:T(8,128)(2,1)}, bf16[1,256,384]{2,1,0:T(8,128)(2,1)}, u32[]{:S(2)}, u32[]{:S(2)}) collective-permute-start(bf16[1,256,384]{2,1,0:T(8,128)(2,1)} %get-tuple-element.265), channel_id=1, source_target_pairs={{0,3},{1,2},{2,1},{3,0},{4,7},{5,6},{6,5},{7,4},{8,11},{9,10},{10,... | collective-permute-start | bytes 589832 | tf_op jit(solution)/shard_map/ppermute | solution.py:1035
  316.2 8.1 %collective-permute-start.33 = (bf16[112,384]{1,0:T(8,128)(2,1)S(1)}, bf16[112,384]{1,0:T(8,128)(2,1)S(1)}, u32[]{:S(2)}, u32[]{:S(2)}) collective-permute-start(bf16[112,384]{1,0:T(8,128)(2,1)S(1)} %pad_maximum_fusion.1), channel_id=1, source_target_pairs={{0,16},{1,17},{2,18},{3,19},{4,20},{5,21},{6,22},{7,23},{8,24},{9,... | collective-permute-start | bytes 258056 | tf_op jit(solution)/shard_map/ppermute | solution.py:1030
  317.3 8.8 %collective-permute-start.34 = (bf16[112,384]{1,0:T(8,128)(2,1)S(1)}, bf16[112,384]{1,0:T(8,128)(2,1)S(1)}, u32[]{:S(2)}, u32[]{:S(2)}) collective-permute-start(bf16[112,384]{1,0:T(8,128)(2,1)S(1)} %pad_maximum_fusion.1), channel_id=1, source_target_pairs={{0,18},{1,19},{2,16},{3,17},{4,22},{5,23},{6,20},{7,21},{8,26},{9,... | collective-permute-start | bytes 258056 | tf_op jit(solution)/shard_map/ppermute | solution.py:1030
  326.2 13.8 %copy-start.14 = (bf16[1,256,384]{2,1,0:T(8,128)(2,1)}, bf16[1,256,384]{2,1,0:T(8,128)(2,1)S(1)}, u32[]{:S(2)}) copy-start(bf16[1,256,384]{2,1,0:T(8,128)(2,1)S(1)} %collective-permute-done.35.refs_1_) | copy-start | bytes 589828
  327.7 19.1 %collective-permute-start.40 = (bf16[448,384]{1,0:T(8,128)(2,1)S(1)}, bf16[448,384]{1,0:T(8,128)(2,1)S(1)}, u32[]{:S(2)}, u32[]{:S(2)}) collective-permute-start(bf16[448,384]{1,0:T(8,128)(2,1)S(1)} %constant_dynamic-update-slice_fusion), channel_id=1, source_target_pairs={{0,12},{1,13},{2,14},{3,15},{4,8},{5,9},{6,10},{7,11},{8,4},{9,5},... | collective-permute-start | bytes 1032200 | tf_op jit(solution)/shard_map/ppermute | solution.py:1030
  327.9 18.8 %collective-permute-start.39 = (bf16[448,384]{1,0:T(8,128)(2,1)S(1)}, bf16[448,384]{1,0:T(8,128)(2,1)}, u32[]{:S(2)}, u32[]{:S(2)}) collective-permute-start(bf16[448,384]{1,0:T(8,128)(2,1)S(1)} %constant_dynamic-update-slice_fusion), channel_id=1, source_target_pairs={{0,4},{1,5},{2,6},{3,7},{4,0},{5,1},{6,2},{7,3},{8,12},{9,13},{10,... | collective-permute-start | bytes 1032200 | tf_op jit(solution)/shard_map/ppermute | solution.py:1030
  329.5 17.3 %collective-permute-start.38 = (bf16[448,384]{1,0:T(8,128)(2,1)S(1)}, bf16[448,384]{1,0:T(8,128)(2,1)}, u32[]{:S(2)}, u32[]{:S(2)}) collective-permute-start(bf16[448,384]{1,0:T(8,128)(2,1)S(1)} %constant_dynamic-update-slice_fusion), channel_id=1, source_target_pairs={{0,8},{1,9},{2,10},{3,11},{4,12},{5,13},{6,14},{7,15},{8,0},{9,1},... | collective-permute-start | bytes 1032200 | tf_op jit(solution)/shard_map/ppermute | solution.py:1030
  349.1 3.5 collective-permute-start.41
  (23 other events, 82.3 us)
Sparse Core Ops, SparseCore 0:
  237.2 75.2 all-gather.1
